TPU v7x, 32 devices: a whole 2x2x4 slice. The times are simulated.
32 devices in a mesh: branch: 2 (over x), dp: 16 (over z, y, core).
Axes of the slice: x: 2, y: 2, z: 4, core: 2. Of those that a mesh axis runs over, the one named last changes fastest.
Arguments:
- inputs: bfloat16 [96, 816, 512], P('dp'), may hold values from -6 to 6
- window_count: int32 [16], P('dp'), may hold values from 1 to 6, as said below
- branch_blocks: bfloat16 [2, 2, 23552, 512], P('branch', None, 'dp')
- branch_gains: float32 [2, 512], P('branch'), may hold values from 0.1 to 1.9
- branch_biases: float32 [2, 4, 512], P('branch'), may hold values from -2.5 to 2.5
- merge_weight: bfloat16 [1024, 512], replicated, may hold values from -0.1875 to 0.1875
- ff_in: bfloat16 [512, 2048], replicated, may hold values from -0.25 to 0.25
- ff_in_bias: float32 [2048], replicated, may hold values from -2.5 to 2.5
- ff_out: bfloat16 [2048, 512], replicated, may hold values from -0.25 to 0.25
- shared_biases: float32 [4, 512], replicated, may hold values from -2.5 to 2.5
- shared_gains: float32 [2, 512], replicated, may hold values from 0.1 to 1.9
- d_out: bfloat16 [48, 2, 1, 816, 512], P('dp', 'branch'), may hold values from -6 to 6
Outputs:
- layer_out: bfloat16 [48, 2, 1, 816, 512], P('dp', 'branch')
- grad_inputs: bfloat16 [48, 2, 1, 816, 512], P('dp', 'branch')
- grad_branch_blocks: float32 [2, 2, 23552, 512], P('branch', None, 'dp')
- grad_branch_gains: float32 [2, 512], P('branch')
- grad_branch_biases: float32 [2, 4, 512], P('branch')
- grad_merge_weight: float32 [1024, 512], replicated
- grad_ff_in: float32 [512, 2048], replicated
- grad_ff_in_bias: float32 [2048], replicated
- grad_ff_out: float32 [2048, 512], replicated
- grad_shared_biases: float32 [4, 512], replicated
- grad_shared_gains: float32 [2, 512], replicated
Inputs may be any that keep to these rules, and one draw needn't show every extreme that they name: window_count[j] is the number of live windows among windows j * 6 to (j + 1) * 6 - 1, the live ones first; at least one entry equals 6.
All inputs are finite; a program needn't handle non-finite values.
Results may differ from a plain program's by a relative error of at most 0.015.
Values may be sent and summed in bfloat16 or wider, within the bound.
A program may use at most 512 MiB of HBM per device.

v0:
```python
from functools import partial

import jax
import jax.numpy as jnp
from jax import lax
from jax.sharding import PartitionSpec as P

SCALE_A = 12
SCALE_B = 16
MICRO = 3
GRAD_GROUPS = 2
BLOCKS = 92


EPSILON = 1e-05


def layer_norm(values, norm_gain, norm_shift):
    centre = values - jnp.mean(values, axis=-1, keepdims=True)
    spread = jnp.mean(centre * centre, axis=-1, keepdims=True)
    return centre * lax.rsqrt(spread + EPSILON) * norm_gain + norm_shift


def gelu_exact(values):
    return jax.nn.gelu(values, approximate=False)


def column_sum(values):
    return jnp.sum(values.astype(jnp.float32), axis=(0, 1))


def pad_taps(values, tap_total):
    return jnp.pad(values, ((0, 0), (0, tap_total - values.shape[1]), (0, 0)))


def past_windows(values, tap_count, begin, finish):
    batch_size, length, channels = values.shape
    padded = jnp.concatenate(
        [jnp.zeros((batch_size, tap_count - 1, channels), values.dtype), values], axis=1
    )
    offsets = jnp.arange(length)[:, None] + jnp.arange(begin, finish)[None, :]
    return padded[:, offsets, :]


def future_windows(values, tap_count):
    batch_size, length, channels = values.shape
    padded = jnp.concatenate(
        [values, jnp.zeros((batch_size, tap_count - 1, channels), values.dtype)], axis=1
    )
    offsets = jnp.arange(length)[:, None] + (tap_count - 1) - jnp.arange(tap_count)[None, :]
    return padded[:, offsets, :]


def split_blocks(blocks, stride, tap_count):
    return (
        blocks[:stride],
        blocks[stride : stride + tap_count],
        blocks[stride + tap_count : 2 * stride + tap_count],
    )


def branch_forward(stride, tap_total, values, blocks, norm_gain, biases):
    batch_size, length, channels = values.shape
    tap_count = length // stride
    down_weight, iso_weight, up_weight = split_blocks(blocks, stride, tap_count)
    tap_rows = values.reshape(batch_size, tap_count, stride, channels)
    act_full = jnp.tanh(
        jnp.einsum("btrd,rdo->bto", tap_rows, down_weight, preferred_element_type=jnp.float32)
        + biases[0]
    )
    windows = past_windows(act_full.astype(jnp.bfloat16), tap_count, 0, tap_count)
    iso_full = jnp.tanh(
        jnp.einsum("btsd,sdo->bto", windows, iso_weight, preferred_element_type=jnp.float32)
        + biases[1]
    )
    expanded = jnp.einsum(
        "bte,red->btrd",
        iso_full.astype(jnp.bfloat16),
        up_weight,
        preferred_element_type=jnp.float32,
    )
    residual = (
        expanded.reshape(batch_size, length, channels) + biases[2] + values.astype(jnp.float32)
    )
    branch_out = layer_norm(residual, norm_gain, biases[3])
    return (branch_out, residual, pad_taps(act_full, tap_total), pad_taps(iso_full, tap_total))


def branch_backward(
    stride, tap_total, values, grad_branch, residual, act_full, iso_full, blocks, norm_gain, biases
):
    batch_size, length, channels = values.shape
    tap_count = length // stride
    down_weight, iso_weight, up_weight = split_blocks(blocks, stride, tap_count)
    act_used = act_full[:, :tap_count]
    iso_used = iso_full[:, :tap_count]
    unused, norm_back = jax.vjp(layer_norm, residual, norm_gain, biases[3])
    grad_residual, grad_gain, grad_shift = norm_back(grad_branch.astype(jnp.float32))
    grad_expanded = grad_residual.astype(jnp.bfloat16)
    grad_taps = grad_expanded.reshape(batch_size, tap_count, stride, channels)
    grad_iso_out = jnp.einsum(
        "btrd,red->bte", grad_taps, up_weight, preferred_element_type=jnp.float32
    )
    grad_iso = (grad_iso_out * (1.0 - iso_used * iso_used)).astype(jnp.bfloat16)
    grad_act = jnp.einsum(
        "btso,sdo->btd",
        future_windows(grad_iso, tap_count),
        iso_weight,
        preferred_element_type=jnp.float32,
    )
    grad_down = (grad_act * (1.0 - act_used * act_used)).astype(jnp.bfloat16)
    grad_rows = jnp.einsum(
        "bto,rdo->btrd", grad_down, down_weight, preferred_element_type=jnp.float32
    )
    grad_values = grad_residual + grad_rows.reshape(batch_size, length, channels)
    vectors = jnp.stack(
        [
            grad_gain,
            column_sum(grad_down),
            column_sum(grad_iso),
            column_sum(grad_expanded),
            grad_shift,
        ]
    )
    return (
        grad_values,
        vectors,
        pad_taps(grad_down, tap_total),
        pad_taps(grad_iso, tap_total),
        grad_expanded,
    )


def group_grads(
    group_index, stride, values, activation, isometric, grad_down, grad_iso, grad_expanded
):
    batch_size, length, channels = values.shape
    tap_count = length // stride
    per_group = BLOCKS // GRAD_GROUPS
    first_block = group_index * per_group
    end_block = first_block + per_group
    pieces = []
    covered = 0
    begin, finish = (max(first_block, 0), min(end_block, stride))
    if begin < finish:
        tap_rows = values.reshape(batch_size, tap_count, stride, channels)
        pieces.append(
            jnp.einsum(
                "btrd,bto->rdo",
                tap_rows,
                grad_down[:, :tap_count],
                preferred_element_type=jnp.float32,
            )
        )
        covered += finish - begin
    begin, finish = (max(first_block, stride), min(end_block, stride + tap_count))
    windows = past_windows(activation[:, :tap_count], tap_count, begin - stride, finish - stride)
    pieces.append(
        jnp.einsum(
            "btsd,bto->sdo", windows, grad_iso[:, :tap_count], preferred_element_type=jnp.float32
        )
    )
    covered += finish - begin
    begin, finish = (max(first_block, stride + tap_count), min(end_block, 2 * stride + tap_count))
    if begin < finish:
        grad_taps = grad_expanded.reshape(batch_size, tap_count, stride, channels)
        pieces.append(
            jnp.einsum(
                "bte,btrd->red",
                isometric[:, :tap_count],
                grad_taps,
                preferred_element_type=jnp.float32,
            )
        )
        covered += finish - begin
    if covered < per_group:
        pieces.append(jnp.zeros((per_group - covered, channels, channels), jnp.float32))
    return jnp.concatenate(pieces, axis=0).reshape(per_group * channels, channels)


def group_term(
    group_index, branch_index, values, activation, isometric, grad_down, grad_iso, grad_expanded
):
    return lax.cond(
        branch_index == 0,
        partial(group_grads, group_index, SCALE_A),
        partial(group_grads, group_index, SCALE_B),
        values,
        activation,
        isometric,
        grad_down,
        grad_iso,
        grad_expanded,
    )


def per_device(
    inputs,
    window_count,
    branch_blocks,
    branch_gains,
    branch_biases,
    merge_weight,
    ff_in,
    ff_in_bias,
    ff_out,
    shared_biases,
    shared_gains,
    d_out,
):
    branch_index = lax.axis_index("branch")
    slot_total, length, channels = inputs.shape
    per_micro = slot_total // MICRO
    half_micro = per_micro // 2
    tap_total = max(length // SCALE_A, length // SCALE_B)
    gathered = lax.all_gather(branch_blocks, "dp", axis=2, tiled=True)
    blocks = gathered.reshape(-1, channels, channels)
    norm_gain = branch_gains[0]
    biases = branch_biases[0]
    live_count = window_count[0]
    forward_pair = (
        partial(branch_forward, SCALE_A, tap_total),
        partial(branch_forward, SCALE_B, tap_total),
    )
    backward_pair = (
        partial(branch_backward, SCALE_A, tap_total),
        partial(branch_backward, SCALE_B, tap_total),
    )
    shared_totals = [
        jnp.zeros(merge_weight.shape, jnp.float32),
        jnp.zeros(ff_in.shape, jnp.float32),
        jnp.zeros(ff_in_bias.shape, jnp.float32),
        jnp.zeros(ff_out.shape, jnp.float32),
        jnp.zeros(shared_biases.shape, jnp.float32),
        jnp.zeros(shared_gains.shape, jnp.float32),
    ]
    vector_total = jnp.zeros((5, channels), jnp.float32)
    kept_parts = []
    outputs = []
    input_parts = []
    for micro_index in range(MICRO):
        start = micro_index * per_micro
        values = inputs[start : start + per_micro]
        branch_out, residual, act_full, iso_full = lax.cond(
            branch_index == 0, forward_pair[0], forward_pair[1], values, blocks, norm_gain, biases
        )
        joined = lax.all_to_all(
            branch_out.astype(jnp.bfloat16), "branch", split_axis=0, concat_axis=2, tiled=True
        )
        merged = (
            jnp.einsum("btk,ko->bto", joined, merge_weight, preferred_element_type=jnp.float32)
            + shared_biases[0]
        )
        normed_full, norm_one_back = jax.vjp(layer_norm, merged, shared_gains[0], shared_biases[1])
        normed = normed_full.astype(jnp.bfloat16)
        inner_pre = (
            jnp.einsum("btd,df->btf", normed, ff_in, preferred_element_type=jnp.float32)
            + ff_in_bias
        )
        hidden_full, gelu_back = jax.vjp(gelu_exact, inner_pre)
        hidden = hidden_full.astype(jnp.bfloat16)
        outer_pre = (
            jnp.einsum("btf,fd->btd", hidden, ff_out, preferred_element_type=jnp.float32)
            + shared_biases[2]
        )
        result, norm_two_back = jax.vjp(
            layer_norm, merged + outer_pre, shared_gains[1], shared_biases[3]
        )
        window_ids = start + branch_index * half_micro + jnp.arange(half_micro)
        alive_mask = (window_ids < live_count).astype(jnp.float32)[:, None, None]
        outputs.append((result * alive_mask).astype(jnp.bfloat16))
        cotangent = d_out[micro_index, 0].astype(jnp.float32) * alive_mask
        grad_sum, grad_gain_two, grad_shift_two = norm_two_back(cotangent)
        grad_outer = grad_sum.astype(jnp.bfloat16)
        grad_hidden = jnp.einsum(
            "btd,fd->btf", grad_outer, ff_out, preferred_element_type=jnp.float32
        )
        grad_inner = gelu_back(grad_hidden)[0].astype(jnp.bfloat16)
        grad_normed = jnp.einsum(
            "btf,df->btd", grad_inner, ff_in, preferred_element_type=jnp.float32
        )
        grad_norm_in, grad_gain_one, grad_shift_one = norm_one_back(grad_normed)
        grad_merged = (grad_sum + grad_norm_in).astype(jnp.bfloat16)
        grad_joined = jnp.einsum(
            "bto,ko->btk", grad_merged, merge_weight, preferred_element_type=jnp.float32
        ).astype(jnp.bfloat16)
        terms = (
            jnp.einsum("btk,bto->ko", joined, grad_merged, preferred_element_type=jnp.float32),
            jnp.einsum("btd,btf->df", normed, grad_inner, preferred_element_type=jnp.float32),
            column_sum(grad_inner),
            jnp.einsum("btf,btd->fd", hidden, grad_outer, preferred_element_type=jnp.float32),
            jnp.stack(
                [column_sum(grad_merged), grad_shift_one, column_sum(grad_outer), grad_shift_two]
            ),
            jnp.stack([grad_gain_one, grad_gain_two]),
        )
        shared_totals = [running + addend for running, addend in zip(shared_totals, terms)]
        grad_branch = lax.all_to_all(grad_joined, "branch", split_axis=2, concat_axis=0, tiled=True)
        grad_values, vectors, grad_down, grad_iso, grad_expanded = lax.cond(
            branch_index == 0,
            backward_pair[0],
            backward_pair[1],
            values,
            grad_branch,
            residual,
            act_full,
            iso_full,
            blocks,
            norm_gain,
            biases,
        )
        vector_total = vector_total + vectors
        summed_values = lax.psum_scatter(
            grad_values.astype(jnp.bfloat16), "branch", scatter_dimension=0, tiled=True
        )
        input_parts.append(summed_values)
        activation = act_full.astype(jnp.bfloat16)
        isometric = iso_full.astype(jnp.bfloat16)
        kept_parts.append((activation, isometric, grad_down, grad_iso, grad_expanded))
    activation_all = jnp.concatenate([entry[0] for entry in kept_parts], axis=0)
    isometric_all = jnp.concatenate([entry[1] for entry in kept_parts], axis=0)
    grad_down_all = jnp.concatenate([entry[2] for entry in kept_parts], axis=0)
    grad_iso_all = jnp.concatenate([entry[3] for entry in kept_parts], axis=0)
    grad_expanded_all = jnp.concatenate([entry[4] for entry in kept_parts], axis=0)
    block_result = []
    for group_index in range(GRAD_GROUPS):
        term = group_term(
            group_index,
            branch_index,
            inputs,
            activation_all,
            isometric_all,
            grad_down_all,
            grad_iso_all,
            grad_expanded_all,
        )
        block_result.append(lax.psum_scatter(term, "dp", scatter_dimension=0, tiled=True))
    vector_full = jnp.where((jnp.arange(2) == branch_index)[:, None, None], vector_total[None], 0.0)
    summed = lax.psum(
        (
            shared_totals[0],
            shared_totals[1],
            shared_totals[2],
            shared_totals[3],
            shared_totals[4],
            shared_totals[5],
            vector_full,
        ),
        ("branch", "dp"),
    )
    own_vectors = lax.dynamic_slice_in_dim(summed[6], branch_index, 1, 0)
    layer_out = jnp.stack(outputs)[:, None]
    grad_inputs = jnp.stack(input_parts)[:, None]
    grad_blocks = jnp.stack(block_result)[None]
    return (
        layer_out,
        grad_inputs,
        grad_blocks,
        own_vectors[:, 0],
        own_vectors[:, 1:],
        summed[0],
        summed[1],
        summed[2],
        summed[3],
        summed[4],
        summed[5],
    )


def solution(mesh):
    placed = (
        P("dp", None, None),
        P("dp"),
        P("branch", None, "dp", None),
        P("branch", None),
        P("branch", None, None),
        P(),
        P(),
        P(),
        P(),
        P(),
        P(),
        P("dp", "branch", None, None, None),
    )
    return jax.shard_map(
        per_device,
        mesh=mesh,
        in_specs=placed,
        out_specs=(
            P("dp", "branch", None, None, None),
            P("dp", "branch", None, None, None),
            P("branch", None, "dp", None),
            P("branch", None),
            P("branch", None, None),
            P(),
            P(),
            P(),
            P(),
            P(),
            P(),
        ),
        check_vma=False,
    )
```

profile of v0, /device:TPU:19, one launch (start us, length us, event | category | flops | bytes accessed | tf_op | source)
XLA Modules:
  0.0 2377.8 jit_solution(8030178385065969234)
XLA Ops:
  15.6 232.7 %all-gather.2.cloned.1.call-done = bf16[1,2,23552,512]{3,2,1,0:T(8,128)(2,1)} async-done(((bf16[1,2,1472,512]{3,2,1,0:T(8,128)(2,1)}), bf16[1,2,23552,512]{3,2,1,0:T(8,128)(2,1)}) %all-gather.2.cloned.1.call-update) | async-done | bytes 48234512 | tf_op jit(solution)/shard_map/all_gather | solution.py:216
  248.3 63.9 %conditional.10 = (bf16[2,816,512]{2,1,0:T(8,128)(2,1)}, f32[2,816,512]{2,1,0:T(8,128)}, f32[2,68,512]{2,1,0:T(8,128)S(1)}, f32[2,68,512]{2,1,0:T(8,128)}) conditional(s32[]{:T(128)} %convert_element_type.450, (bf16[2,816,512]{2,0,1:T(2,128)(2,1)}, bf16[92,512,512]{2,1,0:T(8,128)(2,1)}, f32[4,512]{1,0:T(4,128)S(1)}, ...), branch_computations={%region_20.0_spmd, %region_23.0_spmd} | conditional | flops 6570222080 | bytes 131432216 | solution.py:244
  257.2 16.4 gather_fusion.8
  312.2 35.2 %all-to-all-start.2 = ((bf16[2,816,512]{2,1,0:T(8,128)(2,1)}), bf16[2,816,512]{2,1,0:T(8,128)(2,1)}, u32[]{:S(2)}, u32[]{:S(2)}) async-start(bf16[2,816,512]{2,1,0:T(8,128)(2,1)} %get-tuple-element.375), calls=%async_computation.2 | async-start | bytes 3342336 | tf_op jit(solution)/shard_map/all_to_all | solution.py:247
  351.8 63.6 %conditional.9 = (bf16[2,816,512]{2,1,0:T(8,128)(2,1)}, f32[2,816,512]{2,1,0:T(8,128)}, f32[2,68,512]{2,1,0:T(8,128)S(1)}, f32[2,68,512]{2,1,0:T(8,128)}) conditional(s32[]{:T(128)} %convert_element_type.450, (bf16[2,816,512]{2,0,1:T(2,128)(2,1)}, bf16[92,512,512]{2,1,0:T(8,128)(2,1)}, f32[4,512]{1,0:T(4,128)S(1)}, ...), branch_computations={%region_10.0_spmd, %region_13.0_spmd} | conditional | flops 6570222080 | bytes 131432216 | solution.py:244
  360.2 16.4 gather_fusion.6
  415.5 28.3 %all-to-all-start.1 = ((bf16[2,816,512]{2,1,0:T(8,128)(2,1)}), bf16[2,816,512]{2,1,0:T(8,128)(2,1)}, u32[]{:S(2)}, u32[]{:S(2)}) async-start(bf16[2,816,512]{2,1,0:T(8,128)(2,1)} %get-tuple-element.374), calls=%async_computation.1 | async-start | bytes 3342336 | tf_op jit(solution)/shard_map/all_to_all | solution.py:247
  450.0 57.1 %conditional.8 = (bf16[2,816,512]{2,1,0:T(8,128)(2,1)}, f32[2,816,512]{2,1,0:T(8,128)}, f32[2,68,512]{2,1,0:T(8,128)S(1)}, f32[2,68,512]{2,1,0:T(8,128)}) conditional(s32[]{:T(128)} %convert_element_type.450, (bf16[2,816,512]{2,0,1:T(2,128)(2,1)}, bf16[92,512,512]{2,1,0:T(8,128)(2,1)}, f32[4,512]{1,0:T(4,128)S(1)}, ...), branch_computations={%region_0.3_spmd, %region_3.6_spmd} | conditional | flops 6570222080 | bytes 131432216 | solution.py:244
  458.3 16.4 gather_fusion.4
  513.1 34.7 %all-to-all-start = ((bf16[2,816,512]{2,1,0:T(8,128)(2,1)}), bf16[2,816,512]{2,1,0:T(8,128)(2,1)}, u32[]{:S(2)}, u32[]{:S(2)}) async-start(bf16[2,816,512]{2,1,0:T(8,128)(2,1)} %get-tuple-element.373), calls=%async_computation | async-start | bytes 3342336 | tf_op jit(solution)/shard_map/all_to_all | solution.py:247
  577.6 51.1 %multiply_convert_fusion.2 = (bf16[816,2048]{1,0:T(8,128)(2,1)S(1)}, f32[816,2048]{1,0:T(8,128)}, bf16[816,2048]{1,0:T(8,128)(2,1)S(1)}, f32[816,2048]{1,0:T(8,1...) fusion(f32[2048]{0:T(1024)S(1)} %copy-done.153, f32[816,2048]{1,0:T(8,128)S(1)} %fusion.625, ...), kind=kOutput, calls=%fused_computation.503 | convolution fusion | flops 2044256256 | bytes 53922176 | tf_op jit(solution)/shard_map/btd,df->btf/dot_general | solution.py:257
  709.6 32.9 %all_to_all.99 = bf16[2,2,208896]{2,1,0:T(2,128)(2,1)S(1)} all-to-all(bf16[2,2,208896]{2,1,0:T(2,128)(2,1)} %reshape.2176), channel_id=1, replica_groups=mesh['branch'=2,'dp'=16] {'branch'}, dimensions={0} | all-to-all | bytes 3342336 | tf_op jit(solution)/shard_map/all_to_all | solution.py:298
  755.0 72.9 %conditional.13 = (f32[5,512]{1,0:T(8,128)S(1)}, bf16[2,68,512]{2,1,0:T(8,128)(2,1)S(1)}, bf16[2,68,512]{2,1,0:T(8,128)(2,1)S(1)}, bf16[2,816,512]{2,1,0:T(8,128...) conditional(s32[]{:T(128)} %convert_element_type.450, (f32[2,816,512]{2,1,0:T(8,128)}, ...), branch_computations={%region_84.94_spmd, %region_94.104_spmd} | conditional | flops 6586659328 | bytes 125944344 | solution.py:299
  776.3 16.4 gather_fusion.14
  861.2 27.8 %all_to_all.100 = bf16[2,2,208896]{2,1,0:T(2,128)(2,1)S(1)} all-to-all(bf16[2,2,208896]{2,1,0:T(2,128)(2,1)} %reshape.2180), channel_id=1, replica_groups=mesh['branch'=2,'dp'=16] {'branch'}, dimensions={0} | all-to-all | bytes 3342336 | tf_op jit(solution)/shard_map/all_to_all | solution.py:298
  901.5 73.3 %conditional.11 = (f32[5,512]{1,0:T(8,128)S(1)}, bf16[2,68,512]{2,1,0:T(8,128)(2,1)S(1)}, bf16[2,68,512]{2,1,0:T(8,128)(2,1)S(1)}, bf16[2,816,512]{2,1,0:T(8,128...) conditional(s32[]{:T(128)} %convert_element_type.450, (f32[2,816,512]{2,1,0:T(8,128)}, ...), branch_computations={%region_34.44_spmd, %region_44.54_spmd} | conditional | flops 6586659328 | bytes 125944344 | solution.py:299
  923.1 16.4 gather_fusion.10
  939.5 14.6 convert_reduce_fusion.3
  1008.0 34.4 %all_to_all.101 = bf16[2,2,208896]{2,1,0:T(2,128)(2,1)S(1)} all-to-all(bf16[2,2,208896]{2,1,0:T(2,128)(2,1)} %reshape.2178), channel_id=1, replica_groups=mesh['branch'=2,'dp'=16] {'branch'}, dimensions={0} | all-to-all | bytes 3342336 | tf_op jit(solution)/shard_map/all_to_all | solution.py:298
  1054.9 75.0 %conditional.12 = (f32[5,512]{1,0:T(8,128)S(1)}, bf16[2,68,512]{2,1,0:T(8,128)(2,1)}, bf16[2,68,512]{2,1,0:T(8,128)(2,1)S(1)}, bf16[2,816,512]{2,1,0:T(8,128)(2,...) conditional(s32[]{:T(128)} %convert_element_type.450, (f32[2,816,512]{2,1,0:T(8,128)}, ...), branch_computations={%region_59.69_spmd, %region_69.79_spmd} | conditional | flops 6586659328 | bytes 124838360 | solution.py:299
  1076.3 16.4 gather_fusion.12
  1092.7 14.6 convert_reduce_fusion.11
  1144.0 65.2 %conditional.15 = (f32[46,512,512]{2,1,0:T(8,128)}) conditional(s32[]{:T(128)} %convert_element_type.450, (bf16[6,68,512]{2,0,1:T(8,128)(2,1)S(1)}, bf16[6,68,512]{2,1,0:T(8,128)(2,1)S(1)}, bf16[6,816,512]{2,1,0:T(8,128)(2,1)}, bf16[6,68,512]{2,1,0:T(8,128)(2,1)S(1)}) %tuple.367, (bf16[6,68,512]{2,0,1:T(8,128)(2,1)S(1)}, ...), branch_computations={%region_108.109_spmd, %region_109.110_spmd} | conditional | flops 9851908096 | bytes 204500416 | solution.py:184
  1178.5 30.4 %maximum_maximum_fusion = f32[46,512,512]{2,1,0:T(8,128)} fusion(f32[16,512,512]{2,1,0:T(8,128)} %convolution_bitcast_fusion.2, f32[21,512,512]{2,1,0:T(8,128)} %convolution_bitcast_fusion.3, f32[46]{0:T(128)S(1)} %pad.72.clone), kind=kLoop, calls=%fused_computation.441 | loop fusion | flops 24117248 | bytes 87031992 | tf_op jit(solution)/shard_map/cond/branch_0_fun/concatenate | solution.py:178
  1211.1 125.9 %conditional.14 = (f32[46,512,512]{2,1,0:T(8,128)}) conditional(s32[]{:T(128)} %convert_element_type.450, (bf16[6,816,512]{2,1,0:T(8,128)(2,1)}, bf16[6,68,512]{2,1,0:T(8,128)(2,1)S(1)}, bf16[6,68,512]{2,0,1:T(8,128)(2,1)S(1)}, bf16[6,68,512]{2,1,0:T(8,128)(2,1)S(1)}) %tuple.369, (bf16[6,816,512]{2,1,0:T(8,128)(2,1)}, ...), branch_computations={%region_105.106_spmd, %region_106.107_spmd} | conditional | flops 9851908096 | bytes 204500128 | solution.py:184
  1225.4 27.0 %convolution_bitcast_fusion.1 = f32[16,512,512]{2,1,0:T(8,128)} fusion(bf16[6,51,16,512]{3,2,1,0:T(8,128)(2,1)} %bitcast.947, bf16[6,68,512]{2,1,0:T(8,128)(2,1)S(1)} %get-tuple-element.317), kind=kOutput, calls=%fused_computation.422 | convolution fusion | flops 2566914048 | bytes 22134784 | tf_op jit(solution)/shard_map/cond/branch_0_fun/btrd,bto->rdo/dot_general | solution.py:148
  1252.3 33.1 %convolution_bitcast_fusion = f32[30,512,512]{2,1,0:T(8,128)} fusion(bf16[51,30,6,512]{3,2,1,0:T(8,128)(2,1)} %bitcast.973, bf16[6,68,512]{2,1,0:T(8,128)(2,1)S(1)} %get-tuple-element.319), kind=kOutput, calls=%fused_computation.419 | convolution fusion | flops 4812963840 | bytes 41201664 | tf_op jit(solution)/shard_map/cond/branch_0_fun/btsd,bto->sdo/dot_general | solution.py:159
  1285.5 38.1 %pad_maximum_fusion = f32[46,512,512]{2,1,0:T(8,128)} fusion(f32[30,512,512]{2,1,0:T(8,128)} %convolution_bitcast_fusion, f32[16,512,512]{2,1,0:T(8,128)} %convolution_bitcast_fusion.1), kind=kLoop, calls=%fused_computation.418 | loop fusion | flops 12058624 | bytes 96468992 | tf_op jit(solution)/shard_map/cond/branch_0_fun/concatenate | solution.py:178
  1369.7 67.3 %all-reduce.28 = (f32[2,5,512]{2,1,0:T(8,128)S(1)}, f32[2048]{0:T(1024)}, f32[4,512]{1,0:T(4,128)}, f32[2,512]{1,0:T(2,128)}) all-reduce(f32[2,5,512]{2,1,0:T(8,128)S(1)} %broadcast_select_fusion, f32[2048]{0:T(1024)S(1)} %add_add_fusion.19, f32[4,512]{1,0:T(4,128)S(1)} %fusion.613, ...), channel_id=1, replica_groups=mesh['branch'=2,'dp'=16] {'branch','dp'}, use_global_device_ids=true, to_apply=%region_111.112 | all-reduce | flops 10240 | bytes 81920 | tf_op jit(solution)/shard_map/psum | solution.py:339
  1441.5 255.9 %reduce-scatter.14.cloned.1.call-done = f32[1472,512]{1,0:T(8,128)} async-done(((f32[23552,512]{1,0:T(8,128)}), f32[1472,512]{1,0:T(8,128)}) %reduce-scatter.14.cloned.1.call-update) | async-done | bytes 3014672 | tf_op jit(solution)/shard_map/reduce_scatter | solution.py:337
  1697.4 453.8 %reduce-scatter.12.cloned.1.call-done = f32[1472,512]{1,0:T(8,128)} async-done(((f32[23552,512]{1,0:T(8,128)}), f32[1472,512]{1,0:T(8,128)}) %reduce-scatter.12.cloned.1.call-update) | async-done | bytes 3014672 | tf_op jit(solution)/shard_map/reduce_scatter | solution.py:337
  2157.2 204.5 %all-reduce.32.cloned.1.call-done = (f32[1024,512]{1,0:T(8,128)}, f32[512,2048]{1,0:T(8,128)}, f32[2048,512]{1,0:T(8,128)}) async-done(((f32[1024,512]{1,0:T(8,128)}, f32[512,2048]{1,0:T(8,128)}, f32[2048,512]{1,0:T(8,128)}), (f32[1024,512]{1,0:T(8,128)}, f32[512,2048]{1,0:T(8,128)}, f32[2048,512]{1,0:T(8,128)})) %all-reduce.32.cloned.1.call-update) | async-done | bytes 10485776 | tf_op jit(solution)/shard_map/psum | solution.py:339
  (571 shorter events, 568.3 us)
Async XLA Ops:
  7.2 565.1 %copy-start = (bf16[512,2048]{1,0:T(8,128)(2,1)S(1)}, bf16[512,2048]{1,0:T(8,128)(2,1)}, u32[]{:S(2)}) copy-start(bf16[512,2048]{1,0:T(8,128)(2,1)} %param.34) | copy-start | bytes 6291460
  7.2 241.1 %all-gather.2.cloned.1.call-start = ((), (), s32[]{:S(2)}) async-start(), calls=%async_computation.11 | async-start | bytes 51249152 | tf_op jit(solution)/shard_map/all_gather | solution.py:216
  12.7 235.6 %copy-start.71 = (f32[1,512]{1,0:T(1,128)S(1)}, f32[1,512]{1,0:T(1,128)}, u32[]{:S(2)}) copy-start(f32[1,512]{1,0:T(1,128)} %param.31) | copy-start | bytes 6148
  12.7 235.6 %copy-start.87 = (f32[1,4,512]{2,1,0:T(4,128)S(1)}, f32[1,4,512]{2,1,0:T(4,128)}, u32[]{:S(2)}) copy-start(f32[1,4,512]{2,1,0:T(4,128)} %param.32) | copy-start | bytes 24580
  312.2 39.6 %copy-start.73 = (f32[2,68,512]{2,1,0:T(8,128)}, f32[2,68,512]{2,1,0:T(8,128)S(1)}, u32[]{:S(2)}) copy-start(f32[2,68,512]{2,1,0:T(8,128)S(1)} %get-tuple-element.388) | copy-start | bytes 835588
  312.2 103.2 %all-to-all-start.2 = ((bf16[2,816,512]{2,1,0:T(8,128)(2,1)}), bf16[2,816,512]{2,1,0:T(8,128)(2,1)}, u32[]{:S(2)}, u32[]{:S(2)}) async-start(bf16[2,816,512]{2,1,0:T(8,128)(2,1)} %get-tuple-element.375), calls=%async_computation.2 | async-start | bytes 3342336 | tf_op jit(solution)/shard_map/all_to_all | solution.py:247
  415.4 33.9 %copy-start.76 = (f32[2,68,512]{2,1,0:T(8,128)}, f32[2,68,512]{2,1,0:T(8,128)S(1)}, u32[]{:S(2)}) copy-start(f32[2,68,512]{2,1,0:T(8,128)S(1)} %get-tuple-element.383) | copy-start | bytes 835588
  415.5 28.3 %copy-start.140 = (f32[2,512]{1,0:T(2,128)S(1)}, f32[2,512]{1,0:T(2,128)}, u32[]{:S(2)}) copy-start(f32[2,512]{1,0:T(2,128)} %param.38) | copy-start | bytes 12292
  415.5 33.9 %copy-start.133 = (f32[4,512]{1,0:T(4,128)S(1)}, f32[4,512]{1,0:T(4,128)}, u32[]{:S(2)}) copy-start(f32[4,512]{1,0:T(4,128)} %param.37) | copy-start | bytes 24580
  415.5 97.6 %all-to-all-start.1 = ((bf16[2,816,512]{2,1,0:T(8,128)(2,1)}), bf16[2,816,512]{2,1,0:T(8,128)(2,1)}, u32[]{:S(2)}, u32[]{:S(2)}) async-start(bf16[2,816,512]{2,1,0:T(8,128)(2,1)} %get-tuple-element.374), calls=%async_computation.1 | async-start | bytes 3342336 | tf_op jit(solution)/shard_map/all_to_all | solution.py:247
  444.4 235.6 %copy-start.88 = (f32[1,512]{1,0:T(1,128)}, f32[1,512]{1,0:T(1,128)S(1)}, u32[]{:S(2)}) copy-start(f32[1,512]{1,0:T(1,128)S(1)} %get-tuple-element.817) | copy-start | bytes 6148
  450.0 126.8 %copy-start.95 = (f32[1,512]{1,0:T(1,128)}, f32[1,512]{1,0:T(1,128)S(1)}, u32[]{:S(2)}) copy-start(f32[1,512]{1,0:T(1,128)S(1)} %get-tuple-element.813) | copy-start | bytes 6148
  513.1 61.6 %copy-start.110 = (f32[816]{0:T(1024)}, f32[816]{0:T(1024)S(1)}, u32[]{:S(2)}) copy-start(f32[816]{0:T(1024)S(1)} %broadcast_multiply_fusion.13) | copy-start | bytes 9796
  513.1 53.8 %all-to-all-start = ((bf16[2,816,512]{2,1,0:T(8,128)(2,1)}), bf16[2,816,512]{2,1,0:T(8,128)(2,1)}, u32[]{:S(2)}, u32[]{:S(2)}) async-start(bf16[2,816,512]{2,1,0:T(8,128)(2,1)} %get-tuple-element.373), calls=%async_computation | async-start | bytes 3342336 | tf_op jit(solution)/shard_map/all_to_all | solution.py:247
  547.8 890.4 %reduce-scatter.10.cloned.1.call-start = ((), (), s32[]{:S(2)}) async-start(), calls=%async_computation.14 | async-start | bytes 2506752 | tf_op jit(solution)/shard_map/reduce_scatter | solution.py:313
  552.9 19.4 copy-start.90
  554.1 16.5 copy-start.113
  554.5 16.1 copy-start.115
  554.5 20.2 copy-start.123
  554.5 17.7 copy-start.97
  571.8 108.1 %copy-start.13 = (f32[816,512]{1,0:T(8,128)}, f32[816,512]{1,0:T(8,128)S(1)}, u32[]{:S(2)}) copy-start(f32[816,512]{1,0:T(8,128)S(1)} %get-tuple-element.829) | copy-start | bytes 5013508
  571.8 108.1 %copy-start.93 = (f32[816]{0:T(1024)}, f32[816]{0:T(1024)S(1)}, u32[]{:S(2)}) copy-start(f32[816]{0:T(1024)S(1)} %broadcast_multiply_fusion.17) | copy-start | bytes 9796
  572.2 107.7 %copy-start.100 = (f32[816]{0:T(1024)}, f32[816]{0:T(1024)S(1)}, u32[]{:S(2)}) copy-start(f32[816]{0:T(1024)S(1)} %fusion.615) | copy-start | bytes 9796
  577.6 51.1 %copy-start.154 = (f32[816,2048]{1,0:T(8,128)}, f32[816,2048]{1,0:T(8,128)S(1)}, u32[]{:S(2)}) copy-start(f32[816,2048]{1,0:T(8,128)S(1)} %fusion.625) | copy-start | bytes 20054020
  577.6 51.1 %copy-start.147 = (f32[1,512]{1,0:T(1,128)S(1)}, f32[1,512]{1,0:T(1,128)}, u32[]{:S(2)}) copy-start(f32[1,512]{1,0:T(1,128)} %get-tuple-element.815) | copy-start | bytes 6148
  577.6 51.1 %copy-start.148 = (bf16[2048,512]{1,0:T(8,128)(2,1)S(1)}, bf16[2048,512]{1,0:T(8,128)(2,1)}, u32[]{:S(2)}) copy-start(bf16[2048,512]{1,0:T(8,128)(2,1)} %param.36) | copy-start | bytes 6291460
  643.5 23.4 copy-start.21
  832.8 605.3 %reduce-scatter.6.cloned.1.call-start = ((), (), s32[]{:S(2)}) async-start(), calls=%async_computation.12 | async-start | bytes 2506752 | tf_op jit(solution)/shard_map/reduce_scatter | solution.py:313
  979.7 458.4 %reduce-scatter.8.cloned.1.call-start = ((), (), s32[]{:S(2)}) async-start(), calls=%async_computation.13 | async-start | bytes 2506752 | tf_op jit(solution)/shard_map/reduce_scatter | solution.py:313
  1134.7 562.7 %reduce-scatter.14.cloned.1.call-start = ((), (), s32[]{:S(2)}) async-start(), calls=%async_computation.16 | async-start | bytes 51249152 | tf_op jit(solution)/shard_map/reduce_scatter | solution.py:337
  1209.2 942.0 %reduce-scatter.12.cloned.1.call-start = ((), (), s32[]{:S(2)}) async-start(), calls=%async_computation.15 | async-start | bytes 51249152 | tf_op jit(solution)/shard_map/reduce_scatter | solution.py:337
  1337.0 1024.7 %all-reduce.32.cloned.1.call-start = ((), (), s32[]{:S(2)}) async-start(), calls=%async_computation.17 | async-start | bytes 20971520 | tf_op jit(solution)/shard_map/psum | solution.py:339
  (124 other events, 467.4 us)
Sparse Core Ops, SparseCore 0:
  9.6 238.6 all-gather.1
  832.9 33.4 reduce-scatter.9
  979.9 41.7 reduce-scatter.5
  1134.9 41.3 reduce-scatter.7
  1209.3 488.0 reduce-scatter.13
  1702.2 448.9 reduce-scatter.11
  2158.4 203.3 all-reduce.31
where the time goes:
time: 2390 us; the launch traced here: 2380 us
  waiting for transfers between devices  1160 us (49%)
  matrix products  371 us (16%)
  local copies, waits for them, and re-layouts  265 us (11%)
  other arithmetic  227 us (9%)
  blocking collectives  163 us (7%)
  starting transfers between devices  98.6 us (4%)
  loops' own time  77.7 us (3%)
    reduce_scatter x2, waiting for transfers between devices, per_device(): lax.psum_scatter(term, 'dp', scatter_dimension=0, tiled=True)  710 us
    all_gather x1, waiting for transfers between devices, per_device(): gathered = lax.all_gather(branch_blocks, 'dp', axis=2, tiled=True)  233 us
    psum x1, waiting for transfers between devices, per_device(): lax.psum((shared_totals[0], shared_totals[1], shared_totals[2], shared_to...  205 us
    all_to_all x3, starting transfers between devices, per_device(): lax.all_to_all(branch_out.astype(jnp.bfloat16), 'branch', split_axis=0, c...  98.2 us
    all_to_all x3, blocking collectives, per_device(): lax.all_to_all(grad_joined, 'branch', split_axis=2, concat_axis=0, tiled=...  95.2 us
    unnamed x301, local copies, waits for them, and re-layouts  68.6 us
    concatenate x2, other arithmetic, group_grads(): jnp.concatenate(pieces, axis=0).reshape(per_group * channels, channels)  68.6 us
    psum x1, blocking collectives, per_device(): lax.psum((shared_totals[0], shared_totals[1], shared_totals[2], shared_to...  67.3 us
  transfers between devices with their start and end apart: 10, of which 5 were waited for; matrix products, arithmetic and copies ran while one was open for 24% of the time, Pallas kernels for 0%

commit v1 on v0

v1 whole, which is shorter than its diff:
```python
import functools
import jax, jax.numpy as jnp
from jax import lax
from jax.experimental import pallas as pl
from jax.experimental.pallas import tpu as pltpu

MESH = pl.DeviceIdType.MESH
ANY = pl.BlockSpec(memory_space=pl.ANY)


def place():
    me = lax.axis_index("dp")
    return lax.axis_index("branch"), me, me // 4, (me // 2) % 2, me % 2


def meet(depth, b, me, z):
    barrier = pltpu.get_barrier_semaphore()
    y, c = (me // 2) % 2, me % 2
    pl.semaphore_signal(barrier, 1, device_id=(b, me + 1 - 2 * c), device_id_type=MESH)
    pl.semaphore_signal(barrier, 1, device_id=(b, me + 2 - 4 * y), device_id_type=MESH)

    @pl.when(z > 0)
    def _():
        pl.semaphore_signal(barrier, 1, device_id=(b, me - 4), device_id_type=MESH)

    @pl.when(z < depth - 1)
    def _():
        pl.semaphore_signal(barrier, 1, device_id=(b, me + 4), device_id_type=MESH)

    count = 2 + jnp.where(z > 0, 1, 0) + jnp.where(z < depth - 1, 1, 0)
    pl.semaphore_wait(barrier, count)


def gather_body(depth, npd, rows, base, ranges, swaps, src, dst, hold, local_sem, recv_sem, send_sem):
    b, me, z, y, c = place()
    meet(depth, b, me, z)
    (a0, a1), (b0, b1) = ranges
    q0 = jnp.where(b == 0, a0, b0)
    q1 = jnp.where(b == 0, a1, b1)
    swap = jnp.where(b == 0, swaps[0], swaps[1])
    core_peer, y_peer = (b, me + 1 - 2 * c), (b, me + 2 - 4 * y)

    def chunk(ref, index):
        return ref.at[pl.ds(pl.multiple_of(index * rows, 8), rows), :]

    def own(i):
        return src.at[pl.ds(pl.multiple_of(base + i * rows, 8), rows), :]

    def remote(kind, q, device, from_own=False):
        k = q - q0
        return pltpu.make_async_remote_copy(
            own(q - me * npd) if from_own else chunk(dst, k), chunk(dst, k), send_sem.at[kind, k], recv_sem.at[k],
            device_id=device, device_id_type=MESH,
        )

    def each_own(what):
        for i in range(npd):
            q = me * npd + i

            @pl.when(jnp.logical_and(q >= q0, q < q1))
            def _():
                what(q, i)

    def take(q, i):
        return pltpu.make_async_copy(own(i), hold.at[i], local_sem.at[0, i])

    def put(q, i):
        return pltpu.make_async_copy(hold.at[i], chunk(dst, q - q0), local_sem.at[1, i])

    each_own(lambda q, i: take(q, i).start())

    def column(j):
        ys = (j // 2) % 2
        return jnp.where(j == swap, 1 - ys, ys)

    def each(core, steps, what):
        def over(zs, t, s):
            for ys in (y, 1 - y):
                j = (zs * 2 + ys) * 2 + core
                col = column(j)
                i = s - t - jnp.where(ys != col, 1, 0) - jnp.where(y != col, 1, 0)
                i = jnp.where(jnp.logical_and(t == 0, ys == y), s, i)
                q = j * npd + i

                @pl.when(jnp.logical_and(jnp.logical_and(i >= 0, i < npd), jnp.logical_and(q >= q0, q < q1)))
                def _():
                    what(q, j)

        def over_steps(s, carry):
            def over_far(t, inner):
                @pl.when(z >= t)
                def _():
                    over(z - t, t, s)

                @pl.when(jnp.logical_and(z + t < depth, t > 0))
                def _():
                    over(z + t, t, s)

                return inner

            return lax.fori_loop(0, depth, over_far, carry)

        lax.fori_loop(0, npd + depth + 1, over_steps, 0)

    def sends(q, j, act, from_own=False):
        zs, ys = j // 4, (j // 2) % 2
        col = column(j)
        chain = y == col

        @pl.when(jnp.logical_and(chain, jnp.logical_and(z >= zs, z < depth - 1)))
        def _():
            act(remote(0, q, (b, me + 4), from_own))

        @pl.when(jnp.logical_and(chain, jnp.logical_and(z <= zs, z > 0)))
        def _():
            act(remote(1, q, (b, me - 4), from_own))

        start_here = jnp.logical_and(z == zs, ys != col)

        @pl.when(chain != start_here)
        def _():
            act(remote(2, q, y_peer, from_own))

        act(remote(3, q, core_peer, from_own))

    def forward(q, j):
        @pl.when(me == j)
        def _():
            sends(q, j, lambda copy: copy.start(), True)

        @pl.when(me != j)
        def _():
            remote(3, q, core_peer).wait_recv()
            sends(q, j, lambda copy: copy.start())

    each(c, npd + depth + 1, forward)

    def swap_own(q, i):
        take(q, i).wait()
        put(q, i).start()

    each_own(swap_own)

    def finish(q, carry):
        j = q // npd

        @pl.when(c == j % 2)
        def _():
            sends(q, j, lambda copy: copy.wait_send())

        @pl.when(c != j % 2)
        def _():
            remote(3, q, core_peer).wait_recv()

        return carry

    lax.fori_loop(q0, q1, finish, 0)
    each_own(lambda q, i: put(q, i).wait())


def gather_rows(mesh, src, base, rows, npd, ranges, collective_id, swaps=(-1, -1)):
    depth = mesh.shape["dp"] // 4
    count = max(r[1] - r[0] for r in ranges)
    return pl.pallas_call(
        functools.partial(gather_body, depth, npd, rows, base, ranges, swaps),
        out_shape=jax.ShapeDtypeStruct((count * rows, src.shape[1]), src.dtype),
        in_specs=[ANY],
        out_specs=ANY,
        scratch_shapes=[
            pltpu.VMEM((npd, rows, src.shape[1]), src.dtype),
            pltpu.SemaphoreType.DMA((2, npd)),
            pltpu.SemaphoreType.DMA((count,)),
            pltpu.SemaphoreType.DMA((4, count)),
        ],
        compiler_params=pltpu.CompilerParams(collective_id=collective_id, has_side_effects=True),
    )(src)


def reduce_body(depth, npd, rows, ranges, swaps, lag, src, out, own, rc, ry, rz, fin, acc, own_sem, rc_sem, ry_sem, rz_sem, fin_sem, send_sem, fin_send):
    b, me, z, y, c = place()
    meet(depth, b, me, z)
    (a0, a1), (b0, b1) = ranges
    q0 = jnp.where(b == 0, a0, b0)
    q1 = jnp.where(b == 0, a1, b1)
    swap = jnp.where(b == 0, swaps[0], swaps[1])
    pair0 = q0 // npd // 2
    core_peer, y_peer = (b, me + 1 - 2 * c), (b, me + 2 - 4 * y)
    up, down = (b, jnp.minimum(me + 4, 4 * depth - 1)), (b, jnp.maximum(me - 4, 0))

    def column(j):
        ys = (j // 2) % 2
        return jnp.where(j == swap, 1 - ys, ys)

    def slot(j, i):
        return (j // 2 - pair0) * npd + i

    def part(j, i):
        return src.at[pl.ds(pl.multiple_of((j * npd + i - q0) * rows, 8), rows), :]

    def keep(j, i):
        return pltpu.make_async_copy(part(j, i), own.at[slot(j, i)], own_sem.at[slot(j, i)])

    def remote(kind, frm, to, sem, k, device):
        return pltpu.make_async_remote_copy(
            frm, to, send_sem.at[kind, k], sem, device_id=device, device_id_type=MESH
        )

    def to_core(j, i):
        k = slot(j, i)
        return remote(0, part(j, i), rc.at[k], rc_sem.at[k], k, core_peer)

    def to_y(j, i):
        k = slot(j, i)
        return remote(1, own.at[k], ry.at[k], ry_sem.at[k], k, y_peer)

    def to_z(j, i, way):
        k = slot(j, i)
        return remote(2, own.at[k], rz.at[way, k], rz_sem.at[way, k], k, (up, down)[way])

    def to_owner(j, i):
        return pltpu.make_async_remote_copy(
            own.at[slot(j, i)], fin.at[i], fin_send.at[i], fin_sem.at[i], device_id=y_peer, device_id_type=MESH
        )

    def owners(n, core, what):
        pos, i = n // npd, n % npd
        rising = pos + jnp.where(pos >= z, 1, 0)
        falling = depth - 1 - pos
        falling = falling - jnp.where(falling <= z, 1, 0)
        zs = jnp.where(pos == depth - 1, z, jnp.where(z >= depth // 2, rising, falling))
        for ys in (0, 1):
            j = (zs * 2 + ys) * 2 + core
            q = j * npd + i

            @pl.when(jnp.logical_and(q >= q0, q < q1))
            def _():
                what(j, i, zs, ys)

    total = depth * npd

    def begin(n, carry):
        owners(n, 1 - c, lambda j, i, zs, ys: to_core(j, i).start())
        owners(n, c, lambda j, i, zs, ys: keep(j, i).start())
        return carry

    lax.fori_loop(0, total, begin, 0)

    def cross(j, i, zs, ys):
        @pl.when(column(j) != y)
        def _():
            k = slot(j, i)
            keep(j, i).wait()
            to_core(j, i).wait_recv()
            own[k] = (own[k].astype(jnp.float32) + rc[k].astype(jnp.float32)).astype(own.dtype)
            to_y(j, i).start()

    def chain(j, i, zs, ys):
        @pl.when(column(j) == y)
        def _():
            k = slot(j, i)
            keep(j, i).wait()
            to_core(j, i).wait_recv()
            to_y(j, i).wait_recv()
            acc[...] = own[k].astype(jnp.float32) + rc[k].astype(jnp.float32) + ry[k].astype(jnp.float32)

            @pl.when(jnp.logical_and(z >= zs, z < depth - 1))
            def _():
                to_z(j, i, 1).wait_recv()
                acc[...] += rz[1, k].astype(jnp.float32)

            @pl.when(jnp.logical_and(z <= zs, z > 0))
            def _():
                to_z(j, i, 0).wait_recv()
                acc[...] += rz[0, k].astype(jnp.float32)

            @pl.when(jnp.logical_and(z == zs, ys == y))
            def _():
                out[i] = acc[...].astype(out.dtype)

            @pl.when(jnp.logical_not(jnp.logical_and(z == zs, ys == y)))
            def _():
                own[k] = acc[...].astype(own.dtype)

            @pl.when(z > zs)
            def _():
                to_z(j, i, 1).start()

            @pl.when(z < zs)
            def _():
                to_z(j, i, 0).start()

            @pl.when(jnp.logical_and(z == zs, ys != y))
            def _():
                to_owner(j, i).start()

    def step(s, carry):
        @pl.when(s < total)
        def _():
            owners(s, c, cross)

        @pl.when(s >= lag)
        def _():
            owners(s - lag, c, chain)

        return carry

    lax.fori_loop(0, total + lag, step, 0)

    def sent(j, i, zs, ys):
        @pl.when(column(j) != y)
        def _():
            to_y(j, i).wait_send()

            @pl.when(me == j)
            def _():
                to_owner(j, i).wait_recv()
                out[i] = fin[i].astype(out.dtype)

        @pl.when(column(j) == y)
        def _():
            @pl.when(z != zs)
            def _():
                to_z(j, i, 0).wait_send()

            @pl.when(jnp.logical_and(z == zs, ys != y))
            def _():
                to_owner(j, i).wait_send()

    def end(n, carry):
        owners(n, 1 - c, lambda j, i, zs, ys: to_core(j, i).wait_send())
        owners(n, c, sent)
        return carry

    lax.fori_loop(0, total, end, 0)


def reduce_rows(mesh, src, rows, npd, ranges, collective_id, dtype, swaps=(-1, -1), lag=2):
    depth = mesh.shape["dp"] // 4
    pairs = max((r[1] + npd - 1) // npd // 2 + (r[1] + npd - 1) // npd % 2 - r[0] // npd // 2 for r in ranges)
    held, width = pairs * npd, src.shape[1]
    block = (held, rows, width)
    return pl.pallas_call(
        functools.partial(reduce_body, depth, npd, rows, ranges, swaps, lag),
        out_shape=jax.ShapeDtypeStruct((npd, rows, width), dtype),
        in_specs=[ANY],
        out_specs=pl.BlockSpec(memory_space=pltpu.VMEM),
        scratch_shapes=[
            pltpu.VMEM(block, src.dtype),
            pltpu.VMEM(block, src.dtype),
            pltpu.VMEM(block, src.dtype),
            pltpu.VMEM((2, *block), src.dtype),
            pltpu.VMEM((npd, rows, width), src.dtype),
            pltpu.VMEM((rows, width), jnp.float32),
            pltpu.SemaphoreType.DMA((held,)),
            pltpu.SemaphoreType.DMA((held,)),
            pltpu.SemaphoreType.DMA((held,)),
            pltpu.SemaphoreType.DMA((2, held)),
            pltpu.SemaphoreType.DMA((npd,)),
            pltpu.SemaphoreType.DMA((3, held)),
            pltpu.SemaphoreType.DMA((npd,)),
        ],
        compiler_params=pltpu.CompilerParams(
            collective_id=collective_id, has_side_effects=True, vmem_limit_bytes=50 * 2**20
        ),
    )(src)
SCALES = (12, 16)
MICRO = 3
GROUPS = 2
EPSILON = 1e-05
BF, F32 = jnp.bfloat16, jnp.float32
MIB = 2**20


def up_to(value, step):
    return (value + step - 1) // step * step


def dot(a, b):
    return jnp.dot(a, b, preferred_element_type=F32)


def dot_bt(a, b):
    return lax.dot_general(a, b, (((1,), (1,)), ((), ())), preferred_element_type=F32)


def dot_at(a, b):
    return lax.dot_general(a, b, (((0,), (0,)), ((), ())), preferred_element_type=F32)


def mean(values):
    return jnp.mean(values, axis=-1, keepdims=True)


def normalise(values):
    centre = values - mean(values)
    rho = lax.rsqrt(mean(centre * centre) + EPSILON)
    return centre * rho, rho


def norm_back(q_gain, xhat, rho):
    return rho * (q_gain - mean(q_gain) - xhat * mean(q_gain * xhat))


def column_sum(values):
    return jnp.sum(values, axis=0, keepdims=True)


VMEM = pl.BlockSpec(memory_space=pltpu.VMEM)


def whole_call(body, out_shape, scratch, limit, cost=None):
    return pl.pallas_call(
        body,
        out_shape=out_shape,
        out_specs=jax.tree.map(lambda _: VMEM, out_shape),
        scratch_shapes=scratch,
        compiler_params=pltpu.CompilerParams(vmem_limit_bytes=limit * MIB),
        cost_estimate=cost,
    )


LANES = 128


def panels(ref, lead, rows):
    return jnp.concatenate([ref[(*lead, p, rows, slice(None))] for p in range(ref.shape[-3])], axis=1)


def set_panels(ref, lead, rows, values):
    for p in range(ref.shape[-3]):
        ref[(*lead, p, rows, slice(None))] = values[:, p * LANES : (p + 1) * LANES]


def down_body(k, n, pitch, off, x, weight, bias, pre, act, taps, spread):
    slots, length, width = x.shape
    many = slots * pitch
    spread[:, length:, :] = jnp.zeros((spread.shape[0], spread.shape[1] - length, LANES), F32)

    def window(w, carry):
        set_panels(spread, (), slice(0, length), x[w].astype(F32))
        for r in range(k):
            taps[pl.ds(pl.multiple_of(w * pitch, 16), pitch), r * width : (r + 1) * width] = panels(
                spread, (), pl.ds(r, pitch, stride=k)
            ).astype(BF)
        return carry

    lax.fori_loop(0, slots, window, 0)
    total = dot(taps[:many, : k * width], weight[off : off + k * width, :]) + bias[0:1, :]
    tall = pre.shape[1]
    for w in range(slots):
        rows = fit(total[w * pitch : (w + 1) * pitch], tall)
        pre[w] = rows
        step = lax.broadcasted_iota(jnp.int32, rows.shape, 0)
        act[w] = jnp.where(step < n, jnp.tanh(rows), 0.0).astype(BF)


def fit(values, tall):
    rows = values.shape[0]
    if rows >= tall:
        return values[:tall]
    return jnp.concatenate([values, jnp.zeros((tall - rows, values.shape[1]), values.dtype)], axis=0)


def expand(k, n, pitch, off, iso_rows, weight, spread):
    width = iso_rows.shape[1]
    slots = spread.shape[0]

    def tap(r, carry):
        rows = dot(iso_rows[...], weight[pl.ds(pl.multiple_of(off + r * width, 16), width), :])
        for w in range(slots):
            set_panels(spread, (w,), pl.ds(r, pitch, stride=k), rows[w * pitch : (w + 1) * pitch])
        return carry

    lax.fori_loop(0, k, tap, 0)


def iso_of(n, pitch, pre_iso, bias):
    rows = fit(jnp.tanh(pre_iso + bias[1:2, :]), pitch)
    step = lax.broadcasted_iota(jnp.int32, rows.shape, 0)
    return jnp.where(step < n, rows, 0.0)


def up_body(k, n, pitch, off, live, pre_iso, weight, x, gain, bias, out, iso_rows, spread):
    slots, length, width = x.shape
    for w in range(slots):
        iso = iso_of(n, pitch, pre_iso[w], bias)
        iso_rows[w * pitch : (w + 1) * pitch, :] = jnp.where(w < live[0], iso, 0.0).astype(BF)
    expand(k, n, pitch, off, iso_rows, weight, spread)

    def window(w, carry):
        values = panels(spread, (w,), slice(0, length)) + bias[2:3, :] + x[w].astype(F32)
        xhat, _ = normalise(values)
        out[w] = (xhat * gain[0:1, :] + bias[3:4, :]).astype(BF)
        return carry

    lax.fori_loop(0, slots, window, 0)


def up_back_body(k, n, pitch, off, live, grad, pre_iso, weight, x, gain, bias, grad_iso, vectors, grad_taps, part, iso_rows, spread):
    slots, length, width = x.shape
    for w in range(slots):
        iso = iso_of(n, pitch, pre_iso[w], bias)
        iso_rows[w * pitch : (w + 1) * pitch, :] = jnp.where(w < live[0], iso, 0.0).astype(BF)
    expand(k, n, pitch, off, iso_rows, weight, spread)
    vectors[...] = jnp.zeros_like(vectors)

    def window(w, carry):
        values = panels(spread, (w,), slice(0, length)) + bias[2:3, :] + x[w].astype(F32)
        xhat, rho = normalise(values)
        q = grad[w].astype(F32)
        residual = norm_back(q * gain[0:1, :], xhat, rho)
        set_panels(spread, (w,), slice(0, length), residual)
        vectors[0:1, :] += column_sum(q * xhat)
        vectors[3:4, :] += column_sum(residual.astype(BF).astype(F32))
        vectors[4:5, :] += column_sum(q)
        return carry

    lax.fori_loop(0, slots, window, 0)

    def tap(w, carry):
        for r in range(k):
            grad_taps[pl.ds(pl.multiple_of(w * pitch, 16), pitch), r * width : (r + 1) * width] = panels(
                spread, (w,), pl.ds(r, pitch, stride=k)
            ).astype(BF)
        return carry

    lax.fori_loop(0, slots, tap, 0)
    total = jnp.zeros((slots * pitch, width), F32)
    for r in range(k):
        rows = grad_taps[: slots * pitch, r * width : (r + 1) * width]
        total += dot_bt(rows, weight[off + r * width : off + (r + 1) * width, :])
        part[off + r * width : off + (r + 1) * width, :] = dot_at(iso_rows[...], rows).astype(BF)
    tall = grad_iso.shape[1]
    for w in range(slots):
        iso = iso_of(n, pitch, pre_iso[w], bias)
        slope = jnp.where(lax.broadcasted_iota(jnp.int32, iso.shape, 0) < n, 1.0 - iso * iso, 0.0)
        back = total[w * pitch : (w + 1) * pitch] * slope
        back = jnp.where(w < live[0], back, 0.0).astype(BF)
        vectors[2:3, :] += column_sum(back.astype(F32))
        grad_iso[w] = fit(back.astype(F32), tall).astype(BF)


def down_back_body(k, n, pitch, off, live, grad_act, pre, grad_taps, taps, weight, out, vector, part, rows, spread):
    slots, length, width = out.shape
    vector[...] = jnp.zeros_like(vector)
    for w in range(slots):
        act = jnp.tanh(fit(pre[w], pitch))
        step = lax.broadcasted_iota(jnp.int32, act.shape, 0)
        back = fit(grad_act[w], pitch) * (1.0 - act * act)
        back = jnp.where(jnp.logical_and(step < n, w < live[0]), back, 0.0).astype(BF)
        vector[...] += column_sum(back.astype(F32))
        rows[w * pitch : (w + 1) * pitch, :] = back
    for r in range(k):
        back = dot_bt(rows[...], weight[off + r * width : off + (r + 1) * width, :])
        back += grad_taps[: slots * pitch, r * width : (r + 1) * width].astype(F32)
        for w in range(slots):
            set_panels(spread, (w,), pl.ds(r, pitch, stride=k), back[w * pitch : (w + 1) * pitch])
        part[off + r * width : off + (r + 1) * width, :] = dot_at(
            taps[: slots * pitch, r * width : (r + 1) * width], rows[...]
        ).astype(BF)

    def window(w, carry):
        out[w] = panels(spread, (w,), slice(0, length)).astype(BF)
        return carry

    lax.fori_loop(0, slots, window, 0)


SUBLANES = 8


def shifted(copies, start, tall):
    rows = pl.multiple_of(start // SUBLANES * SUBLANES, SUBLANES)
    return copies[start % SUBLANES, pl.ds(rows, tall), :].astype(BF)


def late_copies(copies, values):
    tall = values.shape[0]
    for b in range(SUBLANES):
        copies[b, tall - b : 2 * tall - b, :] = values


def early_copies(copies, values):
    tall = values.shape[0]
    for b in range(SUBLANES):
        copies[b, : tall - b, :] = values[b:]


PACK = 8


def iso_specs(tall, width, pieces):
    def spec(e):
        def at(step, order, count, shift):
            last = jnp.maximum(count[0] - 1, 0) // PACK
            return order[jnp.minimum(step, last) * PACK + e], 0, 0

        return pl.BlockSpec((1, tall, width), at)

    return [spec(e) for e in range(PACK)]


def scatter_out(order, count, slots_ref, sem, out, tall, step, steps):
    def copy(at, e):
        where = jnp.minimum(at * PACK + e, order.shape[0] - 1)
        return pltpu.make_async_copy(
            slots_ref.at[at % 2, e], out.at[order[where]], sem.at[at % 2, e]
        )

    live = pl.cdiv(count[0], PACK)

    @pl.when(step < live)
    def _():
        for e in range(PACK):
            @pl.when(step * PACK + e < count[0])
            def _():
                copy(step, e).start()

    @pl.when(jnp.logical_and(step >= 1, step <= live))
    def _():
        for e in range(PACK):
            @pl.when((step - 1) * PACK + e < count[0])
            def _():
                copy(step - 1, e).wait()

    @pl.when(jnp.logical_and(step == steps - 1, live == steps))
    def _():
        for e in range(PACK):
            @pl.when(step * PACK + e < count[0])
            def _():
                copy(step, e).wait()


def iso_forward_body(tall, pitch, blocks, steps, order, count, shift, *refs):
    acts, (weight, out, buffer, columns, ready, sem) = refs[:PACK], refs[PACK:]
    step = pl.program_id(0)
    width = weight.shape[1]

    @pl.when(step == 0)
    def _():
        buffer[...] = jnp.zeros_like(buffer)
        columns[...] = jnp.zeros_like(columns)

    @pl.when(step * PACK < count[0])
    def _():
        for e in range(PACK):
            late_copies(buffer, jnp.where(step * PACK + e < count[0], acts[e][0].astype(F32), 0.0))
            for m in range(blocks):
                columns[e * pitch : e * pitch + tall, m * width : (m + 1) * width] = shifted(buffer, tall - shift[m], tall)
        total = dot(columns[...], weight[...])
        for e in range(PACK):
            ready[step % 2, e] = total[e * pitch : e * pitch + tall].astype(BF)

    scatter_out(order, count, ready, sem, out, tall, step, steps)


def iso_back_body(tall, pitch, blocks, steps, order, count, shift, *refs):
    acts, grads = refs[:PACK], refs[PACK : 2 * PACK]
    weight, out, kernel_grad, buffer, columns, gathered, ahead, ready, sem = refs[2 * PACK :]
    step = pl.program_id(0)
    width = weight.shape[1]

    @pl.when(step == 0)
    def _():
        buffer[...] = jnp.zeros_like(buffer)
        columns[...] = jnp.zeros_like(columns)
        gathered[...] = jnp.zeros_like(gathered)
        ahead[...] = jnp.zeros_like(ahead)
        kernel_grad[...] = jnp.zeros_like(kernel_grad)

    @pl.when(step * PACK < count[0])
    def _():
        for e in range(PACK):
            alive = step * PACK + e < count[0]
            late_copies(buffer, jnp.where(alive, acts[e][0].astype(F32), 0.0))
            for m in range(blocks):
                columns[e * pitch : e * pitch + tall, m * width : (m + 1) * width] = shifted(buffer, tall - shift[m], tall)
            gathered[e * pitch : e * pitch + tall, :] = jnp.where(alive, grads[e][0].astype(F32), 0.0).astype(BF)
        for m in range(blocks):
            kernel_grad[m * width : (m + 1) * width, :] += dot_at(columns[:, m * width : (m + 1) * width], gathered[...])
        for e in range(PACK):
            alive = step * PACK + e < count[0]
            early_copies(ahead, jnp.where(alive, grads[e][0].astype(F32), 0.0))
            for m in range(blocks):
                columns[e * pitch : e * pitch + tall, m * width : (m + 1) * width] = shifted(ahead, shift[m], tall)
        total = dot_bt(columns[:, :width], weight[:width, :])
        for m in range(1, blocks):
            total += dot_bt(columns[:, m * width : (m + 1) * width], weight[m * width : (m + 1) * width, :])
        for e in range(PACK):
            ready[step % 2, e] = total[e * pitch : e * pitch + tall].astype(BF)

    scatter_out(order, count, ready, sem, out, tall, step, steps)


def iso_call(back, order, count, shift, weight, *windows):
    many, tall, width = windows[0].shape
    blocks = weight.shape[0] // width
    pitch = up_to(tall, 16)
    steps = many // PACK
    held = pl.BlockSpec(weight.shape, lambda step, *_: (0, 0))
    out_shape = [jax.ShapeDtypeStruct((many, tall, width), BF)]
    out_specs = [ANY]
    copies = pltpu.VMEM((SUBLANES, 2 * tall, width), F32)
    scratch = [copies, pltpu.VMEM((PACK * pitch, blocks * width), BF)]
    if back:
        out_shape.append(jax.ShapeDtypeStruct(weight.shape, F32))
        out_specs.append(held)
        scratch += [pltpu.VMEM((PACK * pitch, width), BF), copies]
    scratch += [pltpu.VMEM((2, PACK, tall, width), BF), pltpu.SemaphoreType.DMA((2, PACK))]
    body = iso_back_body if back else iso_forward_body
    flops = 2 * many * tall * weight.size * (2 if back else 1) // 3
    return pl.pallas_call(
        functools.partial(body, tall, pitch, blocks, steps),
        out_shape=out_shape,
        grid_spec=pltpu.PrefetchScalarGridSpec(
            num_scalar_prefetch=3,
            grid=(steps,),
            in_specs=[s for _ in windows for s in iso_specs(tall, width, steps)] + [held],
            out_specs=out_specs,
            scratch_shapes=scratch,
        ),
        compiler_params=pltpu.CompilerParams(vmem_limit_bytes=56 * MIB),
        cost_estimate=pl.CostEstimate(flops=flops, bytes_accessed=4 * MIB, transcendentals=0),
    )(order, count, shift, *[v for v in windows for _ in range(PACK)], weight)


def feed_body(per_window, tile, live, half, own, other, d_out, merge_own, merge_other, ff_in, ff_in_bias, ff_out, biases, gains,
              layer_out, grad_own, grad_other, normed_out, hidden_out, inner_out, outer_out, merged_out, bias_grad, sums, slope):
    step = pl.program_id(0)
    alive = jnp.where(2 * (step // per_window) + half[0] < live[0], 1.0, 0.0)

    @pl.when(step == 0)
    def _():
        bias_grad[...] = jnp.zeros_like(bias_grad)
        sums[...] = jnp.zeros_like(sums)

    merged = dot(own[...], merge_own[...]) + dot(other[...], merge_other[...]) + biases[0:1, :]
    xhat_one, rho_one = normalise(merged)
    normed = (xhat_one * gains[0:1, :] + biases[1:2, :]).astype(BF)
    normed_out[...] = normed
    units = ff_in.shape[1]
    total = merged + biases[2:3, :]
    for u in range(0, units, tile):
        inner = dot(normed, ff_in[:, u : u + tile]) + ff_in_bias[:, u : u + tile]
        phi_total = 0.5 * (1.0 + lax.erf(inner * 0.7071067811865476))
        hidden = (inner * phi_total).astype(BF)
        slope[:, u : u + tile] = phi_total + inner * (jnp.exp(-0.5 * inner * inner) * 0.3989422804014327)
        hidden_out[:, u : u + tile] = hidden
        total += dot(hidden, ff_out[u : u + tile, :])
    xhat_two, rho_two = normalise(total)
    layer_out[...] = ((xhat_two * gains[1:2, :] + biases[3:4, :]) * alive).astype(BF)
    q = d_out[...].astype(F32) * alive
    grad_sum = norm_back(q * gains[1:2, :], xhat_two, rho_two)
    grad_outer = grad_sum.astype(BF)
    outer_out[...] = grad_outer
    back = jnp.zeros_like(merged)
    for u in range(0, units, tile):
        grad_inner = (dot_bt(grad_outer, ff_out[u : u + tile, :]) * slope[:, u : u + tile]).astype(BF)
        inner_out[:, u : u + tile] = grad_inner
        bias_grad[:, u : u + tile] += column_sum(grad_inner.astype(F32))
        back += dot_bt(grad_inner, ff_in[:, u : u + tile])
    grad_merged = (grad_sum + norm_back(back * gains[0:1, :], xhat_one, rho_one)).astype(BF)
    merged_out[...] = grad_merged
    grad_own[...] = dot_bt(grad_merged, merge_own[...]).astype(BF)
    grad_other[...] = dot_bt(grad_merged, merge_other[...]).astype(BF)
    sums[0:1, :] += column_sum(grad_merged.astype(F32))
    sums[1:2, :] += column_sum(back)
    sums[2:3, :] += column_sum(grad_outer.astype(F32))
    sums[3:4, :] += column_sum(q)
    sums[4:5, :] += column_sum(back * xhat_one)
    sums[5:6, :] += column_sum(q * xhat_two)


def feed_call(live, half, own, other, d_out, merge_own, merge_other, ff_in, ff_in_bias, ff_out, biases, gains, per_window):
    rows, width = own.shape
    units = ff_in.shape[1]
    block = rows // (MICRO * per_window)
    steps = rows // block

    def rowed(columns):
        return pl.BlockSpec((block, columns), lambda step, *_: (step, 0))

    def held(shape):
        return pl.BlockSpec(shape, lambda step, *_: (0, 0))

    def shaped(columns):
        return jax.ShapeDtypeStruct((rows, columns), BF)

    weights = (merge_own, merge_other, ff_in, ff_in_bias, ff_out, biases, gains)
    return pl.pallas_call(
        functools.partial(feed_body, per_window, 512),
        out_shape=[shaped(width), shaped(width), shaped(width), shaped(width), shaped(units), shaped(units), shaped(width),
                   shaped(width), jax.ShapeDtypeStruct((1, units), F32), jax.ShapeDtypeStruct((8, width), F32)],
        grid_spec=pltpu.PrefetchScalarGridSpec(
            num_scalar_prefetch=2,
            grid=(steps,),
            in_specs=[rowed(width)] * 3 + [held(v.shape) for v in weights],
            out_specs=[rowed(width)] * 4 + [rowed(units)] * 2 + [rowed(width)] * 2 + [held((1, units)), held((8, width))],
            scratch_shapes=[pltpu.VMEM((block, units), F32)],
        ),
        compiler_params=pltpu.CompilerParams(vmem_limit_bytes=56 * MIB),
        cost_estimate=pl.CostEstimate(flops=rows * width * units * 2 * 5, bytes_accessed=40 * MIB, transcendentals=rows * units),
    )(live, half, own, other, d_out, *weights)


def branch_index_pair(branch, first, second, *operands):
    return lax.cond(branch == 0, first, second, *operands)


def solution(mesh):
    def per_device(inputs, window_count, branch_blocks, branch_gains, branch_biases, merge_weight, ff_in, ff_in_bias, ff_out,
                   shared_biases, shared_gains, d_out):
        members = mesh.shape["dp"]
        branch, me = lax.axis_index("branch"), lax.axis_index("dp")
        slots, length, width = inputs.shape
        group_rows = branch_blocks.shape[2] * members
        share = branch_blocks.shape[2]
        taps_of = [length // k for k in SCALES]
        tall = up_to(max(taps_of), 8)
        pitches = [up_to(n, 16) for n in taps_of]
        reach = max(SCALES)
        most = slots * max(pitches)
        live = window_count.astype(jnp.int32)
        half = branch.astype(jnp.int32)[None]
        gain, bias = branch_gains, branch_biases[0]

        npd = 8 if share % 64 == 0 else 1
        chunk = share // npd
        down_ranges = tuple((0, -(-k * width // chunk)) for k in SCALES)
        up_starts = [(k + n) * width - group_rows for k, n in zip(SCALES, taps_of)]
        up_ranges = tuple((s // chunk, -(-(s + k * width) // chunk)) for s, k in zip(up_starts, SCALES))
        up_offs = [s - r[0] * chunk for s, r in zip(up_starts, up_ranges)]
        swaps = (-1, 1) if members == 16 else (-1, -1)
        own_blocks = branch_blocks[0]

        down_weight = gather_rows(mesh, own_blocks[0], 0, chunk, npd, down_ranges, 1, swaps)
        up_weight = gather_rows(mesh, own_blocks[1], 0, chunk, npd, up_ranges, 2)

        blocks = (share + width - 1) // width + 1
        k_of = jnp.where(branch == 0, SCALES[0], SCALES[1])
        n_of = jnp.where(branch == 0, taps_of[0], taps_of[1])
        rows_at = jnp.arange(share)
        padded, shifts, insides, lead = [], [], [], []
        for g in range(GROUPS):
            first = g * group_rows + me * share - k_of * width
            inside = jnp.logical_and(first + rows_at >= 0, first + rows_at < n_of * width)
            start = first // width
            shifts.append(jnp.clip(n_of - 1 - start - jnp.arange(blocks), 0, tall))
            lead.append(first - start * width)
            insides.append(inside)
            kept = jnp.where(inside[:, None], own_blocks[g], 0)
            padded.append(lax.dynamic_update_slice(jnp.zeros((blocks * width, width), BF), kept, (lead[g], 0)))
        iso_weight = jnp.concatenate(padded, axis=0)
        shift = jnp.concatenate(shifts).astype(jnp.int32)

        counts = lax.all_gather(live, "dp", axis=0, tiled=True)
        alive = (jnp.arange(slots)[None, :] < counts[:, None]).reshape(-1)
        places = jnp.arange(members * slots)
        rank = jnp.sum(jnp.logical_and(alive[None, :], places[None, :] < places[:, None]).astype(jnp.int32), axis=1)
        order = jnp.sum(
            jnp.where(jnp.logical_and(alive[:, None], rank[:, None] == places[None, :]), places[:, None], 0), axis=0
        ).astype(jnp.int32)
        count = jnp.sum(counts)[None].astype(jnp.int32)

        def windows_shape(kind):
            return jax.ShapeDtypeStruct((slots, tall, width), kind)

        full = jax.ShapeDtypeStruct((slots, length, width), BF)
        taps_shape = jax.ShapeDtypeStruct((most, reach * width), BF)
        part_shape = jax.ShapeDtypeStruct((max(r[1] - r[0] for r in down_ranges) * chunk, width), BF)
        up_part_shape = jax.ShapeDtypeStruct((max(r[1] - r[0] for r in up_ranges) * chunk, width), BF)
        sm = pl.BlockSpec(memory_space=pltpu.SMEM)

        def call(body, index, off, outs, scratch, scalars, *operands):
            k, n, pitch = SCALES[index], taps_of[index], pitches[index]
            return pl.pallas_call(
                functools.partial(body, k, n, pitch, off),
                out_shape=outs,
                in_specs=[sm] * scalars + [VMEM] * (len(operands) - scalars),
                out_specs=jax.tree.map(lambda _: VMEM, outs),
                scratch_shapes=scratch,
                compiler_params=pltpu.CompilerParams(vmem_limit_bytes=60 * MIB),
            )(*operands)

        def rows_scratch(index):
            return pltpu.VMEM((slots * pitches[index], width), BF)

        def spread_scratch(index, count_of=slots):
            return pltpu.VMEM((count_of, width // LANES, pitches[index] * SCALES[index], LANES), F32)

        def down_of(index):
            def run(x, weight, bias):
                return call(down_body, index, 0, (windows_shape(F32), windows_shape(BF), taps_shape),
                            [pltpu.VMEM((width // LANES, pitches[index] * SCALES[index], LANES), F32)], 0, x, weight, bias)
            return run

        pre, act, taps = branch_index_pair(branch, down_of(0), down_of(1), inputs, down_weight, bias)

        passes = 1 if members <= 32 else slots
        per = slots // passes
        pieces = 2 if per % 2 == 0 else 1

        def spread_windows(values, collective_id):
            flat = values.reshape(slots * tall, width)
            return gather_rows(mesh, flat, 0, slots * tall // 2, 2, ((0, 2 * members),) * 2, collective_id).reshape(
                members * slots, tall, width
            )

        def sum_windows(values, collective_id):
            parts = values.reshape(members, passes, per, tall, width)
            results = [
                reduce_rows(mesh, parts[:, p].reshape(-1, width), per * tall // pieces, pieces,
                            ((0, pieces * members),) * 2, collective_id + p, F32)
                for p in range(passes)
            ]
            return jnp.concatenate([r.reshape(per, tall, width) for r in results], axis=0)

        acts = spread_windows(act, 3)
        [terms] = iso_call(False, order, count, shift, iso_weight, acts)
        pre_iso = sum_windows(terms, 16)

        def up_of(index):
            def run(*operands):
                return call(up_body, index, up_offs[index], full, [rows_scratch(index), spread_scratch(index)], 1, *operands)
            return run

        branch_out = branch_index_pair(branch, up_of(0), up_of(1), live, pre_iso, up_weight, inputs, gain, bias)

        def swap(values):
            return lax.ppermute(values, "branch", [(0, 1), (1, 0)])

        def part_at(values, which):
            return lax.dynamic_index_in_dim(values.reshape(MICRO, 2, length, width), which, 1, keepdims=False)

        own = part_at(branch_out, branch).reshape(-1, width)
        other = swap(part_at(branch_out, 1 - branch)).reshape(-1, width)
        merge_own = lax.dynamic_slice_in_dim(merge_weight, branch * width, width, 0)
        merge_other = lax.dynamic_slice_in_dim(merge_weight, (1 - branch) * width, width, 0)
        (layer_out, grad_own, grad_other, normed, hidden, grad_inner, grad_outer, grad_merged, bias_grad, sums) = feed_call(
            live, half, own, other, d_out.reshape(-1, width), merge_own, merge_other, ff_in, ff_in_bias[None], ff_out,
            shared_biases, shared_gains, 3,
        )
        arrived = swap(grad_other.reshape(MICRO, length, width))
        kept = grad_own.reshape(MICRO, length, width)
        grad_branch = jnp.where(
            branch == 0, jnp.stack([kept, arrived], axis=1), jnp.stack([arrived, kept], axis=1)
        ).reshape(slots, length, width)
        ff_in_grad = dot_at(normed, grad_inner)
        ff_out_grad = dot_at(hidden, grad_outer)
        merge_own_grad, merge_other_grad = dot_at(own, grad_merged), dot_at(other, grad_merged)
        merge_grad = jnp.where(
            branch == 0, jnp.concatenate([merge_own_grad, merge_other_grad]), jnp.concatenate([merge_other_grad, merge_own_grad])
        )
        wide = lax.psum((merge_grad.astype(BF), ff_in_grad.astype(BF), ff_out_grad.astype(BF)), ("branch", "dp"))

        def up_back_of(index):
            def run(*operands):
                return call(up_back_body, index, up_offs[index],
                            (windows_shape(BF), jax.ShapeDtypeStruct((8, width), F32), taps_shape, up_part_shape),
                            [rows_scratch(index), spread_scratch(index)], 1, *operands)
            return run

        grad_iso, vectors, grad_taps, up_part = branch_index_pair(
            branch, up_back_of(0), up_back_of(1), live, grad_branch, pre_iso, up_weight, inputs, gain, bias
        )
        grads = spread_windows(grad_iso, 4)
        back_terms, kernel_grad = iso_call(True, order, count, shift, iso_weight, acts, grads)
        grad_act = sum_windows(back_terms, 32)

        def down_back_of(index):
            def run(*operands):
                return call(down_back_body, index, 0, (full, jax.ShapeDtypeStruct((1, width), F32), part_shape),
                            [rows_scratch(index), spread_scratch(index)], 1, *operands)
            return run

        grad_values, down_vector, down_part = branch_index_pair(
            branch, down_back_of(0), down_back_of(1), live, grad_act, pre, grad_taps, taps, down_weight
        )
        arrived_values = swap(part_at(grad_values, 1 - branch))
        grad_inputs = (part_at(grad_values, branch).astype(F32) + arrived_values.astype(F32)).astype(BF)

        vectors = vectors.at[1].set(down_vector[0])
        both = jnp.where((jnp.arange(2) == branch)[:, None, None], vectors[None, :5], 0.0)
        small = lax.psum((both, bias_grad, sums), ("branch", "dp"))
        own_vectors = lax.dynamic_slice_in_dim(small[0], branch, 1, 0)

        up_sum = reduce_rows(mesh, up_part, chunk, npd, up_ranges, 5, F32).reshape(share, width)
        down_sum = reduce_rows(mesh, down_part, chunk, npd, down_ranges, 6, F32, swaps).reshape(share, width)
        group_grads = []
        for g, side in enumerate((down_sum, up_sum)):
            at = g * group_rows + me * share + rows_at
            low, high = (0, k_of * width) if g == 0 else ((k_of + n_of) * width, (2 * k_of + n_of) * width)
            iso_rows = lax.dynamic_slice(kernel_grad, (g * blocks * width + lead[g], 0), (share, width))
            outside = jnp.where(jnp.logical_and(at >= low, at < high)[:, None], side, 0.0)
            group_grads.append(jnp.where(insides[g][:, None], iso_rows, outside))
        grad_blocks = jnp.stack(group_grads)[None]
        return (
            layer_out.reshape(MICRO, 1, 1, length, width), grad_inputs[:, None, None], grad_blocks,
            own_vectors[:, 0], own_vectors[:, 1:], wide[0].astype(F32), wide[1].astype(F32), small[1][0],
            wide[2].astype(F32), small[2][:4], small[2][4:6],
        )

    from jax.sharding import PartitionSpec as P

    placed = (P("dp", None, None), P("dp"), P("branch", None, "dp", None), P("branch", None), P("branch", None, None), P(), P(), P(),
              P(), P(), P(), P("dp", "branch", None, None, None))
    return jax.shard_map(
        per_device, mesh=mesh, in_specs=placed,
        out_specs=(P("dp", "branch", None, None, None), P("dp", "branch", None, None, None), P("branch", None, "dp", None),
                   P("branch", None), P("branch", None, None), P(), P(), P(), P(), P(), P()),
        check_vma=False,
    )
```

time: 2390 us -> 1030 us (0.43)
  waiting for transfers between devices: 1160 us -> 93.8 us
  Pallas kernels: 0 us -> 729 us
  matrix products: 371 us -> 21.9 us
  local copies, waits for them, and re-layouts: 265 us -> 26.2 us
  other arithmetic: 227 us -> 28.1 us
  starting transfers between devices: 98.6 us -> 0.42 us
  loops' own time: 77.7 us -> 1.19 us
  blocking collectives: 163 us -> 95.1 us
    pallas_call x0 -> x15, Pallas kernels: none -> 729 us  [the longest x4 256 us: gather_rows(): pl.pallas_call(functools.partial(gather_body, depth, npd, rows, base, ran...]
    reduce_scatter x5 -> x0, waiting for transfers between devices: 710 us -> none  [the longest x2 710 us: per_device(): lax.psum_scatter(term, 'dp', scatter_dimension=0, tiled=True)]
    dot_general x49 -> x4, matrix products: 371 us -> 21.9 us  [dot_at(): lax.dot_general(a, b, (((0,), (0,)), ((), ())), preferred_element_type=F32)]
    all_gather x1 -> x0, waiting for transfers between devices: 233 us -> none  [per_device(): gathered = lax.all_gather(branch_blocks, 'dp', axis=2, tiled=True)]
    psum x1, waiting for transfers between devices: 205 us -> 0.01 us  [per_device(): lax.psum((merge_grad.astype(BF), ff_in_grad.astype(BF), ff_out_grad.astyp...]
    gather x8 -> x0, local copies, waits for them, and re-layouts: 111 us -> none  [the longest x5 62.3 us: past_windows(): return padded[:, offsets, :]]
    all_to_all x3 -> x0, starting transfers between devices: 98.2 us -> none  [per_device(): lax.all_to_all(branch_out.astype(jnp.bfloat16), 'branch', split_axis=0, c...]
    all_to_all x3 -> x0, blocking collectives: 95.2 us -> none  [per_device(): lax.all_to_all(grad_joined, 'branch', split_axis=2, concat_axis=0, tiled=...]
  transfers between devices with their start and end apart: 10 -> 4, of which waited for: 5 -> 2; matrix products, arithmetic and copies ran while one was open for 24% -> 6% of each run, Pallas kernels for 0% -> 38%
where the time goes in v1:
time: 1030 us; the launch traced here: 1010 us
  Pallas kernels  729 us (71%)
  blocking collectives  95.1 us (9%)
  waiting for transfers between devices  93.8 us (9%)
  other arithmetic  28.1 us (3%)
  local copies, waits for them, and re-layouts  26.2 us (3%)
  matrix products  21.9 us (2%)
  between operations  15.4 us (1%)
    pallas_call x4, Pallas kernels, gather_rows(): pl.pallas_call(functools.partial(gather_body, depth, npd, rows, base, ran...  256 us
    pallas_call x4, Pallas kernels, reduce_rows(): pl.pallas_call(functools.partial(reduce_body, depth, npd, rows, ranges, s...  242 us
    pallas_call x4, Pallas kernels, call(): pl.pallas_call(functools.partial(body, k, n, pitch, off), out_shape=outs,...  110 us
    ppermute x3, waiting for transfers between devices, swap(): return lax.ppermute(values, 'branch', [(0, 1), (1, 0)])  93.8 us
    psum x1, blocking collectives, per_device(): small = lax.psum((both, bias_grad, sums), ('branch', 'dp'))  87.5 us
    pallas_call x2, Pallas kernels, iso_call(): pl.pallas_call(functools.partial(body, tall, pitch, blocks, steps), out_s...  72 us
    pallas_call x1, Pallas kernels, feed_call(): pl.pallas_call(functools.partial(feed_body, per_window, 512), out_shape=[...  49.2 us
    dot_general x4, matrix products, dot_at(): lax.dot_general(a, b, (((0,), (0,)), ((), ())), preferred_element_type=F32)  21.9 us
  transfers between devices with their start and end apart: 4, of which 2 were waited for; matrix products, arithmetic and copies ran while one was open for 6% of the time, Pallas kernels for 38%

profile of v1, /device:TPU:19, one launch (start us, length us, event | category | flops | bytes accessed | tf_op | source)
XLA Modules:
  0.0 1011.2 jit_solution(7208405256811578917)
XLA Ops:
  9.9 7.6 all-reduce
  19.1 3.7 slice_bitcast_fusion
  22.8 53.9 %shard_map.207 = bf16[8280,512]{1,0:T(8,128)(2,1)} custom-call(bf16[1472,512]{1,0:T(8,128)(2,1)} %get-tuple-element.292.src), custom_call_target="tpu_custom_call" | custom-call | tf_op jit(solution)/shard_map/pallas_call | solution.py:164
  76.7 88.9 %shard_map.203 = bf16[8280,512]{1,0:T(8,128)(2,1)} custom-call(bf16[1472,512]{1,0:T(8,128)(2,1)} %get-tuple-element.293.src), custom_call_target="tpu_custom_call" | custom-call | tf_op jit(solution)/shard_map/pallas_call | solution.py:164
  165.6 15.3 %conditional.4 = ((f32[6,72,512]{2,1,0:T(8,128)}, bf16[6,72,512]{2,1,0:T(8,128)(2,1)S(1)}, bf16[480,8192]{1,0:T(8,128)(2,1)})) conditional(s32[]{:T(128)} %convert_element_type.42, (bf16[6,816,512]{2,1,0:T(8,128)(2,1)}, bf16[8280,512]{1,0:T(8,128)(2,1)}, f32[4,512]{1,0:T(4,128)S(1)}) %tuple.91, (bf16[6,816,512]{2,1,0:T(8,128)(2,1)}, ...), branch_computations={%region_3.4_spmd, %region_4.5_spmd} | conditional | bytes 8 | solution.py:807
  165.6 15.3 %branch_0_fun.5 = (f32[6,72,512]{2,1,0:T(8,128)}, bf16[6,72,512]{2,1,0:T(8,128)(2,1)S(1)}, bf16[480,8192]{1,0:T(8,128)(2,1)}) custom-call(bf16[6,816,512]{2,1,0:T(8,128)(2,1)} %get-tuple-element.140.x, bf16[8280,512]{1,0:T(8,128)(2,1)} %get-tuple-element.141.weight, f32[4,512]{1,0:T(4,128)S(1)} %get-tuple-element.142.bias), custom_call_target="tpu_custom_call" | custom-call | tf_op jit(solution)/shard_map/cond/branch_0_fun/pallas_call | solution.py:876
  180.9 48.3 %shard_map.204 = bf16[6912,512]{1,0:T(8,128)(2,1)} custom-call(bf16[432,512]{1,0:T(8,128)(2,1)S(1)} %bitcast.117), custom_call_target="tpu_custom_call" | custom-call | tf_op jit(solution)/shard_map/pallas_call | solution.py:164
  233.3 23.7 %shard_map.205 = bf16[96,72,512]{2,1,0:T(8,128)(2,1)} custom-call(s32[96]{0:T(128)} %select_reduce_fusion.order, s32[1]{0:T(128)} %bitcast.8.count, s32[8]{0:T(128)} %pad_add_fusion.shift, bf16[96,72,512]{2,1,0:T(8,128)(2,1)} %bitcast.69, bf16[96,72,512]{2,1,0:T(8,128)(2,1)} %bitcast.70, bf16[96,72,512]{2,1,0:T(8,128)(2,1)} %bitcast.71, ...), custom_call_target="tpu_custom_call" | custom-call | flops 9663676416 | bytes 4194304 | tf_op jit(solution)/shard_map/pallas_call | solution.py:712
  257.0 47.3 %shard_map.206 = f32[2,216,512]{2,1,0:T(8,128)S(1)} custom-call(bf16[6912,512]{1,0:T(8,128)(2,1)} %bitcast.99), custom_call_target="tpu_custom_call" | custom-call | tf_op jit(solution)/shard_map/pallas_call | solution.py:342
  304.3 23.1 %conditional.5 = (bf16[3,2,816,512]{3,2,1,0:T(8,128)(2,1)}) conditional(s32[]{:T(128)} %convert_element_type.42, (s32[1]{0:T(128)}, f32[6,72,512]{2,1,0:T(8,128)S(1)}, bf16[8280,512]{1,0:T(8,128)(2,1)}, bf16[6,816,512]{2,1,0:T(8,128)(2,1)}, f32[1,512]{1,0:T(1,128)S(1)}, /*index=5*/f32[4,512]{1,0:T(4,128)S(1)}) %tuple.97, (s32[1]{0:T(128)}, ...), branch_computations={%region_5.6_spmd, %region_6.7_spmd} | conditional | bytes 8 | solution.py:807
  304.3 22.6 %branch_0_fun.6 = bf16[6,816,512]{2,1,0:T(8,128)(2,1)} custom-call(s32[1]{0:T(128)} %get-tuple-element.146.live, f32[6,72,512]{2,1,0:T(8,128)S(1)} %get-tuple-element.147.pre_iso, bf16[8280,512]{1,0:T(8,128)(2,1)} %get-tuple-element.148.weight, bf16[6,816,512]{2,1,0:T(8,128)(2,1)} %get-tuple-element.149.x, f32[1,512]{1,0:T(1,128)S(1)} %get-tuple-element.150.gain, ...), custom_call_target="tpu_custom_call" | custom-call | tf_op jit(solution)/shard_map/cond/branch_0_fun/pallas_call | solution.py:876
  327.4 4.3 dynamic-slice_bitcast_fusion.1
  333.9 52.7 %collective-permute-done = bf16[3,816,512]{2,1,0:T(8,128)(2,1)} collective-permute-done((bf16[3,816,512]{2,1,0:T(8,128)(2,1)S(1)}, bf16[3,816,512]{2,1,0:T(8,128)(2,1)}, u32[]{:S(2)}, u32[]{:S(2)}) %collective-permute-start) | collective-permute-done | bytes 2506784 | tf_op jit(solution)/shard_map/ppermute | solution.py:930
  386.6 49.2 %shard_map.208 = (bf16[2448,512]{1,0:T(8,128)(2,1)}, bf16[2448,512]{1,0:T(8,128)(2,1)}, bf16[2448,512]{1,0:T(8,128)(2,1)}, bf16[2448,512]{1,0:T(8,128)(2,1)}, bf...) custom-call(s32[1]{0:T(128)S(6)} %copy.65.live, ...), custom_call_target="tpu_custom_call" | custom-call | flops 25669140480 | bytes 41943040 | tf_op jit(solution)/shard_map/pallas_call | solution.py:790
  436.1 10.1 %convolution_convert_fusion.1 = bf16[512,2048]{1,0:T(8,128)(2,1)} fusion(bf16[2448,512]{1,0:T(8,128)(2,1)} %get-tuple-element.233, bf16[2448,2048]{1,0:T(8,128)(2,1)} %get-tuple-element.234), kind=kOutput, calls=%fused_computation.10 | convolution fusion | flops 5134876672 | bytes 14630912 | tf_op jit(solution)/shard_map/dot_general | solution.py:387
  446.3 3.4 fusion.21
  452.8 6.8 convolution_convert_fusion
  459.6 41.1 %collective-permute-done.1 = bf16[3,816,512]{2,1,0:T(8,128)(2,1)} collective-permute-done((bf16[3,816,512]{2,1,0:T(8,128)(2,1)}, bf16[3,816,512]{2,1,0:T(8,128)(2,1)}, u32[]{:S(2)}, u32[]{:S(2)}) %collective-permute-start.1) | collective-permute-done | bytes 2506784 | tf_op jit(solution)/shard_map/ppermute | solution.py:930
  500.7 3.8 maximum_select_fusion
  507.3 44.7 %conditional.6 = ((bf16[6,72,512]{2,1,0:T(8,128)(2,1)S(1)}, f32[8,512]{1,0:T(8,128)S(1)}, bf16[480,8192]{1,0:T(8,128)(2,1)}, bf16[8280,512]{1,0:T(8,128)(2,1)})) conditional(s32[]{:T(128)} %convert_element_type.42, (s32[1]{0:T(128)}, bf16[6,816,512]{2,1,0:T(8,128)(2,1)}, f32[6,72,512]{2,1,0:T(8,128)S(1)}, bf16[8280,512]{1,0:T(8,128)(2,1)}, ...), branch_computations={%region_7.8_spmd, %region_8.9_spmd} | conditional | bytes 8 | solution.py:807
  507.4 44.6 %branch_0_fun.7 = (bf16[6,72,512]{2,1,0:T(8,128)(2,1)S(1)}, f32[8,512]{1,0:T(8,128)S(1)}, bf16[480,8192]{1,0:T(8,128)(2,1)}, bf16[8280,512]{1,0:T(8,128)(2,1)}) custom-call(s32[1]{0:T(128)} %get-tuple-element.158.live, bf16[6,816,512]{2,1,0:T(8,128)(2,1)} %get-tuple-element.159.grad, f32[6,72,512]{2,1,0:T(8,128)S(1)} %get-tuple-element.160.pre_iso, ...), custom_call_target="tpu_custom_call" | custom-call | tf_op jit(solution)/shard_map/cond/branch_0_fun/pallas_call | solution.py:876
  552.0 65.1 %shard_map.209 = bf16[6912,512]{1,0:T(8,128)(2,1)} custom-call(bf16[432,512]{1,0:T(8,128)(2,1)S(1)} %bitcast.116), custom_call_target="tpu_custom_call" | custom-call | tf_op jit(solution)/shard_map/pallas_call | solution.py:164
  617.1 48.3 %shard_map.210 = (bf16[96,72,512]{2,1,0:T(8,128)(2,1)}, f32[4096,512]{1,0:T(8,128)}) custom-call(s32[96]{0:T(128)} %select_reduce_fusion.order, s32[1]{0:T(128)} %bitcast.8.count, s32[8]{0:T(128)} %pad_add_fusion.shift, bf16[96,72,512]{2,1,0:T(8,128)(2,1)} %bitcast.77, bf16[96,72,512]{2,1,0:T(8,128)(2,1)} %bitcast.78, bf16[96,72,512]{2,1,0:T(8,128)(2,1)} %bitcast.79, ...), custom_call_target="tpu_custom_call" | custom-call | flops 19327352832 | bytes 4194304 | tf_op jit(solution)/shard_map/pallas_call | solution.py:712
  665.4 45.0 %shard_map.211 = f32[2,216,512]{2,1,0:T(8,128)S(1)} custom-call(bf16[6912,512]{1,0:T(8,128)(2,1)} %bitcast.110), custom_call_target="tpu_custom_call" | custom-call | tf_op jit(solution)/shard_map/pallas_call | solution.py:342
  710.4 32.7 %conditional.7 = (f32[1,512]{1,0:T(1,128)S(1)}, bf16[8280,512]{1,0:T(8,128)(2,1)}, bf16[3,2,816,512]{3,2,1,0:T(8,128)(2,1)}, bf16[3,2,816,512]{3,2,0,1:T(8,128)(2,1)}) conditional(s32[]{:T(128)} %convert_element_type.42, (s32[1]{0:T(128)}, f32[2,216,512]{2,1,0:T(8,128)S(1)}, f32[6,72,512]{2,1,0:T(8,128)S(1)}, bf16[480,8192]{1,0:T(8,128)(2,1)}, ...), branch_computations={%region_9.10_spmd, %region_10.11_spmd} | conditional | bytes 10027040 | solution.py:807
  710.8 27.1 %branch_0_fun.8 = (bf16[6,816,512]{2,1,0:T(8,128)(2,1)}, f32[1,512]{1,0:T(1,128)S(1)}, bf16[8280,512]{1,0:T(8,128)(2,1)}) custom-call(s32[1]{0:T(128)} %get-tuple-element.172.live, f32[6,72,512]{2,1,0:T(8,128)S(1)} %bitcast.108, f32[6,72,512]{2,1,0:T(8,128)S(1)} %get-tuple-element.174.pre, bf16[480,8192]{1,0:T(8,128)(2,1)} %get-tuple-element.175.grad_taps, ...), custom_call_target="tpu_custom_call" | custom-call | tf_op jit(solution)/shard_map/cond/branch_0_fun/pallas_call | solution.py:876
  737.9 5.1 copy.32
  743.2 3.3 dynamic-slice_bitcast_fusion
  746.7 87.5 %all-reduce.1 = (f32[2,5,512]{2,1,0:T(8,128)S(1)}, f32[2048]{0:T(1024)}, f32[8,512]{1,0:T(8,128)S(1)}) all-reduce(f32[2,5,512]{2,1,0:T(8,128)S(1)} %broadcast_select_fusion, f32[2048]{0:T(1024)S(1)} %bitcast.125, f32[8,512]{1,0:T(8,128)S(1)} %copy-done.12), channel_id=1, replica_groups=mesh['branch'=2,'dp'=16] {'branch','dp'}, use_global_device_ids=true, to_apply=%region_11.12 | all-reduce | flops 11264 | bytes 90112 | tf_op jit(solution)/shard_map/psum | solution.py:984
  835.4 64.5 %shard_map.213 = f32[8,184,512]{2,1,0:T(8,128)S(1)} custom-call(bf16[8280,512]{1,0:T(8,128)(2,1)} %get-tuple-element.229.src), custom_call_target="tpu_custom_call" | custom-call | tf_op jit(solution)/shard_map/pallas_call | solution.py:342
  899.9 85.4 %shard_map.212 = f32[8,184,512]{2,1,0:T(8,128)S(1)} custom-call(bf16[8280,512]{1,0:T(8,128)(2,1)} %get-tuple-element.228.src), custom_call_target="tpu_custom_call" | custom-call | tf_op jit(solution)/shard_map/pallas_call | solution.py:342
  999.5 4.6 fusion.3
  (84 shorter events, 31.6 us)
Async XLA Ops:
  7.2 984.2 %all-reduce.5.cloned.1.call-start = ((), (), s32[]{:S(2)}) async-start(), calls=%async_computation | async-start | bytes 10485760 | tf_op jit(solution)/shard_map/psum | solution.py:954
  19.1 210.9 %copy-start.10 = (pred[1472]{0:T(1024)(128)(4,1)}, pred[1472]{0:T(1024)(128)(4,1)S(1)}, u32[]{:S(2)}) copy-start(pred[1472]{0:T(1024)(128)(4,1)S(1)} %get-tuple-element.299) | copy-start | bytes 4420
  19.1 211.4 %copy-start.8 = (pred[1472]{0:T(1024)(128)(4,1)}, pred[1472]{0:T(1024)(128)(4,1)S(1)}, u32[]{:S(2)}) copy-start(pred[1472]{0:T(1024)(128)(4,1)S(1)} %get-tuple-element.298) | copy-start | bytes 4420
  76.7 88.9 %copy-start.6 = (f32[1,4,512]{2,1,0:T(4,128)S(1)}, f32[1,4,512]{2,1,0:T(4,128)}, u32[]{:S(2)}) copy-start(f32[1,4,512]{2,1,0:T(4,128)} %param.26) | copy-start | bytes 24580
  180.9 49.1 %copy-start = (bf16[1,2,1472,512]{3,2,1,0:T(8,128)(2,1)S(1)}, bf16[1,2,1472,512]{3,2,1,0:T(8,128)(2,1)}, u32[]{:S(2)}) copy-start(bf16[1,2,1472,512]{3,2,1,0:T(8,128)(2,1)} %param.24) | copy-start | bytes 9043972
  257.0 47.3 %copy-start.7 = (f32[1,512]{1,0:T(1,128)S(1)}, f32[1,512]{1,0:T(1,128)}, u32[]{:S(2)}) copy-start(f32[1,512]{1,0:T(1,128)} %param.25) | copy-start | bytes 6148
  331.6 55.0 %collective-permute-start = (bf16[3,816,512]{2,1,0:T(8,128)(2,1)S(1)}, bf16[3,816,512]{2,1,0:T(8,128)(2,1)}, u32[]{:S(2)}, u32[]{:S(2)}) collective-permute-start(bf16[3,816,512]{2,1,0:T(8,128)(2,1)S(1)} %get-tuple-element.290), channel_id=1, source_target_pairs={{0,16},{16,0},{1,17},{17,1},{2,18},{18,2},{3,19},{19,3},{4,20},{20... | collective-permute-start | bytes 7520264 | tf_op jit(solution)/shard_map/ppermute | solution.py:930
  435.7 65.0 %collective-permute-start.1 = (bf16[3,816,512]{2,1,0:T(8,128)(2,1)}, bf16[3,816,512]{2,1,0:T(8,128)(2,1)}, u32[]{:S(2)}, u32[]{:S(2)}) collective-permute-start(bf16[3,816,512]{2,1,0:T(8,128)(2,1)} %bitcast.127), channel_id=1, source_target_pairs={{0,16},{16,0},{1,17},{17,1},{2,18},{18,2},{3,19},{19,3},{4,20},{20... | collective-permute-start | bytes 7520264 | tf_op jit(solution)/shard_map/ppermute | solution.py:930
  436.1 10.1 %copy-start.14 = (bf16[2448,512]{1,0:T(8,128)(2,1)S(1)}, bf16[2448,512]{1,0:T(8,128)(2,1)}, u32[]{:S(2)}) copy-start(bf16[2448,512]{1,0:T(8,128)(2,1)} %get-tuple-element.232) | copy-start | bytes 7520260
  446.2 3.4 copy-start.3
  446.2 6.5 slice-start.2
  446.2 6.5 slice-start.3
  449.7 3.1 slice-start.4
  449.7 3.1 copy-start.15
  459.6 41.1 %copy-start.2 = (bf16[2448,512]{1,0:T(8,128)(2,1)S(1)}, bf16[2448,512]{1,0:T(8,128)(2,1)}, u32[]{:S(2)}) copy-start(bf16[2448,512]{1,0:T(8,128)(2,1)} %get-tuple-element.219) | copy-start | bytes 7520260
  665.4 45.1 %copy-start.1 = (f32[6,72,512]{2,1,0:T(8,128)S(1)}, f32[6,72,512]{2,1,0:T(8,128)}, u32[]{:S(2)}) copy-start(f32[6,72,512]{2,1,0:T(8,128)} %get-tuple-element.223) | copy-start | bytes 2654212
  743.1 3.5 copy-start.12
  743.2 3.5 copy-start.13
  746.5 253.0 %collective-permute-start.2 = (bf16[3,816,512]{2,1,0:T(8,128)(2,1)}, bf16[3,816,512]{2,1,0:T(8,128)(2,1)}, u32[]{:S(2)}, u32[]{:S(2)}) collective-permute-start(bf16[3,816,512]{2,1,0:T(8,128)(2,1)} %dynamic-slice_bitcast_fusion), channel_id=1, source_target_pairs={{0,16},{16,0},{1,17},{17,1},{2,18},{18,2},{3,19},{19,3},{4,20},{20... | collective-permute-start | bytes 7520264 | tf_op jit(solution)/shard_map/ppermute | solution.py:930
  835.4 151.1 %slice-start = ((s8[8388608]{0:T(1024)(128)(4,1)}), s8[4194304]{0:T(1024)(128)(4,1)S(1)}, s32[]{:S(2)}) async-start(s8[8388608]{0:T(1024)(128)(4,1)} %bitcast.111), calls=%async_computation.1 | async-start | bytes 8388608
  899.9 86.6 %slice-start.1 = ((s8[8388608]{0:T(1024)(128)(4,1)}), s8[4194304]{0:T(1024)(128)(4,1)S(1)}, s32[]{:S(2)}) async-start(s8[8388608]{0:T(1024)(128)(4,1)} %bitcast.111), calls=%async_computation.2 | async-start | bytes 8388608
  899.9 86.6 %copy-start.9 = (pred[1472]{0:T(1024)(128)(4,1)S(1)}, pred[1472]{0:T(1024)(128)(4,1)}, u32[]{:S(2)}) copy-start(pred[1472]{0:T(1024)(128)(4,1)} %copy-done.8) | copy-start | bytes 4420
  899.9 86.6 %copy-start.11 = (pred[1472]{0:T(1024)(128)(4,1)S(1)}, pred[1472]{0:T(1024)(128)(4,1)}, u32[]{:S(2)}) copy-start(pred[1472]{0:T(1024)(128)(4,1)} %copy-done.10) | copy-start | bytes 4420
  991.4 3.0 copy-start.5
  994.4 2.5 copy-start.4
Sparse Core Ops, SparseCore 0:
  459.7 161.6 all-reduce.4

commit v2 on v1

--- a/solution.py
+++ b/solution.py
@@ -431,7 +431,7 @@
         ref[(*lead, p, rows, slice(None))] = values[:, p * LANES : (p + 1) * LANES]
 
 
-def down_body(k, n, pitch, off, x, weight, bias, pre, act, taps, spread):
+def down_body(k, n, pitch, off, live, x, weight, bias, pre, act, taps, spread):
     slots, length, width = x.shape
     many = slots * pitch
     spread[:, length:, :] = jnp.zeros((spread.shape[0], spread.shape[1] - length, LANES), F32)
@@ -451,7 +451,8 @@
         rows = fit(total[w * pitch : (w + 1) * pitch], tall)
         pre[w] = rows
         step = lax.broadcasted_iota(jnp.int32, rows.shape, 0)
-        act[w] = jnp.where(step < n, jnp.tanh(rows), 0.0).astype(BF)
+        flag = jnp.where(step == tall - 1, jnp.where(w < live[0], 1.0, 0.0), 0.0)
+        act[w] = jnp.where(step < n, jnp.tanh(rows), flag).astype(BF)
 
 
 def fit(values, tall):
@@ -480,23 +481,24 @@
     return jnp.where(step < n, rows, 0.0)
 
 
-def up_body(k, n, pitch, off, live, pre_iso, weight, x, gain, bias, out, iso_rows, spread):
+def up_body(k, n, pitch, off, live, half, pre_iso, weight, x, gain, bias, own, send, iso_rows, spread):
     slots, length, width = x.shape
     for w in range(slots):
         iso = iso_of(n, pitch, pre_iso[w], bias)
         iso_rows[w * pitch : (w + 1) * pitch, :] = jnp.where(w < live[0], iso, 0.0).astype(BF)
     expand(k, n, pitch, off, iso_rows, weight, spread)
 
-    def window(w, carry):
-        values = panels(spread, (w,), slice(0, length)) + bias[2:3, :] + x[w].astype(F32)
-        xhat, _ = normalise(values)
-        out[w] = (xhat * gain[0:1, :] + bias[3:4, :]).astype(BF)
+    def window(m, carry):
+        for out, w in ((send, 2 * m + 1 - half[0]), (own, 2 * m + half[0])):
+            values = panels(spread, (w,), slice(0, length)) + bias[2:3, :] + x[w].astype(F32)
+            xhat, _ = normalise(values)
+            out[m] = (xhat * gain[0:1, :] + bias[3:4, :]).astype(BF)
         return carry
 
-    lax.fori_loop(0, slots, window, 0)
-
-
-def up_back_body(k, n, pitch, off, live, grad, pre_iso, weight, x, gain, bias, grad_iso, vectors, grad_taps, part, iso_rows, spread):
+    lax.fori_loop(0, slots // 2, window, 0)
+
+
+def up_back_body(k, n, pitch, off, live, half, grad_own, grad_arrived, pre_iso, weight, x, gain, bias, grad_iso, vectors, grad_taps, part, iso_rows, spread):
     slots, length, width = x.shape
     for w in range(slots):
         iso = iso_of(n, pitch, pre_iso[w], bias)
@@ -504,18 +506,19 @@
     expand(k, n, pitch, off, iso_rows, weight, spread)
     vectors[...] = jnp.zeros_like(vectors)
 
-    def window(w, carry):
-        values = panels(spread, (w,), slice(0, length)) + bias[2:3, :] + x[w].astype(F32)
-        xhat, rho = normalise(values)
-        q = grad[w].astype(F32)
-        residual = norm_back(q * gain[0:1, :], xhat, rho)
-        set_panels(spread, (w,), slice(0, length), residual)
-        vectors[0:1, :] += column_sum(q * xhat)
-        vectors[3:4, :] += column_sum(residual.astype(BF).astype(F32))
-        vectors[4:5, :] += column_sum(q)
+    def window(m, carry):
+        for grad, w in ((grad_own, 2 * m + half[0]), (grad_arrived, 2 * m + 1 - half[0])):
+            values = panels(spread, (w,), slice(0, length)) + bias[2:3, :] + x[w].astype(F32)
+            xhat, rho = normalise(values)
+            q = grad[m].astype(F32)
+            residual = norm_back(q * gain[0:1, :], xhat, rho)
+            set_panels(spread, (w,), slice(0, length), residual)
+            vectors[0:1, :] += column_sum(q * xhat)
+            vectors[3:4, :] += column_sum(residual.astype(BF).astype(F32))
+            vectors[4:5, :] += column_sum(q)
         return carry
 
-    lax.fori_loop(0, slots, window, 0)
+    lax.fori_loop(0, slots // 2, window, 0)
 
     def tap(w, carry):
         for r in range(k):
@@ -540,8 +543,8 @@
         grad_iso[w] = fit(back.astype(F32), tall).astype(BF)
 
 
-def down_back_body(k, n, pitch, off, live, grad_act, pre, grad_taps, taps, weight, out, vector, part, rows, spread):
-    slots, length, width = out.shape
+def down_back_body(k, n, pitch, off, live, half, grad_act, pre, grad_taps, taps, weight, keep, send, vector, part, rows, spread):
+    slots, (length, width) = pre.shape[0], keep.shape[1:]
     vector[...] = jnp.zeros_like(vector)
     for w in range(slots):
         act = jnp.tanh(fit(pre[w], pitch))
@@ -559,11 +562,12 @@
             taps[: slots * pitch, r * width : (r + 1) * width], rows[...]
         ).astype(BF)
 
-    def window(w, carry):
-        out[w] = panels(spread, (w,), slice(0, length)).astype(BF)
+    def window(m, carry):
+        send[m] = panels(spread, (2 * m + 1 - half[0],), slice(0, length)).astype(BF)
+        keep[m] = panels(spread, (2 * m + half[0],), slice(0, length)).astype(BF)
         return carry
 
-    lax.fori_loop(0, slots, window, 0)
+    lax.fori_loop(0, slots // 2, window, 0)
 
 
 SUBLANES = 8
@@ -724,20 +728,52 @@
     )(order, count, shift, *[v for v in windows for _ in range(PACK)], weight)
 
 
-def feed_body(per_window, tile, live, half, own, other, d_out, merge_own, merge_other, ff_in, ff_in_bias, ff_out, biases, gains,
-              layer_out, grad_own, grad_other, normed_out, hidden_out, inner_out, outer_out, merged_out, bias_grad, sums, slope):
-    step = pl.program_id(0)
-    alive = jnp.where(2 * (step // per_window) + half[0] < live[0], 1.0, 0.0)
+def feed_body(per_window, tile, live, own, bo_send, d_out, merge_weight, ff_in, ff_in_bias, ff_out, biases, gains,
+              layer_out, grad_own, arrived, merge_grad, in_grad, out_grad, bias_grad, sums,
+              slope, hidden_kept, other_slots, grad_slots, merge_sum, in_sum, out_sum, bo_sent, bo_come, back_sent, back_come):
+    step, steps = pl.program_id(0), pl.num_programs(0)
+    branch, me = lax.axis_index("branch"), lax.axis_index("dp")
+    partner = (1 - branch, me)
+    block, width = own.shape
+
+    def forth(at):
+        return pltpu.make_async_remote_copy(
+            bo_send.at[pl.ds(pl.multiple_of(at * block, 8), block), :], other_slots.at[at], bo_sent.at[at], bo_come.at[at],
+            device_id=partner, device_id_type=MESH,
+        )
+
+    def back_copy(at):
+        return pltpu.make_async_remote_copy(
+            grad_slots.at[at], arrived.at[pl.ds(pl.multiple_of(at * block, 8), block), :], back_sent.at[at], back_come.at[at],
+            device_id=partner, device_id_type=MESH,
+        )
 
     @pl.when(step == 0)
     def _():
+        barrier = pltpu.get_barrier_semaphore()
+        pl.semaphore_signal(barrier, 1, device_id=partner, device_id_type=MESH)
+        pl.semaphore_wait(barrier, 1)
+        forth(0).start()
+        forth(1).start()
         bias_grad[...] = jnp.zeros_like(bias_grad)
         sums[...] = jnp.zeros_like(sums)
-
-    merged = dot(own[...], merge_own[...]) + dot(other[...], merge_other[...]) + biases[0:1, :]
+        merge_sum[...] = jnp.zeros_like(merge_sum)
+        in_sum[...] = jnp.zeros_like(in_sum)
+        out_sum[...] = jnp.zeros_like(out_sum)
+
+    forth(step).wait_recv()
+
+    @pl.when(step + 2 < steps)
+    def _():
+        forth(step + 2).start()
+
+    alive = jnp.where(2 * (step // per_window) + branch < live[0], 1.0, 0.0)
+    own_rows, other_rows = own[...], other_slots[step]
+    own_at = pl.ds(pl.multiple_of(branch * width, width), width)
+    other_at = pl.ds(pl.multiple_of((1 - branch) * width, width), width)
+    merged = dot(own_rows, merge_weight[own_at, :]) + dot(other_rows, merge_weight[other_at, :]) + biases[0:1, :]
     xhat_one, rho_one = normalise(merged)
     normed = (xhat_one * gains[0:1, :] + biases[1:2, :]).astype(BF)
-    normed_out[...] = normed
     units = ff_in.shape[1]
     total = merged + biases[2:3, :]
     for u in range(0, units, tile):
@@ -745,24 +781,26 @@
         phi_total = 0.5 * (1.0 + lax.erf(inner * 0.7071067811865476))
         hidden = (inner * phi_total).astype(BF)
         slope[:, u : u + tile] = phi_total + inner * (jnp.exp(-0.5 * inner * inner) * 0.3989422804014327)
-        hidden_out[:, u : u + tile] = hidden
+        hidden_kept[:, u : u + tile] = hidden
         total += dot(hidden, ff_out[u : u + tile, :])
     xhat_two, rho_two = normalise(total)
     layer_out[...] = ((xhat_two * gains[1:2, :] + biases[3:4, :]) * alive).astype(BF)
     q = d_out[...].astype(F32) * alive
     grad_sum = norm_back(q * gains[1:2, :], xhat_two, rho_two)
     grad_outer = grad_sum.astype(BF)
-    outer_out[...] = grad_outer
     back = jnp.zeros_like(merged)
     for u in range(0, units, tile):
         grad_inner = (dot_bt(grad_outer, ff_out[u : u + tile, :]) * slope[:, u : u + tile]).astype(BF)
-        inner_out[:, u : u + tile] = grad_inner
         bias_grad[:, u : u + tile] += column_sum(grad_inner.astype(F32))
         back += dot_bt(grad_inner, ff_in[:, u : u + tile])
+        in_sum[:, u : u + tile] += dot_at(normed, grad_inner)
+        out_sum[u : u + tile, :] += dot_at(hidden_kept[:, u : u + tile], grad_outer)
     grad_merged = (grad_sum + norm_back(back * gains[0:1, :], xhat_one, rho_one)).astype(BF)
-    merged_out[...] = grad_merged
-    grad_own[...] = dot_bt(grad_merged, merge_own[...]).astype(BF)
-    grad_other[...] = dot_bt(grad_merged, merge_other[...]).astype(BF)
+    grad_slots[step] = dot_bt(grad_merged, merge_weight[other_at, :]).astype(BF)
+    back_copy(step).start()
+    grad_own[...] = dot_bt(grad_merged, merge_weight[own_at, :]).astype(BF)
+    merge_sum[own_at, :] += dot_at(own_rows, grad_merged)
+    merge_sum[other_at, :] += dot_at(other_rows, grad_merged)
     sums[0:1, :] += column_sum(grad_merged.astype(F32))
     sums[1:2, :] += column_sum(back)
     sums[2:3, :] += column_sum(grad_outer.astype(F32))
@@ -770,37 +808,126 @@
     sums[4:5, :] += column_sum(back * xhat_one)
     sums[5:6, :] += column_sum(q * xhat_two)
 
-
-def feed_call(live, half, own, other, d_out, merge_own, merge_other, ff_in, ff_in_bias, ff_out, biases, gains, per_window):
+    @pl.when(step == steps - 1)
+    def _():
+        merge_grad[...] = merge_sum[...].astype(BF)
+        in_grad[...] = in_sum[...].astype(BF)
+        out_grad[...] = out_sum[...].astype(BF)
+
+        def finish(at, carry):
+            forth(at).wait_send()
+            back_copy(at).wait_send()
+            back_copy(at).wait_recv()
+            return carry
+
+        lax.fori_loop(0, steps, finish, 0)
+
+
+def feed_call(live, own, bo_send, d_out, merge_weight, ff_in, ff_in_bias, ff_out, biases, gains, per_window, collective_id):
     rows, width = own.shape
     units = ff_in.shape[1]
-    block = rows // (MICRO * per_window)
-    steps = rows // block
+    steps = MICRO * per_window
+    block = rows // steps
 
     def rowed(columns):
         return pl.BlockSpec((block, columns), lambda step, *_: (step, 0))
 
     def held(shape):
-        return pl.BlockSpec(shape, lambda step, *_: (0, 0))
-
-    def shaped(columns):
-        return jax.ShapeDtypeStruct((rows, columns), BF)
-
-    weights = (merge_own, merge_other, ff_in, ff_in_bias, ff_out, biases, gains)
+        return pl.BlockSpec(shape, lambda step, *_: (0, 0), pipeline_mode=pl.Buffered(1))
+
+    def shaped(*shape):
+        return jax.ShapeDtypeStruct(shape, BF)
+
+    weights = (merge_weight, ff_in, ff_in_bias, ff_out, biases, gains)
+    outs = [(rows, width), (rows, width), (rows, width), merge_weight.shape, ff_in.shape, ff_out.shape]
     return pl.pallas_call(
         functools.partial(feed_body, per_window, 512),
-        out_shape=[shaped(width), shaped(width), shaped(width), shaped(width), shaped(units), shaped(units), shaped(width),
-                   shaped(width), jax.ShapeDtypeStruct((1, units), F32), jax.ShapeDtypeStruct((8, width), F32)],
+        out_shape=[shaped(*s) for s in outs] + [jax.ShapeDtypeStruct((1, units), F32), jax.ShapeDtypeStruct((8, width), F32)],
         grid_spec=pltpu.PrefetchScalarGridSpec(
-            num_scalar_prefetch=2,
+            num_scalar_prefetch=1,
             grid=(steps,),
-            in_specs=[rowed(width)] * 3 + [held(v.shape) for v in weights],
-            out_specs=[rowed(width)] * 4 + [rowed(units)] * 2 + [rowed(width)] * 2 + [held((1, units)), held((8, width))],
-            scratch_shapes=[pltpu.VMEM((block, units), F32)],
+            in_specs=[rowed(width), ANY, rowed(width)] + [held(v.shape) for v in weights],
+            out_specs=[rowed(width), rowed(width), ANY] + [held(s) for s in outs[3:]] + [held((1, units)), held((8, width))],
+            scratch_shapes=[
+                pltpu.VMEM((block, units), F32), pltpu.VMEM((block, units), BF), pltpu.VMEM((steps, block, width), BF),
+                pltpu.VMEM((steps, block, width), BF), pltpu.VMEM(merge_weight.shape, F32), pltpu.VMEM(ff_in.shape, F32),
+                pltpu.VMEM(ff_out.shape, F32), pltpu.SemaphoreType.DMA((steps,)), pltpu.SemaphoreType.DMA((steps,)),
+                pltpu.SemaphoreType.DMA((steps,)), pltpu.SemaphoreType.DMA((steps,)),
+            ],
         ),
-        compiler_params=pltpu.CompilerParams(vmem_limit_bytes=56 * MIB),
-        cost_estimate=pl.CostEstimate(flops=rows * width * units * 2 * 5, bytes_accessed=40 * MIB, transcendentals=rows * units),
-    )(live, half, own, other, d_out, *weights)
+        compiler_params=pltpu.CompilerParams(vmem_limit_bytes=58 * MIB, collective_id=collective_id, has_side_effects=True),
+        cost_estimate=pl.CostEstimate(flops=rows * width * units * 2 * 8, bytes_accessed=40 * MIB, transcendentals=rows * units),
+    )(live, own, bo_send, d_out, *weights)
+
+
+def total_body(depth, values, out, pair, come, far, sent_sem, come_sem, far_sent, far_come):
+    b, me, z, y, c = place()
+    peers = ((b, me + 1 - 2 * c), (1 - b, me), (b, me + 2 - 4 * y))
+    barrier = pltpu.get_barrier_semaphore()
+    for peer in peers:
+        pl.semaphore_signal(barrier, 1, device_id=peer, device_id_type=MESH)
+
+    def along(what):
+        def each(other, carry):
+            @pl.when(other != z)
+            def _():
+                what(other)
+
+            return carry
+
+        lax.fori_loop(0, depth, each, 0)
+
+    def at_row(other):
+        return b, me + 4 * (other - z)
+
+    along(lambda other: pl.semaphore_signal(barrier, 1, device_id=at_row(other), device_id_type=MESH))
+    pl.semaphore_wait(barrier, len(peers) + depth - 1)
+    pair[0] = values[...]
+    for step, peer in enumerate(peers):
+        copy = pltpu.make_async_remote_copy(
+            pair.at[step], come.at[step], sent_sem.at[step], come_sem.at[step], device_id=peer, device_id_type=MESH
+        )
+        copy.start()
+        copy.wait()
+        pair[step + 1] = pair[step] + come[step]
+
+    def outward(other):
+        return pltpu.make_async_remote_copy(
+            pair.at[len(peers)], far.at[z], far_sent.at[other], far_come.at[z], device_id=at_row(other), device_id_type=MESH
+        )
+
+    def inward(other):
+        return pltpu.make_async_remote_copy(
+            pair.at[len(peers)], far.at[other], far_sent.at[other], far_come.at[other], device_id=at_row(other), device_id_type=MESH
+        )
+
+    along(lambda other: outward(other).start())
+    far[z] = pair[len(peers)]
+    along(lambda other: outward(other).wait_send())
+    along(lambda other: inward(other).wait_recv())
+    out[...] = far[0]
+
+    def add(other, carry):
+        out[...] += far[other]
+        return carry
+
+    lax.fori_loop(1, depth, add, 0)
+
+
+def total_over(mesh, values, collective_id):
+    depth = mesh.shape["dp"] // 4
+    return pl.pallas_call(
+        functools.partial(total_body, depth),
+        out_shape=jax.ShapeDtypeStruct(values.shape, F32),
+        in_specs=[VMEM],
+        out_specs=VMEM,
+        scratch_shapes=[
+            pltpu.VMEM((4, *values.shape), F32), pltpu.VMEM((3, *values.shape), F32), pltpu.VMEM((depth, *values.shape), F32),
+            pltpu.SemaphoreType.DMA((3,)), pltpu.SemaphoreType.DMA((3,)), pltpu.SemaphoreType.DMA((depth,)),
+            pltpu.SemaphoreType.DMA((depth,)),
+        ],
+        compiler_params=pltpu.CompilerParams(collective_id=collective_id, has_side_effects=True),
+    )(values)
 
 
 def branch_index_pair(branch, first, second, *operands):
@@ -816,7 +943,7 @@
         group_rows = branch_blocks.shape[2] * members
         share = branch_blocks.shape[2]
         taps_of = [length // k for k in SCALES]
-        tall = up_to(max(taps_of), 8)
+        tall = up_to(max(taps_of) + 1, 8)
         pitches = [up_to(n, 16) for n in taps_of]
         reach = max(SCALES)
         most = slots * max(pitches)
@@ -853,19 +980,10 @@
         iso_weight = jnp.concatenate(padded, axis=0)
         shift = jnp.concatenate(shifts).astype(jnp.int32)
 
-        counts = lax.all_gather(live, "dp", axis=0, tiled=True)
-        alive = (jnp.arange(slots)[None, :] < counts[:, None]).reshape(-1)
-        places = jnp.arange(members * slots)
-        rank = jnp.sum(jnp.logical_and(alive[None, :], places[None, :] < places[:, None]).astype(jnp.int32), axis=1)
-        order = jnp.sum(
-            jnp.where(jnp.logical_and(alive[:, None], rank[:, None] == places[None, :]), places[:, None], 0), axis=0
-        ).astype(jnp.int32)
-        count = jnp.sum(counts)[None].astype(jnp.int32)
-
         def windows_shape(kind):
             return jax.ShapeDtypeStruct((slots, tall, width), kind)
 
-        full = jax.ShapeDtypeStruct((slots, length, width), BF)
+        full = jax.ShapeDtypeStruct((slots // 2, length, width), BF)
         taps_shape = jax.ShapeDtypeStruct((most, reach * width), BF)
         part_shape = jax.ShapeDtypeStruct((max(r[1] - r[0] for r in down_ranges) * chunk, width), BF)
         up_part_shape = jax.ShapeDtypeStruct((max(r[1] - r[0] for r in up_ranges) * chunk, width), BF)
@@ -889,12 +1007,12 @@
             return pltpu.VMEM((count_of, width // LANES, pitches[index] * SCALES[index], LANES), F32)
 
         def down_of(index):
-            def run(x, weight, bias):
+            def run(*operands):
                 return call(down_body, index, 0, (windows_shape(F32), windows_shape(BF), taps_shape),
-                            [pltpu.VMEM((width // LANES, pitches[index] * SCALES[index], LANES), F32)], 0, x, weight, bias)
+                            [pltpu.VMEM((width // LANES, pitches[index] * SCALES[index], LANES), F32)], 1, *operands)
             return run
 
-        pre, act, taps = branch_index_pair(branch, down_of(0), down_of(1), inputs, down_weight, bias)
+        pre, act, taps = branch_index_pair(branch, down_of(0), down_of(1), live, inputs, down_weight, bias)
 
         passes = 1 if members <= 32 else slots
         per = slots // passes
@@ -916,52 +1034,37 @@
             return jnp.concatenate([r.reshape(per, tall, width) for r in results], axis=0)
 
         acts = spread_windows(act, 3)
+        alive = acts[:, tall - 1, 0] > 0.5
+        places = jnp.arange(members * slots)
+        rank = jnp.sum(jnp.logical_and(alive[None, :], places[None, :] < places[:, None]).astype(jnp.int32), axis=1)
+        order = jnp.sum(
+            jnp.where(jnp.logical_and(alive[:, None], rank[:, None] == places[None, :]), places[:, None], 0), axis=0
+        ).astype(jnp.int32)
+        count = jnp.sum(alive.astype(jnp.int32))[None]
         [terms] = iso_call(False, order, count, shift, iso_weight, acts)
         pre_iso = sum_windows(terms, 16)
 
         def up_of(index):
             def run(*operands):
-                return call(up_body, index, up_offs[index], full, [rows_scratch(index), spread_scratch(index)], 1, *operands)
+                return call(up_body, index, up_offs[index], (full, full), [rows_scratch(index), spread_scratch(index)], 2, *operands)
             return run
 
-        branch_out = branch_index_pair(branch, up_of(0), up_of(1), live, pre_iso, up_weight, inputs, gain, bias)
-
-        def swap(values):
-            return lax.ppermute(values, "branch", [(0, 1), (1, 0)])
-
-        def part_at(values, which):
-            return lax.dynamic_index_in_dim(values.reshape(MICRO, 2, length, width), which, 1, keepdims=False)
-
-        own = part_at(branch_out, branch).reshape(-1, width)
-        other = swap(part_at(branch_out, 1 - branch)).reshape(-1, width)
-        merge_own = lax.dynamic_slice_in_dim(merge_weight, branch * width, width, 0)
-        merge_other = lax.dynamic_slice_in_dim(merge_weight, (1 - branch) * width, width, 0)
-        (layer_out, grad_own, grad_other, normed, hidden, grad_inner, grad_outer, grad_merged, bias_grad, sums) = feed_call(
-            live, half, own, other, d_out.reshape(-1, width), merge_own, merge_other, ff_in, ff_in_bias[None], ff_out,
-            shared_biases, shared_gains, 3,
-        )
-        arrived = swap(grad_other.reshape(MICRO, length, width))
-        kept = grad_own.reshape(MICRO, length, width)
-        grad_branch = jnp.where(
-            branch == 0, jnp.stack([kept, arrived], axis=1), jnp.stack([arrived, kept], axis=1)
-        ).reshape(slots, length, width)
-        ff_in_grad = dot_at(normed, grad_inner)
-        ff_out_grad = dot_at(hidden, grad_outer)
-        merge_own_grad, merge_other_grad = dot_at(own, grad_merged), dot_at(other, grad_merged)
-        merge_grad = jnp.where(
-            branch == 0, jnp.concatenate([merge_own_grad, merge_other_grad]), jnp.concatenate([merge_other_grad, merge_own_grad])
-        )
-        wide = lax.psum((merge_grad.astype(BF), ff_in_grad.astype(BF), ff_out_grad.astype(BF)), ("branch", "dp"))
+        bo_own, bo_send = branch_index_pair(branch, up_of(0), up_of(1), live, half, pre_iso, up_weight, inputs, gain, bias)
+        (layer_out, grad_own, arrived, merge_grad, ff_in_grad, ff_out_grad, bias_grad, sums) = feed_call(
+            live, bo_own.reshape(-1, width), bo_send.reshape(-1, width), d_out.reshape(-1, width), merge_weight, ff_in,
+            ff_in_bias[None], ff_out, shared_biases, shared_gains, 3, 7,
+        )
+        wide = lax.psum((merge_grad, ff_in_grad, ff_out_grad), ("branch", "dp"))
 
         def up_back_of(index):
             def run(*operands):
                 return call(up_back_body, index, up_offs[index],
                             (windows_shape(BF), jax.ShapeDtypeStruct((8, width), F32), taps_shape, up_part_shape),
-                            [rows_scratch(index), spread_scratch(index)], 1, *operands)
+                            [rows_scratch(index), spread_scratch(index)], 2, *operands)
             return run
 
         grad_iso, vectors, grad_taps, up_part = branch_index_pair(
-            branch, up_back_of(0), up_back_of(1), live, grad_branch, pre_iso, up_weight, inputs, gain, bias
+            branch, up_back_of(0), up_back_of(1), live, half, grad_own.reshape(full.shape), arrived.reshape(full.shape), pre_iso, up_weight, inputs, gain, bias
         )
         grads = spread_windows(grad_iso, 4)
         back_terms, kernel_grad = iso_call(True, order, count, shift, iso_weight, acts, grads)
@@ -969,20 +1072,22 @@
 
         def down_back_of(index):
             def run(*operands):
-                return call(down_back_body, index, 0, (full, jax.ShapeDtypeStruct((1, width), F32), part_shape),
-                            [rows_scratch(index), spread_scratch(index)], 1, *operands)
+                return call(down_back_body, index, 0, (full, full, jax.ShapeDtypeStruct((1, width), F32), part_shape),
+                            [rows_scratch(index), spread_scratch(index)], 2, *operands)
             return run
 
-        grad_values, down_vector, down_part = branch_index_pair(
-            branch, down_back_of(0), down_back_of(1), live, grad_act, pre, grad_taps, taps, down_weight
-        )
-        arrived_values = swap(part_at(grad_values, 1 - branch))
-        grad_inputs = (part_at(grad_values, branch).astype(F32) + arrived_values.astype(F32)).astype(BF)
-
-        vectors = vectors.at[1].set(down_vector[0])
-        both = jnp.where((jnp.arange(2) == branch)[:, None, None], vectors[None, :5], 0.0)
-        small = lax.psum((both, bias_grad, sums), ("branch", "dp"))
-        own_vectors = lax.dynamic_slice_in_dim(small[0], branch, 1, 0)
+        values_keep, values_send, down_vector, down_part = branch_index_pair(
+            branch, down_back_of(0), down_back_of(1), live, half, grad_act, pre, grad_taps, taps, down_weight
+        )
+        arrived_values = lax.ppermute(values_send, "branch", [(0, 1), (1, 0)])
+        grad_inputs = (values_keep.astype(F32) + arrived_values.astype(F32)).astype(BF)
+
+        vectors = jnp.concatenate([vectors[:1], down_vector, vectors[2:5]], axis=0)
+        both = jnp.where((jnp.arange(2) == branch)[:, None, None], vectors[None], 0.0).reshape(10, width)
+        pieces_of = bias_grad.shape[1] // width
+        small = total_over(mesh, jnp.concatenate([sums, bias_grad.reshape(pieces_of, width), both, jnp.zeros((2, width), F32)]), 8)
+        own_vectors = lax.dynamic_slice_in_dim(small[8 + pieces_of :], 5 * branch, 5, 0)[None]
+        bias_total = small[8 : 8 + pieces_of].reshape(-1)
 
         up_sum = reduce_rows(mesh, up_part, chunk, npd, up_ranges, 5, F32).reshape(share, width)
         down_sum = reduce_rows(mesh, down_part, chunk, npd, down_ranges, 6, F32, swaps).reshape(share, width)
@@ -996,8 +1101,8 @@
         grad_blocks = jnp.stack(group_grads)[None]
         return (
             layer_out.reshape(MICRO, 1, 1, length, width), grad_inputs[:, None, None], grad_blocks,
-            own_vectors[:, 0], own_vectors[:, 1:], wide[0].astype(F32), wide[1].astype(F32), small[1][0],
-            wide[2].astype(F32), small[2][:4], small[2][4:6],
+            own_vectors[:, 0], own_vectors[:, 1:], wide[0].astype(F32), wide[1].astype(F32), bias_total,
+            wide[2].astype(F32), small[:4], small[4:6],
         )
 
     from jax.sharding import PartitionSpec as P

time: 1030 us -> 965 us (0.937)
  Pallas kernels: 729 us -> 891 us
  blocking collectives: 95.1 us -> 0 us
  waiting for transfers between devices: 93.8 us -> 0.02 us
  matrix products: 21.9 us -> 0 us
  local copies, waits for them, and re-layouts: 26.2 us -> 14.5 us
    ppermute x3 -> x1, waiting for transfers between devices: 93.8 us -> 0.01 us  [per_device(): arrived_values = lax.ppermute(values_send, 'branch', [(0, 1), (1, 0)])]
    psum x1 -> x0, blocking collectives: 87.5 us -> none  [per_device(): small = lax.psum((both, bias_grad, sums), ('branch', 'dp'))]
    pallas_call x0 -> x1, Pallas kernels: none -> 81.2 us  [total_over(): pl.pallas_call(functools.partial(total_body, depth), out_shape=jax.ShapeD...]
    pallas_call x1, Pallas kernels: 49.2 us -> 115 us  [feed_call(): pl.pallas_call(functools.partial(feed_body, per_window, 512), out_shape=[...]
    pallas_call x4, Pallas kernels: 242 us -> 265 us  [reduce_rows(): pl.pallas_call(functools.partial(reduce_body, depth, npd, rows, ranges, s...]
    dot_general x4 -> x0, matrix products: 21.9 us -> none  [dot_at(): lax.dot_general(a, b, (((0,), (0,)), ((), ())), preferred_element_type=F32)]
    pallas_call x4, Pallas kernels: 256 us -> 236 us  [gather_rows(): pl.pallas_call(functools.partial(gather_body, depth, npd, rows, base, ran...]
    pallas_call x2, Pallas kernels: 72 us -> 84.9 us  [iso_call(): pl.pallas_call(functools.partial(body, tall, pitch, blocks, steps), out_s...]
  transfers between devices with their start and end apart: 4 -> 2, of which waited for: 2 -> 0; matrix products, arithmetic and copies ran while one was open for 6% -> 2% of each run, Pallas kernels for 38% -> 26%
where the time goes in v2:
time: 965 us; the launch traced here: 952 us
  Pallas kernels  891 us (92%)
  other arithmetic  29.3 us (3%)
  between operations  15.5 us (2%)
  local copies, waits for them, and re-layouts  14.5 us (2%)
    pallas_call x4, Pallas kernels, reduce_rows(): pl.pallas_call(functools.partial(reduce_body, depth, npd, rows, ranges, s...  265 us
    pallas_call x4, Pallas kernels, gather_rows(): pl.pallas_call(functools.partial(gather_body, depth, npd, rows, base, ran...  236 us
    pallas_call x1, Pallas kernels, feed_call(): pl.pallas_call(functools.partial(feed_body, per_window, 512), out_shape=[...  115 us
    pallas_call x4, Pallas kernels, call(): pl.pallas_call(functools.partial(body, k, n, pitch, off), out_shape=outs,...  110 us
    pallas_call x2, Pallas kernels, iso_call(): pl.pallas_call(functools.partial(body, tall, pitch, blocks, steps), out_s...  84.9 us
    pallas_call x1, Pallas kernels, total_over(): pl.pallas_call(functools.partial(total_body, depth), out_shape=jax.ShapeD...  81.2 us
  transfers between devices with their start and end apart: 2, of which 0 were waited for; matrix products, arithmetic and copies ran while one was open for 2% of the time, Pallas kernels for 26%

profile of v2, /device:TPU:19, one launch (start us, length us, event | category | flops | bytes accessed | tf_op | source)
XLA Modules:
  0.0 951.8 jit_solution(16131229963999740110)
XLA Ops:
  7.9 3.7 slice_bitcast_fusion
  11.5 73.2 %shard_map.203 = bf16[8280,512]{1,0:T(8,128)(2,1)} custom-call(bf16[1472,512]{1,0:T(8,128)(2,1)} %get-tuple-element.426.src), custom_call_target="tpu_custom_call" | custom-call | tf_op jit(solution)/shard_map/pallas_call | solution.py:164
  84.7 16.0 %conditional.4 = ((f32[6,72,512]{2,1,0:T(8,128)}, bf16[6,72,512]{2,1,0:T(8,128)(2,1)S(1)}, bf16[480,8192]{1,0:T(8,128)(2,1)})) conditional(s32[]{:T(128)} %convert_element_type.36, (s32[1]{0:T(128)}, bf16[6,816,512]{2,1,0:T(8,128)(2,1)}, bf16[8280,512]{1,0:T(8,128)(2,1)}, f32[4,512]{1,0:T(4,128)S(1)}) %tuple.114, (s32[1]{0:T(128)}, ...), branch_computations={%region_0.1_spmd, %region_1.2_spmd} | conditional | bytes 8 | solution.py:934
  84.7 16.0 %branch_0_fun.6 = (f32[6,72,512]{2,1,0:T(8,128)}, bf16[6,72,512]{2,1,0:T(8,128)(2,1)S(1)}, bf16[480,8192]{1,0:T(8,128)(2,1)}) custom-call(s32[1]{0:T(128)} %get-tuple-element.168.live, bf16[6,816,512]{2,1,0:T(8,128)(2,1)} %get-tuple-element.169.x, bf16[8280,512]{1,0:T(8,128)(2,1)} %get-tuple-element.170.weight, f32[4,512]{1,0:T(4,128)S(1)} %get-tuple-element.171.bias), custom_call_target="tpu_custom_call" | custom-call | tf_op jit(solution)/shard_map/cond/branch_0_fun/pallas_call | solution.py:994
  100.7 49.0 %shard_map.204 = bf16[6912,512]{1,0:T(8,128)(2,1)} custom-call(bf16[432,512]{1,0:T(8,128)(2,1)S(1)} %bitcast.92), custom_call_target="tpu_custom_call" | custom-call | tf_op jit(solution)/shard_map/pallas_call | solution.py:164
  149.7 2.7 compare_reduce_fusion
  155.5 2.3 pad_maximum_fusion.refs_8_.refs_16_
  157.8 28.0 %shard_map.205 = bf16[96,72,512]{2,1,0:T(8,128)(2,1)} custom-call(s32[96]{0:T(128)} %select_reduce_fusion.order, s32[1]{0:T(128)} %bitcast.11.count, s32[8]{0:T(128)} %pad_add_fusion.shift, bf16[96,72,512]{2,1,0:T(8,128)(2,1)} %bitcast.53, bf16[96,72,512]{2,1,0:T(8,128)(2,1)} %bitcast.54, bf16[96,72,512]{2,1,0:T(8,128)(2,1)} %bitcast.55, ...), custom_call_target="tpu_custom_call" | custom-call | flops 9663676416 | bytes 4194304 | tf_op jit(solution)/shard_map/pallas_call | solution.py:716
  185.8 46.6 %shard_map.206 = f32[2,216,512]{2,1,0:T(8,128)S(1)} custom-call(bf16[6912,512]{1,0:T(8,128)(2,1)} %bitcast.77), custom_call_target="tpu_custom_call" | custom-call | tf_op jit(solution)/shard_map/pallas_call | solution.py:342
  232.4 54.2 %shard_map.207 = bf16[8280,512]{1,0:T(8,128)(2,1)} custom-call(bf16[1472,512]{1,0:T(8,128)(2,1)} %get-tuple-element.425.src), custom_call_target="tpu_custom_call" | custom-call | tf_op jit(solution)/shard_map/pallas_call | solution.py:164
  286.6 22.3 %conditional.5 = (bf16[2448,512]{1,0:T(8,128)(2,1)}, bf16[2448,512]{1,0:T(8,128)(2,1)}) conditional(s32[]{:T(128)} %convert_element_type.36, (s32[1]{0:T(128)}, s32[1]{0:T(128)}, f32[6,72,512]{2,1,0:T(8,128)S(1)}, bf16[8280,512]{1,0:T(8,128)(2,1)}, bf16[6,816,512]{2,1,0:T(8,128)(2,1)}, /*index=5*/f32[1,512]{1,0:T(1,128)S(1)}, ...), branch_computations={%region_5.6_spmd, %region_6.7_spmd} | conditional | bytes 16 | solution.py:934
  286.6 22.1 %branch_0_fun.7 = (bf16[3,816,512]{2,1,0:T(8,128)(2,1)}, bf16[3,816,512]{2,1,0:T(8,128)(2,1)}) custom-call(s32[1]{0:T(128)} %get-tuple-element.176.live, s32[1]{0:T(128)} %get-tuple-element.177.half, f32[6,72,512]{2,1,0:T(8,128)S(1)} %get-tuple-element.178.pre_iso, bf16[8280,512]{1,0:T(8,128)(2,1)} %get-tuple-element.179.weight, ...), custom_call_target="tpu_custom_call" | custom-call | tf_op jit(solution)/shard_map/cond/branch_0_fun/pallas_call | solution.py:994
  308.9 115.1 %shard_map.208 = (bf16[2448,512]{1,0:T(8,128)(2,1)}, bf16[2448,512]{1,0:T(8,128)(2,1)S(1)}, bf16[2448,512]{1,0:T(8,128)(2,1)}, bf16[1024,512]{1,0:T(8,128)(2,1)}...) custom-call(s32[1]{0:T(128)S(6)} %copy.61.live, ...), custom_call_target="tpu_custom_call" | custom-call | flops 41070624768 | bytes 41943040 | tf_op jit(solution)/shard_map/pallas_call | solution.py:843
  424.0 46.3 %conditional.6 = (bf16[6,72,512]{2,1,0:T(8,128)(2,1)}, bf16[480,8192]{1,0:T(8,128)(2,1)}, bf16[8280,512]{1,0:T(8,128)(2,1)}, f32[1,512]{1,0:T(1,128)S(1)}, f32[3,512]{1,0:T(4,128)S(1)}) conditional(s32[]{:T(128)} %convert_element_type.36, (s32[1]{0:T(128)}, s32[1]{0:T(128)}, bf16[3,816,512]{2,1,0:T(8,128)(2,1)S(1)}, ...), branch_computations={%region_7.8_spmd.clone.clone, %region_8.9_spmd.clone.clone} | conditional | bytes 16424 | solution.py:934
  424.2 44.2 %branch_0_fun.9 = (bf16[6,72,512]{2,1,0:T(8,128)(2,1)}, f32[8,512]{1,0:T(8,128)}, bf16[480,8192]{1,0:T(8,128)(2,1)}, bf16[8280,512]{1,0:T(8,128)(2,1)}) custom-call(s32[1]{0:T(128)} %get-tuple-element.384.live, s32[1]{0:T(128)} %get-tuple-element.385.half, bf16[3,816,512]{2,1,0:T(8,128)(2,1)S(1)} %get-tuple-element.386.grad_own, ...), custom_call_target="tpu_custom_call" | custom-call | tf_op jit(solution)/shard_map/cond/branch_0_fun/pallas_call | solution.py:994
  470.3 59.5 %shard_map.209 = bf16[6912,512]{1,0:T(8,128)(2,1)} custom-call(bf16[432,512]{1,0:T(8,128)(2,1)} %bitcast.21.src), custom_call_target="tpu_custom_call" | custom-call | tf_op jit(solution)/shard_map/pallas_call | solution.py:164
  529.7 57.0 %shard_map.210 = (bf16[96,72,512]{2,1,0:T(8,128)(2,1)}, f32[4096,512]{1,0:T(8,128)}) custom-call(s32[96]{0:T(128)} %select_reduce_fusion.order, s32[1]{0:T(128)} %bitcast.11.count, s32[8]{0:T(128)} %pad_add_fusion.shift, bf16[96,72,512]{2,1,0:T(8,128)(2,1)} %bitcast.61, bf16[96,72,512]{2,1,0:T(8,128)(2,1)} %bitcast.62, bf16[96,72,512]{2,1,0:T(8,128)(2,1)} %bitcast.63, ...), custom_call_target="tpu_custom_call" | custom-call | flops 19327352832 | bytes 4194304 | tf_op jit(solution)/shard_map/pallas_call | solution.py:716
  586.7 48.7 %shard_map.211 = f32[2,216,512]{2,1,0:T(8,128)S(1)} custom-call(bf16[6912,512]{1,0:T(8,128)(2,1)} %bitcast.90), custom_call_target="tpu_custom_call" | custom-call | tf_op jit(solution)/shard_map/pallas_call | solution.py:342
  635.5 27.7 %conditional.7 = ((bf16[3,816,512]{2,1,0:T(8,128)(2,1)}, bf16[3,816,512]{2,1,0:T(8,128)(2,1)}, f32[1,512]{1,0:T(1,128)S(1)}, bf16[8280,512]{1,0:T(8,128)(2,1)})) conditional(s32[]{:T(128)} %convert_element_type.36, (s32[1]{0:T(128)}, s32[1]{0:T(128)}, f32[2,216,512]{2,1,0:T(8,128)S(1)}, f32[6,72,512]{2,1,0:T(8,128)S(1)}, ...), branch_computations={%region_9.10_spmd, %region_10.11_spmd} | conditional | bytes 8 | solution.py:934
  635.7 27.2 %branch_0_fun.8 = (bf16[3,816,512]{2,1,0:T(8,128)(2,1)}, bf16[3,816,512]{2,1,0:T(8,128)(2,1)}, f32[1,512]{1,0:T(1,128)S(1)}, bf16[8280,512]{1,0:T(8,128)(2,1)}) custom-call(s32[1]{0:T(128)} %get-tuple-element.220.live, s32[1]{0:T(128)} %get-tuple-element.221.half, f32[6,72,512]{2,1,0:T(8,128)S(1)} %bitcast.88, f32[6,72,512]{2,1,0:T(8,128)S(1)} %get-tuple-element.223.pre, ...), custom_call_target="tpu_custom_call" | custom-call | tf_op jit(solution)/shard_map/cond/branch_0_fun/pallas_call | solution.py:994
  665.6 81.2 %shard_map.214 = f32[24,512]{1,0:T(8,128)} custom-call(f32[24,512]{1,0:T(8,128)} %maximum_maximum_fusion.values), custom_call_target="tpu_custom_call" | custom-call | tf_op jit(solution)/shard_map/pallas_call | solution.py:919
  748.8 107.7 %shard_map.212 = f32[8,184,512]{2,1,0:T(8,128)S(1)} custom-call(bf16[8280,512]{1,0:T(8,128)(2,1)} %get-tuple-element.381.src), custom_call_target="tpu_custom_call" | custom-call | tf_op jit(solution)/shard_map/pallas_call | solution.py:342
  856.5 61.7 %shard_map.213 = f32[8,184,512]{2,1,0:T(8,128)S(1)} custom-call(bf16[8280,512]{1,0:T(8,128)(2,1)} %get-tuple-element.283.src), custom_call_target="tpu_custom_call" | custom-call | tf_op jit(solution)/shard_map/pallas_call | solution.py:342
  918.2 1.6 copy-done
  920.4 1.3 fusion.18
  923.0 4.7 fusion.2
  927.7 3.3 maximum_bitcast_fusion
  931.0 3.9 fusion.3
  934.9 3.0 convert_element_type.42
  937.9 2.5 convert_element_type.43
  940.5 2.6 convert_element_type.44
  943.1 1.5 copy.62
  (58 shorter events, 10.8 us)
Async XLA Ops:
  7.2 927.7 %all-reduce.3.cloned.1.call-start = ((), (), s32[]{:S(2)}) async-start(), calls=%async_computation | async-start | bytes 10485760 | tf_op jit(solution)/shard_map/psum | solution.py:1057
  11.5 73.2 %copy-start.7 = (f32[1,4,512]{2,1,0:T(4,128)S(1)}, f32[1,4,512]{2,1,0:T(4,128)}, u32[]{:S(2)}) copy-start(f32[1,4,512]{2,1,0:T(4,128)} %param.24) | copy-start | bytes 24580
  100.7 53.9 %copy-start.1 = (bf16[1,2,1472,512]{3,2,1,0:T(8,128)(2,1)S(1)}, bf16[1,2,1472,512]{3,2,1,0:T(8,128)(2,1)}, u32[]{:S(2)}) copy-start(bf16[1,2,1472,512]{3,2,1,0:T(8,128)(2,1)} %param.22) | copy-start | bytes 9043972
  232.4 54.2 %copy-start.8 = (f32[1,512]{1,0:T(1,128)S(1)}, f32[1,512]{1,0:T(1,128)}, u32[]{:S(2)}) copy-start(f32[1,512]{1,0:T(1,128)} %param.23) | copy-start | bytes 6148
  586.7 48.8 %copy-start.2 = (f32[6,72,512]{2,1,0:T(8,128)S(1)}, f32[6,72,512]{2,1,0:T(8,128)}, u32[]{:S(2)}) copy-start(f32[6,72,512]{2,1,0:T(8,128)} %get-tuple-element.276) | copy-start | bytes 2654212
  663.1 0.9 copy-start.10
  663.2 1.7 copy-start.9
  663.2 267.9 %collective-permute-start = (bf16[3,816,512]{2,1,0:T(8,128)(2,1)}, bf16[3,816,512]{2,1,0:T(8,128)(2,1)}, u32[]{:S(2)}, u32[]{:S(2)}) collective-permute-start(bf16[3,816,512]{2,1,0:T(8,128)(2,1)} %get-tuple-element.383), channel_id=1, source_target_pairs={{0,16},{16,0},{1,17},{17,1},{2,18},{18,2},{3,19},{19,3},{4,20},{20... | collective-permute-start | bytes 7520264 | tf_op jit(solution)/shard_map/ppermute | solution.py:1082
  918.2 1.6 copy-start
  927.7 3.3 copy-start.4
  934.9 3.0 copy-start.6
  937.9 2.5 copy-start.5
  940.4 2.6 copy-start.3
Sparse Core Ops, SparseCore 0:
  663.4 180.1 all-reduce.2

commit v3 on v2

--- a/solution.py
+++ b/solution.py
@@ -13,6 +13,14 @@
     return lax.axis_index("branch"), me, me // 4, (me // 2) % 2, me % 2
 
 
+def listed(j, b, lists):
+    found = jnp.bool_(False)
+    for which, owners in enumerate(lists):
+        for owner in owners:
+            found = jnp.logical_or(found, jnp.logical_and(b == which, j == owner))
+    return found
+
+
 def meet(depth, b, me, z):
     barrier = pltpu.get_barrier_semaphore()
     y, c = (me // 2) % 2, me % 2
@@ -31,9 +39,8 @@
     pl.semaphore_wait(barrier, count)
 
 
-def gather_body(depth, npd, rows, base, ranges, swaps, src, dst, hold, local_sem, recv_sem, send_sem):
+def gather_region(depth, npd, rows, base, ranges, swaps, duals, src, dst, hold, local_sem, recv_sem, send_sem):
     b, me, z, y, c = place()
-    meet(depth, b, me, z)
     (a0, a1), (b0, b1) = ranges
     q0 = jnp.where(b == 0, a0, b0)
     q1 = jnp.where(b == 0, a1, b1)
@@ -67,13 +74,11 @@
     def put(q, i):
         return pltpu.make_async_copy(hold.at[i], chunk(dst, q - q0), local_sem.at[1, i])
 
-    each_own(lambda q, i: take(q, i).start())
-
     def column(j):
         ys = (j // 2) % 2
         return jnp.where(j == swap, 1 - ys, ys)
 
-    def each(core, steps, what):
+    def each(core, what):
         def over(zs, t, s):
             for ys in (y, 1 - y):
                 j = (zs * 2 + ys) * 2 + core
@@ -86,7 +91,7 @@
                 def _():
                     what(q, j)
 
-        def over_steps(s, carry):
+        def over_step(s):
             def over_far(t, inner):
                 @pl.when(z >= t)
                 def _():
@@ -98,26 +103,27 @@
 
                 return inner
 
-            return lax.fori_loop(0, depth, over_far, carry)
-
-        lax.fori_loop(0, npd + depth + 1, over_steps, 0)
+            lax.fori_loop(0, depth, over_far, 0)
+
+        return over_step
 
     def sends(q, j, act, from_own=False):
         zs, ys = j // 4, (j // 2) % 2
-        col = column(j)
+        col, dual = column(j), listed(j, b, duals)
         chain = y == col
-
-        @pl.when(jnp.logical_and(chain, jnp.logical_and(z >= zs, z < depth - 1)))
+        along = jnp.logical_or(chain, dual)
+
+        @pl.when(jnp.logical_and(along, jnp.logical_and(z >= zs, z < depth - 1)))
         def _():
             act(remote(0, q, (b, me + 4), from_own))
 
-        @pl.when(jnp.logical_and(chain, jnp.logical_and(z <= zs, z > 0)))
+        @pl.when(jnp.logical_and(along, jnp.logical_and(z <= zs, z > 0)))
         def _():
             act(remote(1, q, (b, me - 4), from_own))
 
         start_here = jnp.logical_and(z == zs, ys != col)
 
-        @pl.when(chain != start_here)
+        @pl.when(jnp.logical_and(chain != start_here, jnp.logical_or(jnp.logical_not(dual), me == j)))
         def _():
             act(remote(2, q, y_peer, from_own))
 
@@ -133,13 +139,14 @@
             remote(3, q, core_peer).wait_recv()
             sends(q, j, lambda copy: copy.start())
 
-    each(c, npd + depth + 1, forward)
+    def begin():
+        each_own(lambda q, i: take(q, i).start())
 
     def swap_own(q, i):
         take(q, i).wait()
         put(q, i).start()
 
-    each_own(swap_own)
+    work = each(c, forward)
 
     def finish(q, carry):
         j = q // npd
@@ -154,31 +161,60 @@
 
         return carry
 
-    lax.fori_loop(q0, q1, finish, 0)
-    each_own(lambda q, i: put(q, i).wait())
-
-
-def gather_rows(mesh, src, base, rows, npd, ranges, collective_id, swaps=(-1, -1)):
-    depth = mesh.shape["dp"] // 4
-    count = max(r[1] - r[0] for r in ranges)
-    return pl.pallas_call(
-        functools.partial(gather_body, depth, npd, rows, base, ranges, swaps),
-        out_shape=jax.ShapeDtypeStruct((count * rows, src.shape[1]), src.dtype),
-        in_specs=[ANY],
-        out_specs=ANY,
-        scratch_shapes=[
-            pltpu.VMEM((npd, rows, src.shape[1]), src.dtype),
+    def end():
+        each_own(swap_own)
+        lax.fori_loop(q0, q1, finish, 0)
+        each_own(lambda q, i: put(q, i).wait())
+
+    return begin, work, end, npd + depth + 1
+
+
+def gather_body(depth, regions, *refs):
+    count = len(regions)
+    src, dsts, scratch = refs[0], refs[1 : 1 + count], refs[1 + count :]
+    b, me, z, y, c = place()
+    meet(depth, b, me, z)
+    phases = [
+        gather_region(depth, *region, src, dsts[r], *scratch[4 * r : 4 * r + 4]) for r, region in enumerate(regions)
+    ]
+    for begin, *_ in phases:
+        begin()
+
+    def step(s, carry):
+        for phase in phases:
+            phase[1](s)
+        return carry
+
+    lax.fori_loop(0, max(phase[3] for phase in phases), step, 0)
+    for phase in phases:
+        phase[2]()
+
+
+def gather_rows(mesh, src, regions, collective_id):
+    depth, width = mesh.shape["dp"] // 4, src.shape[1]
+    shapes, scratch = [], []
+    for npd, rows, _, ranges, *_ in regions:
+        count = max(r[1] - r[0] for r in ranges)
+        shapes.append(jax.ShapeDtypeStruct((count * rows, width), src.dtype))
+        scratch += [
+            pltpu.VMEM((npd, rows, width), src.dtype),
             pltpu.SemaphoreType.DMA((2, npd)),
             pltpu.SemaphoreType.DMA((count,)),
             pltpu.SemaphoreType.DMA((4, count)),
-        ],
+        ]
+    return pl.pallas_call(
+        functools.partial(gather_body, depth, regions),
+        out_shape=shapes,
+        in_specs=[ANY],
+        out_specs=[ANY] * len(shapes),
+        scratch_shapes=scratch,
         compiler_params=pltpu.CompilerParams(collective_id=collective_id, has_side_effects=True),
+        cost_estimate=pl.CostEstimate(flops=5 * 10**10, bytes_accessed=2**24, transcendentals=0),
     )(src)
 
 
-def reduce_body(depth, npd, rows, ranges, swaps, lag, src, out, own, rc, ry, rz, fin, acc, own_sem, rc_sem, ry_sem, rz_sem, fin_sem, send_sem, fin_send):
+def reduce_region(depth, npd, rows, ranges, swaps, duals, lag, src, out, own, rc, ry, rz, acc, own_sem, rc_sem, ry_sem, rz_sem, send_sem):
     b, me, z, y, c = place()
-    meet(depth, b, me, z)
     (a0, a1), (b0, b1) = ranges
     q0 = jnp.where(b == 0, a0, b0)
     q1 = jnp.where(b == 0, a1, b1)
@@ -218,9 +254,8 @@
         return remote(2, own.at[k], rz.at[way, k], rz_sem.at[way, k], k, (up, down)[way])
 
     def to_owner(j, i):
-        return pltpu.make_async_remote_copy(
-            own.at[slot(j, i)], fin.at[i], fin_send.at[i], fin_sem.at[i], device_id=y_peer, device_id_type=MESH
-        )
+        k = slot(j, i)
+        return remote(2, own.at[k], ry.at[k], ry_sem.at[k], k, y_peer)
 
     def owners(n, core, what):
         pos, i = n // npd, n % npd
@@ -238,15 +273,13 @@
 
     total = depth * npd
 
-    def begin(n, carry):
+    def first(n, carry):
         owners(n, 1 - c, lambda j, i, zs, ys: to_core(j, i).start())
         owners(n, c, lambda j, i, zs, ys: keep(j, i).start())
         return carry
 
-    lax.fori_loop(0, total, begin, 0)
-
     def cross(j, i, zs, ys):
-        @pl.when(column(j) != y)
+        @pl.when(jnp.logical_and(column(j) != y, jnp.logical_not(listed(j, b, duals))))
         def _():
             k = slot(j, i)
             keep(j, i).wait()
@@ -255,13 +288,19 @@
             to_y(j, i).start()
 
     def chain(j, i, zs, ys):
-        @pl.when(column(j) == y)
+        dual = listed(j, b, duals)
+
+        @pl.when(jnp.logical_or(column(j) == y, dual))
         def _():
             k = slot(j, i)
             keep(j, i).wait()
             to_core(j, i).wait_recv()
-            to_y(j, i).wait_recv()
-            acc[...] = own[k].astype(jnp.float32) + rc[k].astype(jnp.float32) + ry[k].astype(jnp.float32)
+            acc[...] = own[k].astype(jnp.float32) + rc[k].astype(jnp.float32)
+
+            @pl.when(jnp.logical_or(jnp.logical_not(dual), jnp.logical_and(z == zs, ys == y)))
+            def _():
+                to_y(j, i).wait_recv()
+                acc[...] += ry[k].astype(jnp.float32)
 
             @pl.when(jnp.logical_and(z >= zs, z < depth - 1))
             def _():
@@ -291,32 +330,36 @@
 
             @pl.when(jnp.logical_and(z == zs, ys != y))
             def _():
-                to_owner(j, i).start()
-
-    def step(s, carry):
+                @pl.when(dual)
+                def _():
+                    to_y(j, i).start()
+
+                @pl.when(jnp.logical_not(dual))
+                def _():
+                    to_owner(j, i).start()
+
+    def step(s):
         @pl.when(s < total)
         def _():
             owners(s, c, cross)
 
-        @pl.when(s >= lag)
+        @pl.when(jnp.logical_and(s >= lag, s < total + lag))
         def _():
             owners(s - lag, c, chain)
 
-        return carry
-
-    lax.fori_loop(0, total + lag, step, 0)
-
     def sent(j, i, zs, ys):
-        @pl.when(column(j) != y)
+        dual = listed(j, b, duals)
+
+        @pl.when(jnp.logical_and(column(j) != y, jnp.logical_not(dual)))
         def _():
             to_y(j, i).wait_send()
 
             @pl.when(me == j)
             def _():
                 to_owner(j, i).wait_recv()
-                out[i] = fin[i].astype(out.dtype)
-
-        @pl.when(column(j) == y)
+                out[i] = ry[slot(j, i)].astype(out.dtype)
+
+        @pl.when(jnp.logical_or(column(j) == y, dual))
         def _():
             @pl.when(z != zs)
             def _():
@@ -324,45 +367,81 @@
 
             @pl.when(jnp.logical_and(z == zs, ys != y))
             def _():
-                to_owner(j, i).wait_send()
-
-    def end(n, carry):
+                @pl.when(dual)
+                def _():
+                    to_y(j, i).wait_send()
+
+                @pl.when(jnp.logical_not(dual))
+                def _():
+                    to_owner(j, i).wait_send()
+
+    def last(n, carry):
         owners(n, 1 - c, lambda j, i, zs, ys: to_core(j, i).wait_send())
         owners(n, c, sent)
         return carry
 
-    lax.fori_loop(0, total, end, 0)
-
-
-def reduce_rows(mesh, src, rows, npd, ranges, collective_id, dtype, swaps=(-1, -1), lag=2):
-    depth = mesh.shape["dp"] // 4
-    pairs = max((r[1] + npd - 1) // npd // 2 + (r[1] + npd - 1) // npd % 2 - r[0] // npd // 2 for r in ranges)
-    held, width = pairs * npd, src.shape[1]
-    block = (held, rows, width)
-    return pl.pallas_call(
-        functools.partial(reduce_body, depth, npd, rows, ranges, swaps, lag),
-        out_shape=jax.ShapeDtypeStruct((npd, rows, width), dtype),
-        in_specs=[ANY],
-        out_specs=pl.BlockSpec(memory_space=pltpu.VMEM),
-        scratch_shapes=[
-            pltpu.VMEM(block, src.dtype),
-            pltpu.VMEM(block, src.dtype),
-            pltpu.VMEM(block, src.dtype),
-            pltpu.VMEM((2, *block), src.dtype),
-            pltpu.VMEM((npd, rows, width), src.dtype),
+    return (
+        lambda: lax.fori_loop(0, total, first, 0),
+        step,
+        lambda: lax.fori_loop(0, total, last, 0),
+        total + lag,
+    )
+
+
+def reduce_body(depth, regions, *refs):
+    count = len(regions)
+    srcs, outs, scratch = refs[:count], refs[count : 2 * count], refs[2 * count :]
+    b, me, z, y, c = place()
+    meet(depth, b, me, z)
+    size = len(scratch) // count
+    phases = [
+        reduce_region(depth, *region, srcs[r], outs[r], *scratch[size * r : size * (r + 1)]) for r, region in enumerate(regions)
+    ]
+    for begin, *_ in phases:
+        begin()
+
+    def step(s, carry):
+        for phase in phases:
+            phase[1](s)
+        return carry
+
+    lax.fori_loop(0, max(phase[3] for phase in phases), step, 0)
+    for phase in phases:
+        phase[2]()
+
+
+def reduce_rows(mesh, srcs, regions, collective_id, dtype, lag=2):
+    depth, width = mesh.shape["dp"] // 4, srcs[0].shape[1]
+    kind = srcs[0].dtype
+    shapes, scratch = [], []
+    for npd, rows, ranges, *_ in regions:
+        pairs = max((r[1] + npd - 1) // npd // 2 + (r[1] + npd - 1) // npd % 2 - r[0] // npd // 2 for r in ranges)
+        held = pairs * npd
+        block = (held, rows, width)
+        shapes.append(jax.ShapeDtypeStruct((npd, rows, width), dtype))
+        scratch += [
+            pltpu.VMEM(block, kind),
+            pltpu.VMEM(block, kind),
+            pltpu.VMEM(block, kind),
+            pltpu.VMEM((2, *block), kind),
             pltpu.VMEM((rows, width), jnp.float32),
             pltpu.SemaphoreType.DMA((held,)),
             pltpu.SemaphoreType.DMA((held,)),
             pltpu.SemaphoreType.DMA((held,)),
             pltpu.SemaphoreType.DMA((2, held)),
-            pltpu.SemaphoreType.DMA((npd,)),
             pltpu.SemaphoreType.DMA((3, held)),
-            pltpu.SemaphoreType.DMA((npd,)),
-        ],
+        ]
+    return pl.pallas_call(
+        functools.partial(reduce_body, depth, tuple((*region, lag) for region in regions)),
+        out_shape=shapes,
+        in_specs=[ANY] * len(srcs),
+        out_specs=[pl.BlockSpec(memory_space=pltpu.VMEM)] * len(shapes),
+        scratch_shapes=scratch,
         compiler_params=pltpu.CompilerParams(
-            collective_id=collective_id, has_side_effects=True, vmem_limit_bytes=50 * 2**20
+            collective_id=collective_id, has_side_effects=True, vmem_limit_bytes=60 * 2**20
         ),
-    )(src)
+        cost_estimate=pl.CostEstimate(flops=5 * 10**10, bytes_accessed=2**24, transcendentals=0),
+    )(*srcs)
 SCALES = (12, 16)
 MICRO = 3
 GROUPS = 2
@@ -573,21 +652,14 @@
 SUBLANES = 8
 
 
-def shifted(copies, start, tall):
-    rows = pl.multiple_of(start // SUBLANES * SUBLANES, SUBLANES)
-    return copies[start % SUBLANES, pl.ds(rows, tall), :].astype(BF)
-
-
-def late_copies(copies, values):
-    tall = values.shape[0]
-    for b in range(SUBLANES):
-        copies[b, tall - b : 2 * tall - b, :] = values
-
-
-def early_copies(copies, values):
-    tall = values.shape[0]
-    for b in range(SUBLANES):
-        copies[b, : tall - b, :] = values[b:]
+def shifted(ref, start, tall):
+    width = ref.shape[1]
+    first = pl.multiple_of(start // SUBLANES * SUBLANES, SUBLANES)
+    ahead = start % SUBLANES
+    tiles = ref[pl.ds(first, tall + SUBLANES), :].reshape(tall // SUBLANES + 1, SUBLANES, width)
+    turned = pltpu.roll(tiles, (SUBLANES - ahead) % SUBLANES, 1)
+    row = lax.broadcasted_iota(jnp.int32, (tall // SUBLANES, SUBLANES, width), 1)
+    return jnp.where(row < SUBLANES - ahead, turned[:-1], turned[1:]).reshape(tall, width).astype(BF)
 
 
 PACK = 8
@@ -648,7 +720,7 @@
     @pl.when(step * PACK < count[0])
     def _():
         for e in range(PACK):
-            late_copies(buffer, jnp.where(step * PACK + e < count[0], acts[e][0].astype(F32), 0.0))
+            buffer[tall : 2 * tall, :] = (jnp.where(step * PACK + e < count[0], acts[e][0].astype(F32), 0.0))
             for m in range(blocks):
                 columns[e * pitch : e * pitch + tall, m * width : (m + 1) * width] = shifted(buffer, tall - shift[m], tall)
         total = dot(columns[...], weight[...])
@@ -676,7 +748,7 @@
     def _():
         for e in range(PACK):
             alive = step * PACK + e < count[0]
-            late_copies(buffer, jnp.where(alive, acts[e][0].astype(F32), 0.0))
+            buffer[tall : 2 * tall, :] = (jnp.where(alive, acts[e][0].astype(F32), 0.0))
             for m in range(blocks):
                 columns[e * pitch : e * pitch + tall, m * width : (m + 1) * width] = shifted(buffer, tall - shift[m], tall)
             gathered[e * pitch : e * pitch + tall, :] = jnp.where(alive, grads[e][0].astype(F32), 0.0).astype(BF)
@@ -684,7 +756,7 @@
             kernel_grad[m * width : (m + 1) * width, :] += dot_at(columns[:, m * width : (m + 1) * width], gathered[...])
         for e in range(PACK):
             alive = step * PACK + e < count[0]
-            early_copies(ahead, jnp.where(alive, grads[e][0].astype(F32), 0.0))
+            ahead[:tall, :] = (jnp.where(alive, grads[e][0].astype(F32), 0.0))
             for m in range(blocks):
                 columns[e * pitch : e * pitch + tall, m * width : (m + 1) * width] = shifted(ahead, shift[m], tall)
         total = dot_bt(columns[:, :width], weight[:width, :])
@@ -704,7 +776,7 @@
     held = pl.BlockSpec(weight.shape, lambda step, *_: (0, 0))
     out_shape = [jax.ShapeDtypeStruct((many, tall, width), BF)]
     out_specs = [ANY]
-    copies = pltpu.VMEM((SUBLANES, 2 * tall, width), F32)
+    copies = pltpu.VMEM((2 * tall + SUBLANES, width), F32)
     scratch = [copies, pltpu.VMEM((PACK * pitch, blocks * width), BF)]
     if back:
         out_shape.append(jax.ShapeDtypeStruct(weight.shape, F32))
@@ -958,10 +1030,11 @@
         up_ranges = tuple((s // chunk, -(-(s + k * width) // chunk)) for s, k in zip(up_starts, SCALES))
         up_offs = [s - r[0] * chunk for s, r in zip(up_starts, up_ranges)]
         swaps = (-1, 1) if members == 16 else (-1, -1)
-        own_blocks = branch_blocks[0]
-
-        down_weight = gather_rows(mesh, own_blocks[0], 0, chunk, npd, down_ranges, 1, swaps)
-        up_weight = gather_rows(mesh, own_blocks[1], 0, chunk, npd, up_ranges, 2)
+        none = ((), ())
+        own_rows = branch_blocks.reshape(GROUPS * share, width)
+        down_weight, up_weight = gather_rows(
+            mesh, own_rows, ((npd, chunk, 0, down_ranges, swaps, none), (npd, chunk, share, up_ranges, (-1, -1), none)), 1
+        )
 
         blocks = (share + width - 1) // width + 1
         k_of = jnp.where(branch == 0, SCALES[0], SCALES[1])
@@ -975,7 +1048,7 @@
             shifts.append(jnp.clip(n_of - 1 - start - jnp.arange(blocks), 0, tall))
             lead.append(first - start * width)
             insides.append(inside)
-            kept = jnp.where(inside[:, None], own_blocks[g], 0)
+            kept = jnp.where(inside[:, None], own_rows[g * share : (g + 1) * share], 0)
             padded.append(lax.dynamic_update_slice(jnp.zeros((blocks * width, width), BF), kept, (lead[g], 0)))
         iso_weight = jnp.concatenate(padded, axis=0)
         shift = jnp.concatenate(shifts).astype(jnp.int32)
@@ -1020,15 +1093,14 @@
 
         def spread_windows(values, collective_id):
             flat = values.reshape(slots * tall, width)
-            return gather_rows(mesh, flat, 0, slots * tall // 2, 2, ((0, 2 * members),) * 2, collective_id).reshape(
-                members * slots, tall, width
-            )
+            [every] = gather_rows(mesh, flat, ((2, slots * tall // 2, 0, ((0, 2 * members),) * 2, (-1, -1), none),), collective_id)
+            return every.reshape(members * slots, tall, width)
 
         def sum_windows(values, collective_id):
             parts = values.reshape(members, passes, per, tall, width)
             results = [
-                reduce_rows(mesh, parts[:, p].reshape(-1, width), per * tall // pieces, pieces,
-                            ((0, pieces * members),) * 2, collective_id + p, F32)
+                reduce_rows(mesh, [parts[:, p].reshape(-1, width)],
+                            ((pieces, per * tall // pieces, ((0, pieces * members),) * 2, (-1, -1), none),), collective_id + p, F32)[0]
                 for p in range(passes)
             ]
             return jnp.concatenate([r.reshape(per, tall, width) for r in results], axis=0)
@@ -1069,6 +1141,7 @@
         grads = spread_windows(grad_iso, 4)
         back_terms, kernel_grad = iso_call(True, order, count, shift, iso_weight, acts, grads)
         grad_act = sum_windows(back_terms, 32)
+        grad_act, wide = lax.optimization_barrier((grad_act, wide))
 
         def down_back_of(index):
             def run(*operands):
@@ -1079,24 +1152,29 @@
         values_keep, values_send, down_vector, down_part = branch_index_pair(
             branch, down_back_of(0), down_back_of(1), live, half, grad_act, pre, grad_taps, taps, down_weight
         )
-        arrived_values = lax.ppermute(values_send, "branch", [(0, 1), (1, 0)])
-        grad_inputs = (values_keep.astype(F32) + arrived_values.astype(F32)).astype(BF)
-
         vectors = jnp.concatenate([vectors[:1], down_vector, vectors[2:5]], axis=0)
         both = jnp.where((jnp.arange(2) == branch)[:, None, None], vectors[None], 0.0).reshape(10, width)
         pieces_of = bias_grad.shape[1] // width
         small = total_over(mesh, jnp.concatenate([sums, bias_grad.reshape(pieces_of, width), both, jnp.zeros((2, width), F32)]), 8)
+        values_send, small = lax.optimization_barrier((values_send, small))
+        arrived_values = lax.ppermute(values_send, "branch", [(0, 1), (1, 0)])
+        grad_inputs = (values_keep.astype(F32) + arrived_values.astype(F32)).astype(BF)
         own_vectors = lax.dynamic_slice_in_dim(small[8 + pieces_of :], 5 * branch, 5, 0)[None]
         bias_total = small[8 : 8 + pieces_of].reshape(-1)
 
-        up_sum = reduce_rows(mesh, up_part, chunk, npd, up_ranges, 5, F32).reshape(share, width)
-        down_sum = reduce_rows(mesh, down_part, chunk, npd, down_ranges, 6, F32, swaps).reshape(share, width)
+        up_sum, down_sum = [
+            total.reshape(share, width)
+            for total in reduce_rows(
+                mesh, [up_part, down_part], ((npd, chunk, up_ranges, (-1, -1), none), (npd, chunk, down_ranges, swaps, none)), 5,
+                BF, 6,
+            )
+        ]
         group_grads = []
         for g, side in enumerate((down_sum, up_sum)):
             at = g * group_rows + me * share + rows_at
             low, high = (0, k_of * width) if g == 0 else ((k_of + n_of) * width, (2 * k_of + n_of) * width)
             iso_rows = lax.dynamic_slice(kernel_grad, (g * blocks * width + lead[g], 0), (share, width))
-            outside = jnp.where(jnp.logical_and(at >= low, at < high)[:, None], side, 0.0)
+            outside = jnp.where(jnp.logical_and(at >= low, at < high)[:, None], side.astype(F32), 0.0)
             group_grads.append(jnp.where(insides[g][:, None], iso_rows, outside))
         grad_blocks = jnp.stack(group_grads)[None]
         return (

time: 965 us -> 803 us (0.83); the launches traced: 952 us -> 802 us
  Pallas kernels: 891 us -> 749 us
    pallas_call x1, Pallas kernels: 81.2 us -> 12.7 us  [total_over(): pl.pallas_call(functools.partial(total_body, depth), out_shape=jax.ShapeD...]
    pallas_call x8 -> x6, Pallas kernels: 501 us -> 433 us  [the longest x3 219 us: reduce_rows(): pl.pallas_call(functools.partial(reduce_body, depth, tuple(((*region, lag...]
  transfers between devices with their start and end apart: 2 -> 2, of which waited for: 0 -> 0; matrix products, arithmetic and copies ran while one was open for 2% -> 3% of each run, Pallas kernels for 26% -> 41%
where the time goes in v3:
time: 803 us; the launch traced here: 802 us
  Pallas kernels  749 us (93%)
  other arithmetic  25.5 us (3%)
  between operations  15.6 us (2%)
  local copies, waits for them, and re-layouts  9.14 us (1%)
    pallas_call x3, Pallas kernels, reduce_rows(): pl.pallas_call(functools.partial(reduce_body, depth, tuple(((*region, lag...  219 us
    pallas_call x3, Pallas kernels, gather_rows(): pl.pallas_call(functools.partial(gather_body, depth, regions), out_shape=...  214 us
    pallas_call x1, Pallas kernels, feed_call(): pl.pallas_call(functools.partial(feed_body, per_window, 512), out_shape=[...  114 us
    pallas_call x4, Pallas kernels, call(): pl.pallas_call(functools.partial(body, k, n, pitch, off), out_shape=outs,...  112 us
    pallas_call x2, Pallas kernels, iso_call(): pl.pallas_call(functools.partial(body, tall, pitch, blocks, steps), out_s...  76.9 us
  transfers between devices with their start and end apart: 2, of which 0 were waited for; matrix products, arithmetic and copies ran while one was open for 3% of the time, Pallas kernels for 41%

profile of v3, /device:TPU:19, one launch (start us, length us, event | category | flops | bytes accessed | tf_op | source)
XLA Modules:
  0.0 802.0 jit_solution(3323196139358529039)
XLA Ops:
  7.3 107.3 %shard_map.203 = (bf16[8280,512]{1,0:T(8,128)(2,1)}, bf16[8280,512]{1,0:T(8,128)(2,1)}) custom-call(bf16[2944,512]{1,0:T(8,128)(2,1)} %bitcast.90), custom_call_target="tpu_custom_call" | custom-call | flops 49999998976 | bytes 16777216 | tf_op jit(solution)/shard_map/pallas_call | solution.py:205
  114.6 18.6 %conditional.4 = ((f32[6,72,512]{2,1,0:T(8,128)}, bf16[6,72,512]{2,1,0:T(8,128)(2,1)}, bf16[480,8192]{1,0:T(8,128)(2,1)})) conditional(s32[]{:T(128)} %convert_element_type.48, (s32[1]{0:T(128)}, bf16[6,816,512]{2,1,0:T(8,128)(2,1)}, bf16[8280,512]{1,0:T(8,128)(2,1)}, f32[4,512]{1,0:T(4,128)S(1)}) %tuple.119, (s32[1]{0:T(128)}, ...), branch_computations={%region_0.1_spmd, %region_1.2_spmd} | conditional | bytes 8 | solution.py:1006
  114.6 18.6 %branch_0_fun.6 = (f32[6,72,512]{2,1,0:T(8,128)}, bf16[6,72,512]{2,1,0:T(8,128)(2,1)}, bf16[480,8192]{1,0:T(8,128)(2,1)}) custom-call(s32[1]{0:T(128)} %get-tuple-element.168.live, bf16[6,816,512]{2,1,0:T(8,128)(2,1)} %get-tuple-element.169.x, bf16[8280,512]{1,0:T(8,128)(2,1)} %get-tuple-element.170.weight, f32[4,512]{1,0:T(4,128)S(1)} %get-tuple-element.171.bias), custom_call_target="tpu_custom_call" | custom-call | tf_op jit(solution)/shard_map/cond/branch_0_fun/pallas_call | solution.py:1067
  133.2 48.1 %shard_map.204 = bf16[6912,512]{1,0:T(8,128)(2,1)} custom-call(bf16[432,512]{1,0:T(8,128)(2,1)} %bitcast.105), custom_call_target="tpu_custom_call" | custom-call | flops 49999998976 | bytes 16777216 | tf_op jit(solution)/shard_map/pallas_call | solution.py:205
  181.3 2.7 compare_reduce_fusion
  187.3 2.3 pad_maximum_fusion.refs_8_.refs_16_
  190.1 24.6 %shard_map.205 = bf16[96,72,512]{2,1,0:T(8,128)(2,1)} custom-call(s32[96]{0:T(128)} %select_reduce_fusion.order, s32[1]{0:T(128)} %bitcast.9.count, s32[8]{0:T(128)} %pad_add_fusion.shift, bf16[96,72,512]{2,1,0:T(8,128)(2,1)} %bitcast.53, bf16[96,72,512]{2,1,0:T(8,128)(2,1)} %bitcast.54, bf16[96,72,512]{2,1,0:T(8,128)(2,1)} %bitcast.55, ...), custom_call_target="tpu_custom_call" | custom-call | flops 9663676416 | bytes 4194304 | tf_op jit(solution)/shard_map/pallas_call | solution.py:788
  214.7 47.2 %shard_map.206 = f32[2,216,512]{2,1,0:T(8,128)S(1)} custom-call(bf16[6912,512]{1,0:T(8,128)(2,1)} %bitcast.85), custom_call_target="tpu_custom_call" | custom-call | flops 49999998976 | bytes 16777216 | tf_op jit(solution)/shard_map/pallas_call | solution.py:434
  262.0 22.3 %conditional.5 = (bf16[2448,512]{1,0:T(8,128)(2,1)}, bf16[2448,512]{1,0:T(8,128)(2,1)}) conditional(s32[]{:T(128)} %convert_element_type.48, (s32[1]{0:T(128)}, s32[1]{0:T(128)}, f32[6,72,512]{2,1,0:T(8,128)S(1)}, bf16[8280,512]{1,0:T(8,128)(2,1)}, bf16[6,816,512]{2,1,0:T(8,128)(2,1)}, /*index=5*/f32[1,512]{1,0:T(1,128)S(1)}, ...), branch_computations={%region_5.6_spmd, %region_6.7_spmd} | conditional | bytes 16 | solution.py:1006
  262.0 22.1 %branch_0_fun.7 = (bf16[3,816,512]{2,1,0:T(8,128)(2,1)}, bf16[3,816,512]{2,1,0:T(8,128)(2,1)}) custom-call(s32[1]{0:T(128)} %get-tuple-element.176.live, s32[1]{0:T(128)} %get-tuple-element.177.half, f32[6,72,512]{2,1,0:T(8,128)S(1)} %get-tuple-element.178.pre_iso, bf16[8280,512]{1,0:T(8,128)(2,1)} %get-tuple-element.179.weight, ...), custom_call_target="tpu_custom_call" | custom-call | tf_op jit(solution)/shard_map/cond/branch_0_fun/pallas_call | solution.py:1067
  284.3 114.2 %shard_map.207 = (bf16[2448,512]{1,0:T(8,128)(2,1)}, bf16[2448,512]{1,0:T(8,128)(2,1)S(1)}, bf16[2448,512]{1,0:T(8,128)(2,1)}, bf16[1024,512]{1,0:T(8,128)(2,1)}...) custom-call(s32[1]{0:T(128)S(6)} %copy.61.live, ...), custom_call_target="tpu_custom_call" | custom-call | flops 41070624768 | bytes 41943040 | tf_op jit(solution)/shard_map/pallas_call | solution.py:915
  398.5 47.4 %conditional.6 = (bf16[6,72,512]{2,1,0:T(8,128)(2,1)}, bf16[480,8192]{1,0:T(8,128)(2,1)}, bf16[8280,512]{1,0:T(8,128)(2,1)}, f32[1,512]{1,0:T(1,128)}, f32[3,512]{1,0:T(4,128)}) conditional(s32[]{:T(128)} %convert_element_type.48, (s32[1]{0:T(128)}, s32[1]{0:T(128)}, bf16[3,816,512]{2,1,0:T(8,128)(2,1)S(1)}, ...), branch_computations={%region_7.8_spmd.clone.clone, %region_8.9_spmd.clone.clone} | conditional | bytes 16424 | solution.py:1006
  398.8 44.2 %branch_0_fun.9 = (bf16[6,72,512]{2,1,0:T(8,128)(2,1)}, f32[8,512]{1,0:T(8,128)}, bf16[480,8192]{1,0:T(8,128)(2,1)}, bf16[8280,512]{1,0:T(8,128)(2,1)}) custom-call(s32[1]{0:T(128)} %get-tuple-element.402.live, s32[1]{0:T(128)} %get-tuple-element.403.half, bf16[3,816,512]{2,1,0:T(8,128)(2,1)S(1)} %get-tuple-element.404.grad_own, ...), custom_call_target="tpu_custom_call" | custom-call | tf_op jit(solution)/shard_map/cond/branch_0_fun/pallas_call | solution.py:1067
  443.0 1.3 slice.67
  444.3 1.3 slice.66
  446.0 58.5 %shard_map.208 = bf16[6912,512]{1,0:T(8,128)(2,1)} custom-call(bf16[432,512]{1,0:T(8,128)(2,1)} %bitcast.20.refs_0_), custom_call_target="tpu_custom_call" | custom-call | flops 49999998976 | bytes 16777216 | tf_op jit(solution)/shard_map/pallas_call | solution.py:205
  504.5 52.2 %shard_map.209 = (bf16[96,72,512]{2,1,0:T(8,128)(2,1)}, f32[4096,512]{1,0:T(8,128)}) custom-call(s32[96]{0:T(128)} %select_reduce_fusion.order, s32[1]{0:T(128)} %bitcast.9.count, s32[8]{0:T(128)} %pad_add_fusion.shift, bf16[96,72,512]{2,1,0:T(8,128)(2,1)} %bitcast.61, bf16[96,72,512]{2,1,0:T(8,128)(2,1)} %bitcast.62, bf16[96,72,512]{2,1,0:T(8,128)(2,1)} %bitcast.63, ...), custom_call_target="tpu_custom_call" | custom-call | flops 19327352832 | bytes 4194304 | tf_op jit(solution)/shard_map/pallas_call | solution.py:788
  558.2 47.6 %shard_map.210 = f32[2,216,512]{2,1,0:T(8,128)S(1)} custom-call(bf16[6912,512]{1,0:T(8,128)(2,1)} %bitcast.99), custom_call_target="tpu_custom_call" | custom-call | flops 49999998976 | bytes 16777216 | tf_op jit(solution)/shard_map/pallas_call | solution.py:434
  605.9 27.6 %conditional.7 = ((bf16[3,816,512]{2,1,0:T(8,128)(2,1)}, bf16[3,816,512]{2,1,0:T(8,128)(2,1)}, f32[1,512]{1,0:T(1,128)S(1)}, bf16[8280,512]{1,0:T(8,128)(2,1)})) conditional(s32[]{:T(128)} %convert_element_type.48, (s32[1]{0:T(128)}, s32[1]{0:T(128)}, f32[6,72,512]{2,1,0:T(8,128)S(1)}, f32[6,72,512]{2,1,0:T(8,128)S(1)}, ...), branch_computations={%region_12.13_spmd, %region_13.14_spmd} | conditional | bytes 8 | solution.py:1006
  606.1 27.2 %branch_0_fun.8 = (bf16[3,816,512]{2,1,0:T(8,128)(2,1)}, bf16[3,816,512]{2,1,0:T(8,128)(2,1)}, f32[1,512]{1,0:T(1,128)S(1)}, bf16[8280,512]{1,0:T(8,128)(2,1)}) custom-call(s32[1]{0:T(128)} %get-tuple-element.220.live, s32[1]{0:T(128)} %get-tuple-element.221.half, f32[6,72,512]{2,1,0:T(8,128)S(1)} %get-tuple-element.222.grad_act, ...), custom_call_target="tpu_custom_call" | custom-call | tf_op jit(solution)/shard_map/cond/branch_0_fun/pallas_call | solution.py:1067
  633.6 0.7 pad_maximum_fusion.1
  634.4 0.7 maximum_maximum_fusion.values
  635.1 12.7 %shard_map.211 = f32[24,512]{1,0:T(8,128)} custom-call(f32[24,512]{1,0:T(8,128)} %maximum_maximum_fusion.values), custom_call_target="tpu_custom_call" | custom-call | tf_op jit(solution)/shard_map/pallas_call | solution.py:991
  647.8 1.3 collective-permute-start
  649.1 124.5 %shard_map.212 = (bf16[8,184,512]{2,1,0:T(8,128)(2,1)}, bf16[8,184,512]{2,1,0:T(8,128)(2,1)}) custom-call(bf16[8280,512]{1,0:T(8,128)(2,1)} %get-tuple-element.303.refs_0_, bf16[8280,512]{1,0:T(8,128)(2,1)} %get-tuple-element.399.refs_1_), custom_call_target="tpu_custom_call" | custom-call | flops 49999998976 | bytes 16777216 | tf_op jit(solution)/shard_map/pallas_call | solution.py:434
  776.1 4.3 convert_element_type.59
  780.4 2.7 convert_element_type.60
  783.1 1.6 convert_element_type.58
  786.3 1.5 fusion.4
  787.8 3.3 maximum_bitcast_fusion
  791.1 2.2 fusion.5
  793.3 1.5 copy.62
  (72 shorter events, 8.7 us)
Async XLA Ops:
  7.2 598.7 %all-reduce.3.cloned.1.call-start = ((), (), s32[]{:S(2)}) async-start(), calls=%async_computation | async-start | bytes 10485760 | tf_op jit(solution)/shard_map/psum | solution.py:1129
  7.3 107.3 %copy-start.8 = (f32[1,4,512]{2,1,0:T(4,128)S(1)}, f32[1,4,512]{2,1,0:T(4,128)}, u32[]{:S(2)}) copy-start(f32[1,4,512]{2,1,0:T(4,128)} %param.24) | copy-start | bytes 24580
  133.2 53.1 %copy-start.1 = (bf16[1,2,1472,512]{3,2,1,0:T(8,128)(2,1)S(1)}, bf16[1,2,1472,512]{3,2,1,0:T(8,128)(2,1)}, u32[]{:S(2)}) copy-start(bf16[1,2,1472,512]{3,2,1,0:T(8,128)(2,1)} %param.22) | copy-start | bytes 9043972
  185.5 1.3 copy-start.11
  185.5 1.3 copy-start.13
  214.7 47.3 %copy-start.10 = (f32[1,512]{1,0:T(1,128)S(1)}, f32[1,512]{1,0:T(1,128)}, u32[]{:S(2)}) copy-start(f32[1,512]{1,0:T(1,128)} %param.23) | copy-start | bytes 6148
  504.5 53.0 %copy-start.16 = (f32[1,2048]{1,0:T(1,128)S(1)}, f32[1,2048]{1,0:T(1,128)}, u32[]{:S(2)}) copy-start(f32[1,2048]{1,0:T(1,128)} %get-tuple-element.298) | copy-start | bytes 24580
  558.2 47.7 %copy-start = (f32[6,72,512]{2,1,0:T(8,128)S(1)}, f32[6,72,512]{2,1,0:T(8,128)}, u32[]{:S(2)}) copy-start(f32[6,72,512]{2,1,0:T(8,128)} %get-tuple-element.292) | copy-start | bytes 2654212
  605.9 28.5 %copy-start.15 = (f32[8,512]{1,0:T(8,128)S(1)}, f32[8,512]{1,0:T(8,128)}, u32[]{:S(2)}) copy-start(f32[8,512]{1,0:T(8,128)} %get-tuple-element.297) | copy-start | bytes 49156
  647.8 143.3 %collective-permute-start = (bf16[3,816,512]{2,1,0:T(8,128)(2,1)}, bf16[3,816,512]{2,1,0:T(8,128)(2,1)S(1)}, u32[]{:S(2)}, u32[]{:S(2)}) collective-permute-start(bf16[3,816,512]{2,1,0:T(8,128)(2,1)} %get-tuple-element.301), channel_id=1, source_target_pairs={{0,16},{16,0},{1,17},{17,1},{2,18},{18,2},{3,19},{19,3},{4,20},{20... | collective-permute-start | bytes 7520264 | tf_op jit(solution)/shard_map/ppermute | solution.py:1160
  649.1 124.6 %copy-start.9 = (f32[24,512]{1,0:T(8,128)S(1)}, f32[24,512]{1,0:T(8,128)}, u32[]{:S(2)}) copy-start(f32[24,512]{1,0:T(8,128)} %shard_map.211) | copy-start | bytes 147460
  776.1 4.3 copy-start.4
  776.1 9.2 %slice-start = ((s8[8388608]{0:T(1024)(128)(4,1)}), s8[4194304]{0:T(1024)(128)(4,1)S(1)}, s32[]{:S(2)}) async-start(s8[8388608]{0:T(1024)(128)(4,1)} %bitcast.86), calls=%async_computation.1 | async-start | bytes 8388608
  780.4 2.7 copy-start.7
  780.4 5.0 slice-start.1
  783.1 2.7 copy-start.5
  783.1 3.2 copy-start.6
  783.1 3.2 copy-start.12
  783.1 3.2 copy-start.14
  787.8 3.3 copy-start.3
  791.1 2.2 copy-start.2
Sparse Core Ops, SparseCore 0:
  398.6 154.4 all-reduce.2

commit v4 on v3

--- a/solution.py
+++ b/solution.py
@@ -487,17 +487,6 @@
 VMEM = pl.BlockSpec(memory_space=pltpu.VMEM)
 
 
-def whole_call(body, out_shape, scratch, limit, cost=None):
-    return pl.pallas_call(
-        body,
-        out_shape=out_shape,
-        out_specs=jax.tree.map(lambda _: VMEM, out_shape),
-        scratch_shapes=scratch,
-        compiler_params=pltpu.CompilerParams(vmem_limit_bytes=limit * MIB),
-        cost_estimate=cost,
-    )
-
-
 LANES = 128
 
 
@@ -510,28 +499,36 @@
         ref[(*lead, p, rows, slice(None))] = values[:, p * LANES : (p + 1) * LANES]
 
 
-def down_body(k, n, pitch, off, live, x, weight, bias, pre, act, taps, spread):
-    slots, length, width = x.shape
-    many = slots * pitch
-    spread[:, length:, :] = jnp.zeros((spread.shape[0], spread.shape[1] - length, LANES), F32)
-
-    def window(w, carry):
-        set_panels(spread, (), slice(0, length), x[w].astype(F32))
-        for r in range(k):
-            taps[pl.ds(pl.multiple_of(w * pitch, 16), pitch), r * width : (r + 1) * width] = panels(
-                spread, (), pl.ds(r, pitch, stride=k)
-            ).astype(BF)
-        return carry
-
-    lax.fori_loop(0, slots, window, 0)
-    total = dot(taps[:many, : k * width], weight[off : off + k * width, :]) + bias[0:1, :]
-    tall = pre.shape[1]
-    for w in range(slots):
-        rows = fit(total[w * pitch : (w + 1) * pitch], tall)
-        pre[w] = rows
-        step = lax.broadcasted_iota(jnp.int32, rows.shape, 0)
-        flag = jnp.where(step == tall - 1, jnp.where(w < live[0], 1.0, 0.0), 0.0)
-        act[w] = jnp.where(step < n, jnp.tanh(rows), flag).astype(BF)
+def stride_of(k):
+    return k if k % 8 else k + 1
+
+
+def put_rows(ref, lead, k, values):
+    stride = stride_of(k)
+    if stride == k:
+        set_panels(ref, lead, slice(0, values.shape[0]), values)
+        return
+    for t in range(values.shape[0] // k):
+        set_panels(ref, lead, slice(t * stride, t * stride + k), values[t * k : (t + 1) * k])
+
+
+def get_rows(ref, lead, k, length):
+    stride = stride_of(k)
+    if stride == k:
+        return panels(ref, lead, slice(0, length))
+    return jnp.concatenate([panels(ref, lead, slice(t * stride, t * stride + k)) for t in range(length // k)], axis=0)
+
+
+def tap_rows(k, r, pitch):
+    return pl.ds(r, pitch, stride=stride_of(k))
+
+
+def at_window(w, pitch):
+    return pl.ds(pl.multiple_of(w * pitch, 16), pitch)
+
+
+def block_of(r, width, off=0):
+    return pl.ds(pl.multiple_of(off + r * width, 16), width)
 
 
 def fit(values, tall):
@@ -541,89 +538,210 @@
     return jnp.concatenate([values, jnp.zeros((tall - rows, values.shape[1]), values.dtype)], axis=0)
 
 
-def expand(k, n, pitch, off, iso_rows, weight, spread):
-    width = iso_rows.shape[1]
-    slots = spread.shape[0]
-
-    def tap(r, carry):
-        rows = dot(iso_rows[...], weight[pl.ds(pl.multiple_of(off + r * width, 16), width), :])
-        for w in range(slots):
-            set_panels(spread, (w,), pl.ds(r, pitch, stride=k), rows[w * pitch : (w + 1) * pitch])
-        return carry
-
-    lax.fori_loop(0, k, tap, 0)
-
-
 def iso_of(n, pitch, pre_iso, bias):
     rows = fit(jnp.tanh(pre_iso + bias[1:2, :]), pitch)
     step = lax.broadcasted_iota(jnp.int32, rows.shape, 0)
     return jnp.where(step < n, rows, 0.0)
 
 
-def up_body(k, n, pitch, off, live, half, pre_iso, weight, x, gain, bias, own, send, iso_rows, spread):
-    slots, length, width = x.shape
-    for w in range(slots):
+def set_iso_rows(n, pitch, live, pre_iso, bias, iso_rows):
+    for w in range(pre_iso.shape[0]):
         iso = iso_of(n, pitch, pre_iso[w], bias)
         iso_rows[w * pitch : (w + 1) * pitch, :] = jnp.where(w < live[0], iso, 0.0).astype(BF)
-    expand(k, n, pitch, off, iso_rows, weight, spread)
-
-    def window(m, carry):
-        for out, w in ((send, 2 * m + 1 - half[0]), (own, 2 * m + half[0])):
-            values = panels(spread, (w,), slice(0, length)) + bias[2:3, :] + x[w].astype(F32)
+
+
+def each_of(count, what):
+    def step(at, carry):
+        what(at)
+        return carry
+
+    lax.fori_loop(0, count, step, 0)
+
+
+def down_body(k, n, pitch, off, live, x, weight, bias, pre, act, taps, x_held, w_held, t_held, total, spread, x_sem, w_sem, t_sem):
+    slots, length, width = x.shape
+
+    def window(w):
+        return pltpu.make_async_copy(x.at[w], x_held.at[w], x_sem.at[w])
+
+    def block(r):
+        return pltpu.make_async_copy(weight.at[block_of(r, width, off), :], w_held.at[r], w_sem.at[r])
+
+    def out(w):
+        rows = at_window(w, pitch)
+        return pltpu.make_async_copy(t_held.at[:, rows, :], taps.at[pl.ds(0, k), rows, :], t_sem.at[w])
+
+    each_of(slots, lambda w: window(w).start())
+    each_of(k, lambda r: block(r).start())
+    used = n * stride_of(k)
+    spread[:, used:, :] = jnp.zeros((spread.shape[0], spread.shape[1] - used, LANES), F32)
+
+    def lay(w):
+        window(w).wait()
+        put_rows(spread, (), k, x_held[w].astype(F32))
+        for r in range(k):
+            t_held[r, at_window(w, pitch), :] = panels(spread, (), tap_rows(k, r, pitch)).astype(BF)
+        out(w).start()
+
+    each_of(slots, lay)
+    total[...] = jnp.zeros_like(total)
+
+    def tap(r):
+        block(r).wait()
+        total[...] += dot(t_held[r], w_held[r])
+
+    each_of(k, tap)
+    tall = pre.shape[1]
+    for w in range(slots):
+        rows = fit(total[w * pitch : (w + 1) * pitch, :] + bias[0:1, :], tall)
+        pre[w] = rows
+        step = lax.broadcasted_iota(jnp.int32, rows.shape, 0)
+        flag = jnp.where(step == tall - 1, jnp.where(w < live[0], 1.0, 0.0), 0.0)
+        act[w] = jnp.where(step < n, jnp.tanh(rows), flag).astype(BF)
+    each_of(slots, lambda w: out(w).wait())
+
+
+def up_body(k, n, pitch, off, live, half, pre_iso, weight, x, gain, bias, own, send, x_held, w_held, o_held, iso_rows, spread,
+            x_sem, w_sem, o_sem):
+    slots, length, width = x.shape
+
+    def window(w):
+        return pltpu.make_async_copy(x.at[w], x_held.at[w], x_sem.at[w])
+
+    def block(r):
+        return pltpu.make_async_copy(weight.at[block_of(r, width, off), :], w_held.at[r], w_sem.at[r])
+
+    def out(which, m):
+        return pltpu.make_async_copy(o_held.at[which, m], (send, own)[which].at[m], o_sem.at[which, m])
+
+    each_of(k, lambda r: block(r).start())
+    each_of(slots, lambda w: window(w).start())
+    set_iso_rows(n, pitch, live, pre_iso, bias, iso_rows)
+
+    def tap(r):
+        block(r).wait()
+        rows = dot(iso_rows[...], w_held[r])
+        for w in range(slots):
+            set_panels(spread, (w,), tap_rows(k, r, pitch), rows[w * pitch : (w + 1) * pitch])
+
+    each_of(k, tap)
+
+    def finish(m):
+        for which, w in enumerate((2 * m + 1 - half[0], 2 * m + half[0])):
+            window(w).wait()
+            values = get_rows(spread, (w,), k, length) + bias[2:3, :] + x_held[w].astype(F32)
             xhat, _ = normalise(values)
-            out[m] = (xhat * gain[0:1, :] + bias[3:4, :]).astype(BF)
-        return carry
-
-    lax.fori_loop(0, slots // 2, window, 0)
-
-
-def up_back_body(k, n, pitch, off, live, half, grad_own, grad_arrived, pre_iso, weight, x, gain, bias, grad_iso, vectors, grad_taps, part, iso_rows, spread):
-    slots, length, width = x.shape
-    for w in range(slots):
-        iso = iso_of(n, pitch, pre_iso[w], bias)
-        iso_rows[w * pitch : (w + 1) * pitch, :] = jnp.where(w < live[0], iso, 0.0).astype(BF)
-    expand(k, n, pitch, off, iso_rows, weight, spread)
+            o_held[which, m] = (xhat * gain[0:1, :] + bias[3:4, :]).astype(BF)
+            out(which, m).start()
+
+    each_of(slots // 2, finish)
+    for which in range(2):
+        each_of(slots // 2, lambda m, which=which: out(which, m).wait())
+
+
+def up_back_body(k, n, pitch, off, live, half, grad_own, grad_arrived, pre_iso, weight, taps, gain, bias, grad_iso, vectors,
+                 grad_taps, part, g_held, w_held, t_held, q_held, p_held, iso_rows, total, spread, g_sem, w_sem, t_sem, q_sem, p_sem):
+    (half_slots, length, width), slots = grad_own.shape, pre_iso.shape[0]
+    many = slots * pitch
+
+    def window(which, m):
+        return pltpu.make_async_copy((grad_own, grad_arrived)[which].at[m], g_held.at[which, m], g_sem.at[which, m])
+
+    def block(r):
+        return pltpu.make_async_copy(weight.at[block_of(r, width, off), :], w_held.at[r], w_sem.at[r])
+
+    def tap_in(r):
+        return pltpu.make_async_copy(taps.at[r, pl.ds(0, many), :], t_held.at[r], t_sem.at[r])
+
+    def tap_out(r):
+        return pltpu.make_async_copy(q_held.at[r], grad_taps.at[r, pl.ds(0, many), :], q_sem.at[r])
+
+    def part_out(r):
+        return pltpu.make_async_copy(p_held.at[r % 2], part.at[block_of(r, width, off), :], p_sem.at[r % 2])
+
+    for which in range(2):
+        each_of(half_slots, lambda m, which=which: window(which, m).start())
+
+    def fetch(r):
+        block(r).start()
+        tap_in(r).start()
+
+    each_of(k, fetch)
+    set_iso_rows(n, pitch, live, pre_iso, bias, iso_rows)
+    used = n * stride_of(k)
+    spread[:, used:, :] = jnp.zeros((spread.shape[0], spread.shape[1] - used, LANES), F32)
+
+    def lay(m):
+        for which, w in enumerate((2 * m + half[0], 2 * m + 1 - half[0])):
+            window(which, m).wait()
+            put_rows(spread, (), k, g_held[which, m].astype(F32))
+            for r in range(k):
+                q_held[r, at_window(w, pitch), :] = panels(spread, (), tap_rows(k, r, pitch)).astype(BF)
+
+    each_of(half_slots, lay)
     vectors[...] = jnp.zeros_like(vectors)
-
-    def window(m, carry):
-        for grad, w in ((grad_own, 2 * m + half[0]), (grad_arrived, 2 * m + 1 - half[0])):
-            values = panels(spread, (w,), slice(0, length)) + bias[2:3, :] + x[w].astype(F32)
-            xhat, rho = normalise(values)
-            q = grad[m].astype(F32)
-            residual = norm_back(q * gain[0:1, :], xhat, rho)
-            set_panels(spread, (w,), slice(0, length), residual)
-            vectors[0:1, :] += column_sum(q * xhat)
-            vectors[3:4, :] += column_sum(residual.astype(BF).astype(F32))
-            vectors[4:5, :] += column_sum(q)
-        return carry
-
-    lax.fori_loop(0, slots // 2, window, 0)
-
-    def tap(w, carry):
-        for r in range(k):
-            grad_taps[pl.ds(pl.multiple_of(w * pitch, 16), pitch), r * width : (r + 1) * width] = panels(
-                spread, (w,), pl.ds(r, pitch, stride=k)
-            ).astype(BF)
-        return carry
-
-    lax.fori_loop(0, slots, tap, 0)
-    total = jnp.zeros((slots * pitch, width), F32)
-    for r in range(k):
-        rows = grad_taps[: slots * pitch, r * width : (r + 1) * width]
-        total += dot_bt(rows, weight[off + r * width : off + (r + 1) * width, :])
-        part[off + r * width : off + (r + 1) * width, :] = dot_at(iso_rows[...], rows).astype(BF)
+    total[...] = jnp.zeros_like(total)
+
+    def tap(r):
+        block(r).wait()
+        tap_in(r).wait()
+        values = dot(iso_rows[...], w_held[r]) + bias[2:3, :] + t_held[r].astype(F32)
+        xhat, rho = normalise(values)
+        q = q_held[r].astype(F32)
+        residual = norm_back(q * gain[0:1, :], xhat, rho).astype(BF)
+        q_held[r] = residual
+        tap_out(r).start()
+        vectors[0:1, :] += column_sum(q * xhat)
+        vectors[3:4, :] += column_sum(residual.astype(F32))
+        vectors[4:5, :] += column_sum(q)
+        total[...] += dot_bt(residual, w_held[r])
+
+        @pl.when(r >= 2)
+        def _():
+            part_out(r - 2).wait()
+
+        p_held[r % 2] = dot_at(iso_rows[...], residual).astype(BF)
+        part_out(r).start()
+
+    each_of(k, tap)
     tall = grad_iso.shape[1]
     for w in range(slots):
         iso = iso_of(n, pitch, pre_iso[w], bias)
         slope = jnp.where(lax.broadcasted_iota(jnp.int32, iso.shape, 0) < n, 1.0 - iso * iso, 0.0)
-        back = total[w * pitch : (w + 1) * pitch] * slope
-        back = jnp.where(w < live[0], back, 0.0).astype(BF)
+        back = jnp.where(w < live[0], total[w * pitch : (w + 1) * pitch, :] * slope, 0.0).astype(BF)
         vectors[2:3, :] += column_sum(back.astype(F32))
         grad_iso[w] = fit(back.astype(F32), tall).astype(BF)
-
-
-def down_back_body(k, n, pitch, off, live, half, grad_act, pre, grad_taps, taps, weight, keep, send, vector, part, rows, spread):
-    slots, (length, width) = pre.shape[0], keep.shape[1:]
+    part_out(k - 2).wait()
+    part_out(k - 1).wait()
+    each_of(k, lambda r: tap_out(r).wait())
+
+
+def down_back_body(k, n, pitch, off, live, half, grad_act, pre, grad_taps, taps, weight, keep, send, vector, part, g_held, w_held,
+                   t_held, p_held, o_held, rows, spread, g_sem, w_sem, t_sem, p_sem, o_sem):
+    slots, (half_slots, length, width) = pre.shape[0], keep.shape
+    many = slots * pitch
+
+    def block(r):
+        return pltpu.make_async_copy(weight.at[block_of(r, width, off), :], w_held.at[r], w_sem.at[r])
+
+    def grad_in(r):
+        return pltpu.make_async_copy(grad_taps.at[r, pl.ds(0, many), :], g_held.at[r], g_sem.at[r])
+
+    def tap_in(r):
+        return pltpu.make_async_copy(taps.at[r, pl.ds(0, many), :], t_held.at[r], t_sem.at[r])
+
+    def part_out(r):
+        return pltpu.make_async_copy(p_held.at[r % 2], part.at[block_of(r, width, off), :], p_sem.at[r % 2])
+
+    def out(which, m):
+        return pltpu.make_async_copy(o_held.at[which, m], (send, keep)[which].at[m], o_sem.at[which, m])
+
+    def fetch(r):
+        block(r).start()
+        grad_in(r).start()
+        tap_in(r).start()
+
+    each_of(k, fetch)
     vector[...] = jnp.zeros_like(vector)
     for w in range(slots):
         act = jnp.tanh(fit(pre[w], pitch))
@@ -632,21 +750,34 @@
         back = jnp.where(jnp.logical_and(step < n, w < live[0]), back, 0.0).astype(BF)
         vector[...] += column_sum(back.astype(F32))
         rows[w * pitch : (w + 1) * pitch, :] = back
-    for r in range(k):
-        back = dot_bt(rows[...], weight[off + r * width : off + (r + 1) * width, :])
-        back += grad_taps[: slots * pitch, r * width : (r + 1) * width].astype(F32)
+
+    def tap(r):
+        block(r).wait()
+        grad_in(r).wait()
+        tap_in(r).wait()
+        back = dot_bt(rows[...], w_held[r]) + g_held[r].astype(F32)
         for w in range(slots):
-            set_panels(spread, (w,), pl.ds(r, pitch, stride=k), back[w * pitch : (w + 1) * pitch])
-        part[off + r * width : off + (r + 1) * width, :] = dot_at(
-            taps[: slots * pitch, r * width : (r + 1) * width], rows[...]
-        ).astype(BF)
-
-    def window(m, carry):
-        send[m] = panels(spread, (2 * m + 1 - half[0],), slice(0, length)).astype(BF)
-        keep[m] = panels(spread, (2 * m + half[0],), slice(0, length)).astype(BF)
-        return carry
-
-    lax.fori_loop(0, slots // 2, window, 0)
+            set_panels(spread, (w,), tap_rows(k, r, pitch), back[w * pitch : (w + 1) * pitch])
+
+        @pl.when(r >= 2)
+        def _():
+            part_out(r - 2).wait()
+
+        p_held[r % 2] = dot_at(t_held[r], rows[...]).astype(BF)
+        part_out(r).start()
+
+    each_of(k, tap)
+
+    def finish(m):
+        for which, w in enumerate((2 * m + 1 - half[0], 2 * m + half[0])):
+            o_held[which, m] = get_rows(spread, (w,), k, length).astype(BF)
+            out(which, m).start()
+
+    each_of(half_slots, finish)
+    part_out(k - 2).wait()
+    part_out(k - 1).wait()
+    for which in range(2):
+        each_of(half_slots, lambda m, which=which: out(which, m).wait())
 
 
 SUBLANES = 8
@@ -1057,32 +1188,38 @@
             return jax.ShapeDtypeStruct((slots, tall, width), kind)
 
         full = jax.ShapeDtypeStruct((slots // 2, length, width), BF)
-        taps_shape = jax.ShapeDtypeStruct((most, reach * width), BF)
+        taps_shape = jax.ShapeDtypeStruct((reach, most, width), BF)
         part_shape = jax.ShapeDtypeStruct((max(r[1] - r[0] for r in down_ranges) * chunk, width), BF)
         up_part_shape = jax.ShapeDtypeStruct((max(r[1] - r[0] for r in up_ranges) * chunk, width), BF)
         sm = pl.BlockSpec(memory_space=pltpu.SMEM)
 
-        def call(body, index, off, outs, scratch, scalars, *operands):
+        def call(body, index, off, outs, held, kinds, *operands):
             k, n, pitch = SCALES[index], taps_of[index], pitches[index]
+            spec = {"s": sm, "v": VMEM, "h": ANY}
+            scratch = {
+                "w": pltpu.VMEM((k, width, width), BF), "t": pltpu.VMEM((k, slots * pitch, width), BF),
+                "x": pltpu.VMEM((slots, length, width), BF), "o": pltpu.VMEM((2, slots // 2, length, width), BF),
+                "p": pltpu.VMEM((2, width, width), BF), "i": pltpu.VMEM((slots * pitch, width), BF),
+                "f": pltpu.VMEM((slots * pitch, width), F32),
+                "1": pltpu.VMEM((width // LANES, pitch * stride_of(k), LANES), F32),
+                "6": pltpu.VMEM((slots, width // LANES, pitch * stride_of(k), LANES), F32),
+                "K": pltpu.SemaphoreType.DMA((k,)), "S": pltpu.SemaphoreType.DMA((slots,)),
+                "H": pltpu.SemaphoreType.DMA((2, slots // 2)), "P": pltpu.SemaphoreType.DMA((2,)),
+            }
             return pl.pallas_call(
                 functools.partial(body, k, n, pitch, off),
                 out_shape=outs,
-                in_specs=[sm] * scalars + [VMEM] * (len(operands) - scalars),
-                out_specs=jax.tree.map(lambda _: VMEM, outs),
-                scratch_shapes=scratch,
+                in_specs=[spec[s] for s in kinds[: len(operands)]],
+                out_specs=tuple(spec[s] for s in kinds[len(operands) :]),
+                scratch_shapes=[scratch[s] for s in held],
                 compiler_params=pltpu.CompilerParams(vmem_limit_bytes=60 * MIB),
+                cost_estimate=pl.CostEstimate(flops=2 * 10**10, bytes_accessed=2**24, transcendentals=0),
             )(*operands)
-
-        def rows_scratch(index):
-            return pltpu.VMEM((slots * pitches[index], width), BF)
-
-        def spread_scratch(index, count_of=slots):
-            return pltpu.VMEM((count_of, width // LANES, pitches[index] * SCALES[index], LANES), F32)
 
         def down_of(index):
             def run(*operands):
-                return call(down_body, index, 0, (windows_shape(F32), windows_shape(BF), taps_shape),
-                            [pltpu.VMEM((width // LANES, pitches[index] * SCALES[index], LANES), F32)], 1, *operands)
+                return call(down_body, index, 0, (windows_shape(F32), windows_shape(BF), taps_shape), "xwtf1SKS", "shhvvvh",
+                            *operands)
             return run
 
         pre, act, taps = branch_index_pair(branch, down_of(0), down_of(1), live, inputs, down_weight, bias)
@@ -1118,7 +1255,7 @@
 
         def up_of(index):
             def run(*operands):
-                return call(up_body, index, up_offs[index], (full, full), [rows_scratch(index), spread_scratch(index)], 2, *operands)
+                return call(up_body, index, up_offs[index], (full, full), "xwoi6SKH", "ssvhhvvhh", *operands)
             return run
 
         bo_own, bo_send = branch_index_pair(branch, up_of(0), up_of(1), live, half, pre_iso, up_weight, inputs, gain, bias)
@@ -1132,11 +1269,11 @@
             def run(*operands):
                 return call(up_back_body, index, up_offs[index],
                             (windows_shape(BF), jax.ShapeDtypeStruct((8, width), F32), taps_shape, up_part_shape),
-                            [rows_scratch(index), spread_scratch(index)], 2, *operands)
+                            "owttpif1HKKKP", "sshhvhhvvvvhh", *operands)
             return run
 
         grad_iso, vectors, grad_taps, up_part = branch_index_pair(
-            branch, up_back_of(0), up_back_of(1), live, half, grad_own.reshape(full.shape), arrived.reshape(full.shape), pre_iso, up_weight, inputs, gain, bias
+            branch, up_back_of(0), up_back_of(1), live, half, grad_own.reshape(full.shape), arrived.reshape(full.shape), pre_iso, up_weight, taps, gain, bias
         )
         grads = spread_windows(grad_iso, 4)
         back_terms, kernel_grad = iso_call(True, order, count, shift, iso_weight, acts, grads)
@@ -1146,7 +1283,7 @@
         def down_back_of(index):
             def run(*operands):
                 return call(down_back_body, index, 0, (full, full, jax.ShapeDtypeStruct((1, width), F32), part_shape),
-                            [rows_scratch(index), spread_scratch(index)], 2, *operands)
+                            "twtpoi6KKKPH", "ssvvhhhhhvh", *operands)
             return run
 
         values_keep, values_send, down_vector, down_part = branch_index_pair(

time: 803 us -> 771 us (0.960); the launches traced: 802 us -> 758 us
  Pallas kernels: 749 us -> 697 us
    pallas_call x4, Pallas kernels: 112 us -> 76.3 us  [call(): pl.pallas_call(functools.partial(body, k, n, pitch, off), out_shape=outs,...]
    pallas_call x2, Pallas kernels: 76.9 us -> 65.3 us  [iso_call(): pl.pallas_call(functools.partial(body, tall, pitch, blocks, steps), out_s...]
  transfers between devices with their start and end apart: 2 -> 2, of which waited for: 0 -> 0; matrix products, arithmetic and copies ran while one was open for 3% -> 3% of each run, Pallas kernels for 41% -> 40%
where the time goes in v4:
time: 771 us; the launch traced here: 758 us
  Pallas kernels  697 us (90%)
  other arithmetic  27.4 us (4%)
  between operations  15.4 us (2%)
  local copies, waits for them, and re-layouts  9.14 us (1%)
  loops' own time  8.54 us (1%)
    pallas_call x3, Pallas kernels, reduce_rows(): pl.pallas_call(functools.partial(reduce_body, depth, tuple(((*region, lag...  219 us
    pallas_call x3, Pallas kernels, gather_rows(): pl.pallas_call(functools.partial(gather_body, depth, regions), out_shape=...  209 us
    pallas_call x1, Pallas kernels, feed_call(): pl.pallas_call(functools.partial(feed_body, per_window, 512), out_shape=[...  114 us
    pallas_call x4, Pallas kernels, call(): pl.pallas_call(functools.partial(body, k, n, pitch, off), out_shape=outs,...  76.3 us
    pallas_call x2, Pallas kernels, iso_call(): pl.pallas_call(functools.partial(body, tall, pitch, blocks, steps), out_s...  65.3 us
  transfers between devices with their start and end apart: 2, of which 0 were waited for; matrix products, arithmetic and copies ran while one was open for 3% of the time, Pallas kernels for 40%

profile of v4, /device:TPU:19, one launch (start us, length us, event | category | flops | bytes accessed | tf_op | source)
XLA Modules:
  0.0 758.5 jit_solution(6079352480268227992)
XLA Ops:
  7.3 107.3 %shard_map.203 = (bf16[8280,512]{1,0:T(8,128)(2,1)}, bf16[8280,512]{1,0:T(8,128)(2,1)}) custom-call(bf16[2944,512]{1,0:T(8,128)(2,1)} %bitcast.80), custom_call_target="tpu_custom_call" | custom-call | flops 49999998976 | bytes 16777216 | tf_op jit(solution)/shard_map/pallas_call | solution.py:205
  114.6 11.7 %conditional.4 = ((f32[6,72,512]{2,1,0:T(8,128)}, bf16[6,72,512]{2,1,0:T(8,128)(2,1)S(1)}, bf16[16,480,512]{2,1,0:T(8,128)(2,1)})) conditional(s32[]{:T(128)} %convert_element_type.48, (s32[1]{0:T(128)}, bf16[6,816,512]{2,1,0:T(8,128)(2,1)}, bf16[8280,512]{1,0:T(8,128)(2,1)}, f32[4,512]{1,0:T(4,128)S(1)}) %tuple.107, (s32[1]{0:T(128)}, ...), branch_computations={%region_0.1_spmd, %region_1.2_spmd} | conditional | flops 20000000000 | bytes 16777224 | solution.py:1137
  114.6 11.7 %branch_0_fun.6 = (f32[6,72,512]{2,1,0:T(8,128)}, bf16[6,72,512]{2,1,0:T(8,128)(2,1)S(1)}, bf16[16,480,512]{2,1,0:T(8,128)(2,1)}) custom-call(s32[1]{0:T(128)} %get-tuple-element.168.live, bf16[6,816,512]{2,1,0:T(8,128)(2,1)} %get-tuple-element.169.x, bf16[8280,512]{1,0:T(8,128)(2,1)} %get-tuple-element.170.weight, f32[4,512]{1,0:T(4,128)S(1)} %get-tuple-element.171.bias), custom_call_target="tpu_custom_call" | custom-call | flops 20000000000 | bytes 16777216 | tf_op jit(solution)/shard_map/cond/branch_0_fun/pallas_call | solution.py:1209
  126.4 48.5 %shard_map.204 = bf16[6912,512]{1,0:T(8,128)(2,1)} custom-call(bf16[432,512]{1,0:T(8,128)(2,1)S(1)} %bitcast.103), custom_call_target="tpu_custom_call" | custom-call | flops 49999998976 | bytes 16777216 | tf_op jit(solution)/shard_map/pallas_call | solution.py:205
  174.8 2.7 compare_reduce_fusion
  180.7 2.3 pad_maximum_fusion.refs_8_.refs_16_
  183.7 21.0 %shard_map.205 = bf16[96,72,512]{2,1,0:T(8,128)(2,1)} custom-call(s32[96]{0:T(128)} %select_reduce_fusion.order, s32[1]{0:T(128)} %bitcast.9.count, s32[8]{0:T(128)} %pad_add_fusion.shift, bf16[96,72,512]{2,1,0:T(8,128)(2,1)} %bitcast.53, bf16[96,72,512]{2,1,0:T(8,128)(2,1)} %bitcast.54, bf16[96,72,512]{2,1,0:T(8,128)(2,1)} %bitcast.55, ...), custom_call_target="tpu_custom_call" | custom-call | flops 9663676416 | bytes 4194304 | tf_op jit(solution)/shard_map/pallas_call | solution.py:919
  204.7 48.2 %shard_map.206 = f32[2,216,512]{2,1,0:T(8,128)} custom-call(bf16[6912,512]{1,0:T(8,128)(2,1)} %bitcast.77), custom_call_target="tpu_custom_call" | custom-call | flops 49999998976 | bytes 16777216 | tf_op jit(solution)/shard_map/pallas_call | solution.py:434
  252.8 13.8 %conditional.5 = (bf16[2448,512]{1,0:T(8,128)(2,1)}, bf16[2448,512]{1,0:T(8,128)(2,1)}) conditional(s32[]{:T(128)} %convert_element_type.48, (s32[1]{0:T(128)}, s32[1]{0:T(128)}, f32[6,72,512]{2,1,0:T(8,128)}, bf16[8280,512]{1,0:T(8,128)(2,1)}, bf16[6,816,512]{2,1,0:T(8,128)(2,1)}, /*index=5*/f32[1,512]{1,0:T(1,128)S(1)}, ...), branch_computations={%region_5.6_spmd, %region_6.7_spmd} | conditional | flops 20000000000 | bytes 16777232 | solution.py:1137
  252.8 13.8 %branch_0_fun.7 = (bf16[3,816,512]{2,1,0:T(8,128)(2,1)}, bf16[3,816,512]{2,1,0:T(8,128)(2,1)}) custom-call(s32[1]{0:T(128)} %get-tuple-element.176.live, s32[1]{0:T(128)} %get-tuple-element.177.half, f32[6,72,512]{2,1,0:T(8,128)} %get-tuple-element.178.pre_iso, bf16[8280,512]{1,0:T(8,128)(2,1)} %get-tuple-element.179.weight, ...), custom_call_target="tpu_custom_call" | custom-call | flops 20000000000 | bytes 16777216 | tf_op jit(solution)/shard_map/cond/branch_0_fun/pallas_call | solution.py:1209
  266.7 114.2 %shard_map.207 = (bf16[2448,512]{1,0:T(8,128)(2,1)}, bf16[2448,512]{1,0:T(8,128)(2,1)S(1)}, bf16[2448,512]{1,0:T(8,128)(2,1)}, bf16[1024,512]{1,0:T(8,128)(2,1)}...) custom-call(s32[1]{0:T(128)S(6)} %copy.61.live, ...), custom_call_target="tpu_custom_call" | custom-call | flops 41070624768 | bytes 41943040 | tf_op jit(solution)/shard_map/pallas_call | solution.py:1046
  380.9 43.1 %conditional.6 = (bf16[6,72,512]{2,1,0:T(8,128)(2,1)S(1)}, bf16[16,480,512]{2,1,0:T(8,128)(2,1)}, bf16[8280,512]{1,0:T(8,128)(2,1)}, f32[1,512]{1,0:T(1,128)}, f32[3,512]{1,0:T(4,128)}) conditional(s32[]{:T(128)} %convert_element_type.48, (s32[1]{0:T(128)}, s32[1]{0:T(128)}, bf16[3,816,512]{2,1,0:T(8,128)(2,1)S(1)}, ...), branch_computations={%region_7.8_spmd.clone.clone, %region_8.9_spmd.clone.clone} | conditional | flops 20000000000 | bytes 16793640 | solution.py:1137
  380.9 32.0 %branch_0_fun.9 = (bf16[6,72,512]{2,1,0:T(8,128)(2,1)S(1)}, f32[8,512]{1,0:T(8,128)}, bf16[16,480,512]{2,1,0:T(8,128)(2,1)}, bf16[8280,512]{1,0:T(8,128)(2,1)}) custom-call(s32[1]{0:T(128)} %get-tuple-element.402.live, s32[1]{0:T(128)} %get-tuple-element.403.half, bf16[3,816,512]{2,1,0:T(8,128)(2,1)S(1)} %get-tuple-element.404.grad_own, ...), custom_call_target="tpu_custom_call" | custom-call | flops 20000000000 | bytes 16777216 | tf_op jit(solution)/shard_map/cond/branch_0_fun/pallas_call | solution.py:1209
  413.0 1.3 slice.67
  414.3 1.3 slice.66
  424.1 52.9 %shard_map.208 = bf16[6912,512]{1,0:T(8,128)(2,1)} custom-call(bf16[432,512]{1,0:T(8,128)(2,1)S(1)} %bitcast.102), custom_call_target="tpu_custom_call" | custom-call | flops 49999998976 | bytes 16777216 | tf_op jit(solution)/shard_map/pallas_call | solution.py:205
  477.0 44.4 %shard_map.209 = (bf16[96,72,512]{2,1,0:T(8,128)(2,1)}, f32[4096,512]{1,0:T(8,128)}) custom-call(s32[96]{0:T(128)} %select_reduce_fusion.order, s32[1]{0:T(128)} %bitcast.9.count, s32[8]{0:T(128)} %pad_add_fusion.shift, bf16[96,72,512]{2,1,0:T(8,128)(2,1)} %bitcast.61, bf16[96,72,512]{2,1,0:T(8,128)(2,1)} %bitcast.62, bf16[96,72,512]{2,1,0:T(8,128)(2,1)} %bitcast.63, ...), custom_call_target="tpu_custom_call" | custom-call | flops 19327352832 | bytes 4194304 | tf_op jit(solution)/shard_map/pallas_call | solution.py:919
  522.9 46.6 %shard_map.210 = f32[2,216,512]{2,1,0:T(8,128)S(1)} custom-call(bf16[6912,512]{1,0:T(8,128)(2,1)} %bitcast.83), custom_call_target="tpu_custom_call" | custom-call | flops 49999998976 | bytes 16777216 | tf_op jit(solution)/shard_map/pallas_call | solution.py:434
  569.5 18.8 %conditional.7 = ((bf16[3,816,512]{2,1,0:T(8,128)(2,1)}, bf16[3,816,512]{2,1,0:T(8,128)(2,1)}, f32[1,512]{1,0:T(1,128)S(1)}, bf16[8280,512]{1,0:T(8,128)(2,1)})) conditional(s32[]{:T(128)} %convert_element_type.48, (s32[1]{0:T(128)}, s32[1]{0:T(128)}, f32[6,72,512]{2,1,0:T(8,128)S(1)}, f32[6,72,512]{2,1,0:T(8,128)S(1)}, ...), branch_computations={%region_12.13_spmd, %region_13.14_spmd} | conditional | flops 20000000000 | bytes 16777224 | solution.py:1137
  569.6 18.7 %branch_0_fun.8 = (bf16[3,816,512]{2,1,0:T(8,128)(2,1)}, bf16[3,816,512]{2,1,0:T(8,128)(2,1)}, f32[1,512]{1,0:T(1,128)S(1)}, bf16[8280,512]{1,0:T(8,128)(2,1)}) custom-call(s32[1]{0:T(128)} %get-tuple-element.220.live, s32[1]{0:T(128)} %get-tuple-element.221.half, f32[6,72,512]{2,1,0:T(8,128)S(1)} %get-tuple-element.222.grad_act, ...), custom_call_target="tpu_custom_call" | custom-call | flops 20000000000 | bytes 16777216 | tf_op jit(solution)/shard_map/cond/branch_0_fun/pallas_call | solution.py:1209
  588.3 0.7 pad_maximum_fusion.1
  589.1 0.7 maximum_maximum_fusion.values
  589.8 12.9 %shard_map.211 = f32[24,512]{1,0:T(8,128)} custom-call(f32[24,512]{1,0:T(8,128)} %maximum_maximum_fusion.values), custom_call_target="tpu_custom_call" | custom-call | tf_op jit(solution)/shard_map/pallas_call | solution.py:1122
  602.7 1.3 collective-permute-start
  604.0 124.5 %shard_map.212 = (bf16[8,184,512]{2,1,0:T(8,128)(2,1)}, bf16[8,184,512]{2,1,0:T(8,128)(2,1)}) custom-call(bf16[8280,512]{1,0:T(8,128)(2,1)} %get-tuple-element.303.refs_0_, bf16[8280,512]{1,0:T(8,128)(2,1)} %get-tuple-element.399.refs_1_), custom_call_target="tpu_custom_call" | custom-call | flops 49999998976 | bytes 16777216 | tf_op jit(solution)/shard_map/pallas_call | solution.py:434
  730.9 4.3 convert_element_type.59
  735.2 2.7 convert_element_type.60
  738.0 1.6 convert_element_type.58
  741.1 1.5 fusion.4
  742.6 3.3 maximum_bitcast_fusion
  745.9 4.0 fusion.5
  749.9 1.5 copy.62
  (70 shorter events, 8.7 us)
Async XLA Ops:
  7.2 562.3 %all-reduce.3.cloned.1.call-start = ((), (), s32[]{:S(2)}) async-start(), calls=%async_computation | async-start | bytes 10485760 | tf_op jit(solution)/shard_map/psum | solution.py:1266
  7.3 107.3 %copy-start.13 = (f32[1,4,512]{2,1,0:T(4,128)S(1)}, f32[1,4,512]{2,1,0:T(4,128)}, u32[]{:S(2)}) copy-start(f32[1,4,512]{2,1,0:T(4,128)} %param.24) | copy-start | bytes 24580
  126.3 53.4 %copy-start = (bf16[1,2,1472,512]{3,2,1,0:T(8,128)(2,1)S(1)}, bf16[1,2,1472,512]{3,2,1,0:T(8,128)(2,1)}, u32[]{:S(2)}) copy-start(bf16[1,2,1472,512]{3,2,1,0:T(8,128)(2,1)} %param.22) | copy-start | bytes 9043972
  179.0 1.3 copy-start.7
  179.0 1.3 copy-start.9
  204.6 48.2 %copy-start.14 = (f32[1,512]{1,0:T(1,128)S(1)}, f32[1,512]{1,0:T(1,128)}, u32[]{:S(2)}) copy-start(f32[1,512]{1,0:T(1,128)} %param.23) | copy-start | bytes 6148
  477.0 45.1 %copy-start.12 = (f32[1,2048]{1,0:T(1,128)S(1)}, f32[1,2048]{1,0:T(1,128)}, u32[]{:S(2)}) copy-start(f32[1,2048]{1,0:T(1,128)} %get-tuple-element.298) | copy-start | bytes 24580
  522.9 46.7 %copy-start.15 = (f32[6,72,512]{2,1,0:T(8,128)S(1)}, f32[6,72,512]{2,1,0:T(8,128)}, u32[]{:S(2)}) copy-start(f32[6,72,512]{2,1,0:T(8,128)} %get-tuple-element.293) | copy-start | bytes 2654212
  569.5 19.6 %copy-start.11 = (f32[8,512]{1,0:T(8,128)S(1)}, f32[8,512]{1,0:T(8,128)}, u32[]{:S(2)}) copy-start(f32[8,512]{1,0:T(8,128)} %get-tuple-element.297) | copy-start | bytes 49156
  602.7 143.2 %collective-permute-start = (bf16[3,816,512]{2,1,0:T(8,128)(2,1)}, bf16[3,816,512]{2,1,0:T(8,128)(2,1)S(1)}, u32[]{:S(2)}, u32[]{:S(2)}) collective-permute-start(bf16[3,816,512]{2,1,0:T(8,128)(2,1)} %get-tuple-element.301), channel_id=1, source_target_pairs={{0,16},{16,0},{1,17},{17,1},{2,18},{18,2},{3,19},{19,3},{4,20},{20... | collective-permute-start | bytes 7520264 | tf_op jit(solution)/shard_map/ppermute | solution.py:1297
  604.0 124.5 %copy-start.6 = (f32[24,512]{1,0:T(8,128)S(1)}, f32[24,512]{1,0:T(8,128)}, u32[]{:S(2)}) copy-start(f32[24,512]{1,0:T(8,128)} %shard_map.211) | copy-start | bytes 147460
  730.9 4.3 copy-start.2
  730.9 9.2 %slice-start = ((s8[8388608]{0:T(1024)(128)(4,1)}), s8[4194304]{0:T(1024)(128)(4,1)S(1)}, s32[]{:S(2)}) async-start(s8[8388608]{0:T(1024)(128)(4,1)} %bitcast.78), calls=%async_computation.1 | async-start | bytes 8388608
  735.2 2.7 copy-start.5
  735.2 5.0 slice-start.1
  737.9 2.7 copy-start.3
  737.9 3.2 copy-start.4
  738.0 3.2 copy-start.8
  738.0 3.2 copy-start.10
  745.9 4.0 copy-start.1
Sparse Core Ops, SparseCore 0:
  381.0 154.6 all-reduce.2

commit v5 on v4

--- a/solution.py
+++ b/solution.py
@@ -68,11 +68,14 @@
             def _():
                 what(q, i)
 
+    def kept(i):
+        return hold.at[i, pl.ds(0, rows), :]
+
     def take(q, i):
-        return pltpu.make_async_copy(own(i), hold.at[i], local_sem.at[0, i])
+        return pltpu.make_async_copy(own(i), kept(i), local_sem.at[0, i])
 
     def put(q, i):
-        return pltpu.make_async_copy(hold.at[i], chunk(dst, q - q0), local_sem.at[1, i])
+        return pltpu.make_async_copy(kept(i), chunk(dst, q - q0), local_sem.at[1, i])
 
     def column(j):
         ys = (j // 2) % 2
@@ -169,25 +172,38 @@
     return begin, work, end, npd + depth + 1
 
 
+def by_branch(b, regions, run):
+    if all(rows[0] == rows[1] for _, rows, *_ in regions):
+        run(0)
+        return
+    for which in range(2):
+        pl.when(b == which)(lambda which=which: run(which))
+
+
 def gather_body(depth, regions, *refs):
     count = len(regions)
     src, dsts, scratch = refs[0], refs[1 : 1 + count], refs[1 + count :]
     b, me, z, y, c = place()
     meet(depth, b, me, z)
-    phases = [
-        gather_region(depth, *region, src, dsts[r], *scratch[4 * r : 4 * r + 4]) for r, region in enumerate(regions)
-    ]
-    for begin, *_ in phases:
-        begin()
-
-    def step(s, carry):
+
+    def run(which):
+        phases = [
+            gather_region(depth, npd, rows[which], *rest, src, dsts[r], *scratch[4 * r : 4 * r + 4])
+            for r, (npd, rows, *rest) in enumerate(regions)
+        ]
+        for begin, *_ in phases:
+            begin()
+
+        def step(s, carry):
+            for phase in phases:
+                phase[1](s)
+            return carry
+
+        lax.fori_loop(0, max(phase[3] for phase in phases), step, 0)
         for phase in phases:
-            phase[1](s)
-        return carry
-
-    lax.fori_loop(0, max(phase[3] for phase in phases), step, 0)
-    for phase in phases:
-        phase[2]()
+            phase[2]()
+
+    by_branch(b, regions, run)
 
 
 def gather_rows(mesh, src, regions, collective_id):
@@ -195,9 +211,9 @@
     shapes, scratch = [], []
     for npd, rows, _, ranges, *_ in regions:
         count = max(r[1] - r[0] for r in ranges)
-        shapes.append(jax.ShapeDtypeStruct((count * rows, width), src.dtype))
+        shapes.append(jax.ShapeDtypeStruct((count * max(rows), width), src.dtype))
         scratch += [
-            pltpu.VMEM((npd, rows, width), src.dtype),
+            pltpu.VMEM((npd, max(rows), width), src.dtype),
             pltpu.SemaphoreType.DMA((2, npd)),
             pltpu.SemaphoreType.DMA((count,)),
             pltpu.SemaphoreType.DMA((4, count)),
@@ -227,6 +243,9 @@
         ys = (j // 2) % 2
         return jnp.where(j == swap, 1 - ys, ys)
 
+    def at(ref, *index):
+        return ref.at[(*index, pl.ds(0, rows), slice(None))]
+
     def slot(j, i):
         return (j // 2 - pair0) * npd + i
 
@@ -234,7 +253,7 @@
         return src.at[pl.ds(pl.multiple_of((j * npd + i - q0) * rows, 8), rows), :]
 
     def keep(j, i):
-        return pltpu.make_async_copy(part(j, i), own.at[slot(j, i)], own_sem.at[slot(j, i)])
+        return pltpu.make_async_copy(part(j, i), at(own, slot(j, i)), own_sem.at[slot(j, i)])
 
     def remote(kind, frm, to, sem, k, device):
         return pltpu.make_async_remote_copy(
@@ -243,19 +262,19 @@
 
     def to_core(j, i):
         k = slot(j, i)
-        return remote(0, part(j, i), rc.at[k], rc_sem.at[k], k, core_peer)
+        return remote(0, part(j, i), at(rc, k), rc_sem.at[k], k, core_peer)
 
     def to_y(j, i):
         k = slot(j, i)
-        return remote(1, own.at[k], ry.at[k], ry_sem.at[k], k, y_peer)
+        return remote(1, at(own, k), at(ry, k), ry_sem.at[k], k, y_peer)
 
     def to_z(j, i, way):
         k = slot(j, i)
-        return remote(2, own.at[k], rz.at[way, k], rz_sem.at[way, k], k, (up, down)[way])
+        return remote(2, at(own, k), at(rz, way, k), rz_sem.at[way, k], k, (up, down)[way])
 
     def to_owner(j, i):
         k = slot(j, i)
-        return remote(2, own.at[k], ry.at[k], ry_sem.at[k], k, y_peer)
+        return remote(2, at(own, k), at(ry, k), ry_sem.at[k], k, y_peer)
 
     def owners(n, core, what):
         pos, i = n // npd, n % npd
@@ -284,7 +303,7 @@
             k = slot(j, i)
             keep(j, i).wait()
             to_core(j, i).wait_recv()
-            own[k] = (own[k].astype(jnp.float32) + rc[k].astype(jnp.float32)).astype(own.dtype)
+            own[k, :rows] = (own[k, :rows].astype(jnp.float32) + rc[k, :rows].astype(jnp.float32)).astype(own.dtype)
             to_y(j, i).start()
 
     def chain(j, i, zs, ys):
@@ -295,30 +314,30 @@
             k = slot(j, i)
             keep(j, i).wait()
             to_core(j, i).wait_recv()
-            acc[...] = own[k].astype(jnp.float32) + rc[k].astype(jnp.float32)
+            acc[:rows] = own[k, :rows].astype(jnp.float32) + rc[k, :rows].astype(jnp.float32)
 
             @pl.when(jnp.logical_or(jnp.logical_not(dual), jnp.logical_and(z == zs, ys == y)))
             def _():
                 to_y(j, i).wait_recv()
-                acc[...] += ry[k].astype(jnp.float32)
+                acc[:rows] += ry[k, :rows].astype(jnp.float32)
 
             @pl.when(jnp.logical_and(z >= zs, z < depth - 1))
             def _():
                 to_z(j, i, 1).wait_recv()
-                acc[...] += rz[1, k].astype(jnp.float32)
+                acc[:rows] += rz[1, k, :rows].astype(jnp.float32)
 
             @pl.when(jnp.logical_and(z <= zs, z > 0))
             def _():
                 to_z(j, i, 0).wait_recv()
-                acc[...] += rz[0, k].astype(jnp.float32)
+                acc[:rows] += rz[0, k, :rows].astype(jnp.float32)
 
             @pl.when(jnp.logical_and(z == zs, ys == y))
             def _():
-                out[i] = acc[...].astype(out.dtype)
+                out[i, :rows] = acc[:rows].astype(out.dtype)
 
             @pl.when(jnp.logical_not(jnp.logical_and(z == zs, ys == y)))
             def _():
-                own[k] = acc[...].astype(own.dtype)
+                own[k, :rows] = acc[:rows].astype(own.dtype)
 
             @pl.when(z > zs)
             def _():
@@ -357,7 +376,7 @@
             @pl.when(me == j)
             def _():
                 to_owner(j, i).wait_recv()
-                out[i] = ry[slot(j, i)].astype(out.dtype)
+                out[i, :rows] = ry[slot(j, i), :rows].astype(out.dtype)
 
         @pl.when(jnp.logical_or(column(j) == y, dual))
         def _():
@@ -394,20 +413,25 @@
     b, me, z, y, c = place()
     meet(depth, b, me, z)
     size = len(scratch) // count
-    phases = [
-        reduce_region(depth, *region, srcs[r], outs[r], *scratch[size * r : size * (r + 1)]) for r, region in enumerate(regions)
-    ]
-    for begin, *_ in phases:
-        begin()
-
-    def step(s, carry):
+
+    def run(which):
+        phases = [
+            reduce_region(depth, npd, rows[which], *rest, srcs[r], outs[r], *scratch[size * r : size * (r + 1)])
+            for r, (npd, rows, *rest) in enumerate(regions)
+        ]
+        for begin, *_ in phases:
+            begin()
+
+        def step(s, carry):
+            for phase in phases:
+                phase[1](s)
+            return carry
+
+        lax.fori_loop(0, max(phase[3] for phase in phases), step, 0)
         for phase in phases:
-            phase[1](s)
-        return carry
-
-    lax.fori_loop(0, max(phase[3] for phase in phases), step, 0)
-    for phase in phases:
-        phase[2]()
+            phase[2]()
+
+    by_branch(b, regions, run)
 
 
 def reduce_rows(mesh, srcs, regions, collective_id, dtype, lag=2):
@@ -417,14 +441,14 @@
     for npd, rows, ranges, *_ in regions:
         pairs = max((r[1] + npd - 1) // npd // 2 + (r[1] + npd - 1) // npd % 2 - r[0] // npd // 2 for r in ranges)
         held = pairs * npd
-        block = (held, rows, width)
-        shapes.append(jax.ShapeDtypeStruct((npd, rows, width), dtype))
+        block = (held, max(rows), width)
+        shapes.append(jax.ShapeDtypeStruct((npd, max(rows), width), dtype))
         scratch += [
             pltpu.VMEM(block, kind),
             pltpu.VMEM(block, kind),
             pltpu.VMEM(block, kind),
             pltpu.VMEM((2, *block), kind),
-            pltpu.VMEM((rows, width), jnp.float32),
+            pltpu.VMEM((max(rows), width), jnp.float32),
             pltpu.SemaphoreType.DMA((held,)),
             pltpu.SemaphoreType.DMA((held,)),
             pltpu.SemaphoreType.DMA((held,)),
@@ -544,9 +568,14 @@
     return jnp.where(step < n, rows, 0.0)
 
 
-def set_iso_rows(n, pitch, live, pre_iso, bias, iso_rows):
-    for w in range(pre_iso.shape[0]):
-        iso = iso_of(n, pitch, pre_iso[w], bias)
+def window_of(ref, tall, slots, w):
+    per = slots // ref.shape[0]
+    return ref[w // per, w % per * tall : (w % per + 1) * tall, :]
+
+
+def set_iso_rows(n, pitch, tall, slots, live, pre_iso, bias, iso_rows):
+    for w in range(slots):
+        iso = iso_of(n, pitch, window_of(pre_iso, tall, slots, w), bias)
         iso_rows[w * pitch : (w + 1) * pitch, :] = jnp.where(w < live[0], iso, 0.0).astype(BF)
 
 
@@ -558,7 +587,7 @@
     lax.fori_loop(0, count, step, 0)
 
 
-def down_body(k, n, pitch, off, live, x, weight, bias, pre, act, taps, x_held, w_held, t_held, total, spread, x_sem, w_sem, t_sem):
+def down_body(k, n, pitch, tall, off, live, x, weight, bias, pre, act, taps, x_held, w_held, t_held, total, spread, x_sem, w_sem, t_sem):
     slots, length, width = x.shape
 
     def window(w):
@@ -591,17 +620,16 @@
         total[...] += dot(t_held[r], w_held[r])
 
     each_of(k, tap)
-    tall = pre.shape[1]
     for w in range(slots):
         rows = fit(total[w * pitch : (w + 1) * pitch, :] + bias[0:1, :], tall)
-        pre[w] = rows
+        pre[w, :tall] = rows
         step = lax.broadcasted_iota(jnp.int32, rows.shape, 0)
         flag = jnp.where(step == tall - 1, jnp.where(w < live[0], 1.0, 0.0), 0.0)
-        act[w] = jnp.where(step < n, jnp.tanh(rows), flag).astype(BF)
+        act[w * tall : (w + 1) * tall, :] = jnp.where(step < n, jnp.tanh(rows), flag).astype(BF)
     each_of(slots, lambda w: out(w).wait())
 
 
-def up_body(k, n, pitch, off, live, half, pre_iso, weight, x, gain, bias, own, send, x_held, w_held, o_held, iso_rows, spread,
+def up_body(k, n, pitch, tall, off, live, half, pre_iso, weight, x, gain, bias, own, send, x_held, w_held, o_held, iso_rows, spread,
             x_sem, w_sem, o_sem):
     slots, length, width = x.shape
 
@@ -616,7 +644,7 @@
 
     each_of(k, lambda r: block(r).start())
     each_of(slots, lambda w: window(w).start())
-    set_iso_rows(n, pitch, live, pre_iso, bias, iso_rows)
+    set_iso_rows(n, pitch, tall, slots, live, pre_iso, bias, iso_rows)
 
     def tap(r):
         block(r).wait()
@@ -639,9 +667,9 @@
         each_of(slots // 2, lambda m, which=which: out(which, m).wait())
 
 
-def up_back_body(k, n, pitch, off, live, half, grad_own, grad_arrived, pre_iso, weight, taps, gain, bias, grad_iso, vectors,
+def up_back_body(k, n, pitch, tall, off, live, half, grad_own, grad_arrived, pre_iso, weight, taps, gain, bias, grad_iso, vectors,
                  grad_taps, part, g_held, w_held, t_held, q_held, p_held, iso_rows, total, spread, g_sem, w_sem, t_sem, q_sem, p_sem):
-    (half_slots, length, width), slots = grad_own.shape, pre_iso.shape[0]
+    (half_slots, length, width), slots = grad_own.shape, 2 * grad_own.shape[0]
     many = slots * pitch
 
     def window(which, m):
@@ -667,7 +695,7 @@
         tap_in(r).start()
 
     each_of(k, fetch)
-    set_iso_rows(n, pitch, live, pre_iso, bias, iso_rows)
+    set_iso_rows(n, pitch, tall, slots, live, pre_iso, bias, iso_rows)
     used = n * stride_of(k)
     spread[:, used:, :] = jnp.zeros((spread.shape[0], spread.shape[1] - used, LANES), F32)
 
@@ -704,19 +732,18 @@
         part_out(r).start()
 
     each_of(k, tap)
-    tall = grad_iso.shape[1]
     for w in range(slots):
-        iso = iso_of(n, pitch, pre_iso[w], bias)
+        iso = iso_of(n, pitch, window_of(pre_iso, tall, slots, w), bias)
         slope = jnp.where(lax.broadcasted_iota(jnp.int32, iso.shape, 0) < n, 1.0 - iso * iso, 0.0)
         back = jnp.where(w < live[0], total[w * pitch : (w + 1) * pitch, :] * slope, 0.0).astype(BF)
         vectors[2:3, :] += column_sum(back.astype(F32))
-        grad_iso[w] = fit(back.astype(F32), tall).astype(BF)
+        grad_iso[w * tall : (w + 1) * tall, :] = fit(back.astype(F32), tall).astype(BF)
     part_out(k - 2).wait()
     part_out(k - 1).wait()
     each_of(k, lambda r: tap_out(r).wait())
 
 
-def down_back_body(k, n, pitch, off, live, half, grad_act, pre, grad_taps, taps, weight, keep, send, vector, part, g_held, w_held,
+def down_back_body(k, n, pitch, tall, off, live, half, grad_act, pre, grad_taps, taps, weight, keep, send, vector, part, g_held, w_held,
                    t_held, p_held, o_held, rows, spread, g_sem, w_sem, t_sem, p_sem, o_sem):
     slots, (half_slots, length, width) = pre.shape[0], keep.shape
     many = slots * pitch
@@ -744,9 +771,9 @@
     each_of(k, fetch)
     vector[...] = jnp.zeros_like(vector)
     for w in range(slots):
-        act = jnp.tanh(fit(pre[w], pitch))
+        act = jnp.tanh(fit(pre[w, :tall], pitch))
         step = lax.broadcasted_iota(jnp.int32, act.shape, 0)
-        back = fit(grad_act[w], pitch) * (1.0 - act * act)
+        back = fit(window_of(grad_act, tall, slots, w), pitch) * (1.0 - act * act)
         back = jnp.where(jnp.logical_and(step < n, w < live[0]), back, 0.0).astype(BF)
         vector[...] += column_sum(back.astype(F32))
         rows[w * pitch : (w + 1) * pitch, :] = back
@@ -800,9 +827,9 @@
     def spec(e):
         def at(step, order, count, shift):
             last = jnp.maximum(count[0] - 1, 0) // PACK
-            return order[jnp.minimum(step, last) * PACK + e], 0, 0
-
-        return pl.BlockSpec((1, tall, width), at)
+            return order[jnp.minimum(step, last) * PACK + e], 0
+
+        return pl.BlockSpec((tall, width), at)
 
     return [spec(e) for e in range(PACK)]
 
@@ -811,7 +838,7 @@
     def copy(at, e):
         where = jnp.minimum(at * PACK + e, order.shape[0] - 1)
         return pltpu.make_async_copy(
-            slots_ref.at[at % 2, e], out.at[order[where]], sem.at[at % 2, e]
+            slots_ref.at[at % 2, e], out.at[pl.ds(pl.multiple_of(order[where] * tall, SUBLANES), tall), :], sem.at[at % 2, e]
         )
 
     live = pl.cdiv(count[0], PACK)
@@ -838,81 +865,96 @@
                 copy(step, e).wait()
 
 
+PARTS = 2
+
+
 def iso_forward_body(tall, pitch, blocks, steps, order, count, shift, *refs):
-    acts, (weight, out, buffer, columns, ready, sem) = refs[:PACK], refs[PACK:]
+    acts, (weight, out), rest = refs[:PACK], refs[PACK : PACK + 2], refs[PACK + 2 :]
+    buffers, columns, (ready, sem) = rest[:PACK], rest[PACK : PACK + PARTS], rest[PACK + PARTS :]
     step = pl.program_id(0)
     width = weight.shape[1]
+    group = PACK // PARTS
 
     @pl.when(step == 0)
     def _():
-        buffer[...] = jnp.zeros_like(buffer)
-        columns[...] = jnp.zeros_like(columns)
+        for ref in (*buffers, *columns):
+            ref[...] = jnp.zeros_like(ref)
 
     @pl.when(step * PACK < count[0])
     def _():
-        for e in range(PACK):
-            buffer[tall : 2 * tall, :] = (jnp.where(step * PACK + e < count[0], acts[e][0].astype(F32), 0.0))
-            for m in range(blocks):
-                columns[e * pitch : e * pitch + tall, m * width : (m + 1) * width] = shifted(buffer, tall - shift[m], tall)
-        total = dot(columns[...], weight[...])
-        for e in range(PACK):
-            ready[step % 2, e] = total[e * pitch : e * pitch + tall].astype(BF)
+        for p in range(PARTS):
+            for at in range(group):
+                e = p * group + at
+                buffers[e][tall : 2 * tall, :] = jnp.where(step * PACK + e < count[0], acts[e][...].astype(F32), 0.0)
+                for m in range(blocks):
+                    columns[p][at * pitch : at * pitch + tall, m * width : (m + 1) * width] = shifted(
+                        buffers[e], tall - shift[m], tall
+                    )
+            total = dot(columns[p][...], weight[...])
+            for at in range(group):
+                ready[step % 2, p * group + at] = total[at * pitch : at * pitch + tall].astype(BF)
 
     scatter_out(order, count, ready, sem, out, tall, step, steps)
 
 
 def iso_back_body(tall, pitch, blocks, steps, order, count, shift, *refs):
     acts, grads = refs[:PACK], refs[PACK : 2 * PACK]
-    weight, out, kernel_grad, buffer, columns, gathered, ahead, ready, sem = refs[2 * PACK :]
+    (weight, out, kernel_grad), rest = refs[2 * PACK : 2 * PACK + 3], refs[2 * PACK + 3 :]
+    buffers, ahead, rest = rest[:PACK], rest[PACK : 2 * PACK], rest[2 * PACK :]
+    columns, later, (gathered, ready, sem) = rest[0], rest[1 : 1 + PARTS], rest[1 + PARTS :]
     step = pl.program_id(0)
     width = weight.shape[1]
+    group = PACK // PARTS
 
     @pl.when(step == 0)
     def _():
-        buffer[...] = jnp.zeros_like(buffer)
-        columns[...] = jnp.zeros_like(columns)
-        gathered[...] = jnp.zeros_like(gathered)
-        ahead[...] = jnp.zeros_like(ahead)
-        kernel_grad[...] = jnp.zeros_like(kernel_grad)
+        for ref in (*buffers, *ahead, columns, *later, gathered, kernel_grad):
+            ref[...] = jnp.zeros_like(ref)
 
     @pl.when(step * PACK < count[0])
     def _():
         for e in range(PACK):
             alive = step * PACK + e < count[0]
-            buffer[tall : 2 * tall, :] = (jnp.where(alive, acts[e][0].astype(F32), 0.0))
-            for m in range(blocks):
-                columns[e * pitch : e * pitch + tall, m * width : (m + 1) * width] = shifted(buffer, tall - shift[m], tall)
-            gathered[e * pitch : e * pitch + tall, :] = jnp.where(alive, grads[e][0].astype(F32), 0.0).astype(BF)
-        for m in range(blocks):
-            kernel_grad[m * width : (m + 1) * width, :] += dot_at(columns[:, m * width : (m + 1) * width], gathered[...])
+            grad = jnp.where(alive, grads[e][...].astype(F32), 0.0)
+            ahead[e][:tall, :] = grad
+            gathered[e * pitch : e * pitch + tall, :] = grad.astype(BF)
+        for p in range(PARTS):
+            for at in range(group):
+                e = p * group + at
+                for m in range(blocks):
+                    later[p][at * pitch : at * pitch + tall, m * width : (m + 1) * width] = shifted(ahead[e], shift[m], tall)
+            total = dot_bt(later[p][:, :width], weight[:width, :])
+            for m in range(1, blocks):
+                total += dot_bt(later[p][:, m * width : (m + 1) * width], weight[m * width : (m + 1) * width, :])
+            for at in range(group):
+                ready[step % 2, p * group + at] = total[at * pitch : at * pitch + tall].astype(BF)
         for e in range(PACK):
             alive = step * PACK + e < count[0]
-            ahead[:tall, :] = (jnp.where(alive, grads[e][0].astype(F32), 0.0))
-            for m in range(blocks):
-                columns[e * pitch : e * pitch + tall, m * width : (m + 1) * width] = shifted(ahead, shift[m], tall)
-        total = dot_bt(columns[:, :width], weight[:width, :])
-        for m in range(1, blocks):
-            total += dot_bt(columns[:, m * width : (m + 1) * width], weight[m * width : (m + 1) * width, :])
-        for e in range(PACK):
-            ready[step % 2, e] = total[e * pitch : e * pitch + tall].astype(BF)
+            buffers[e][tall : 2 * tall, :] = jnp.where(alive, acts[e][...].astype(F32), 0.0)
+        for m in range(blocks):
+            for e in range(PACK):
+                columns[e * pitch : e * pitch + tall, m * width : (m + 1) * width] = shifted(buffers[e], tall - shift[m], tall)
+            kernel_grad[m * width : (m + 1) * width, :] += dot_at(columns[:, m * width : (m + 1) * width], gathered[...])
 
     scatter_out(order, count, ready, sem, out, tall, step, steps)
 
 
-def iso_call(back, order, count, shift, weight, *windows):
-    many, tall, width = windows[0].shape
+def iso_call(back, tall, order, count, shift, weight, *windows):
+    many, (rows, width) = order.shape[0], windows[0].shape
     blocks = weight.shape[0] // width
     pitch = up_to(tall, 16)
     steps = many // PACK
     held = pl.BlockSpec(weight.shape, lambda step, *_: (0, 0))
-    out_shape = [jax.ShapeDtypeStruct((many, tall, width), BF)]
+    out_shape = [jax.ShapeDtypeStruct((rows, width), BF)]
     out_specs = [ANY]
-    copies = pltpu.VMEM((2 * tall + SUBLANES, width), F32)
-    scratch = [copies, pltpu.VMEM((PACK * pitch, blocks * width), BF)]
+    copies = [pltpu.VMEM((2 * tall + SUBLANES, width), F32)] * PACK
+    halves = [pltpu.VMEM((PACK // PARTS * pitch, blocks * width), BF)] * PARTS
     if back:
         out_shape.append(jax.ShapeDtypeStruct(weight.shape, F32))
         out_specs.append(held)
-        scratch += [pltpu.VMEM((PACK * pitch, width), BF), copies]
+        scratch = [*copies, *copies, pltpu.VMEM((PACK * pitch, blocks * width), BF), *halves, pltpu.VMEM((PACK * pitch, width), BF)]
+    else:
+        scratch = [*copies, *halves]
     scratch += [pltpu.VMEM((2, PACK, tall, width), BF), pltpu.SemaphoreType.DMA((2, PACK))]
     body = iso_back_body if back else iso_forward_body
     flops = 2 * many * tall * weight.size * (2 if back else 1) // 3
@@ -1146,7 +1188,9 @@
         group_rows = branch_blocks.shape[2] * members
         share = branch_blocks.shape[2]
         taps_of = [length // k for k in SCALES]
+        members = mesh.shape["dp"]
         tall = up_to(max(taps_of) + 1, 8)
+        talls = [up_to(n + 1, 8) if members <= 32 else tall for n in taps_of]
         pitches = [up_to(n, 16) for n in taps_of]
         reach = max(SCALES)
         most = slots * max(pitches)
@@ -1164,7 +1208,7 @@
         none = ((), ())
         own_rows = branch_blocks.reshape(GROUPS * share, width)
         down_weight, up_weight = gather_rows(
-            mesh, own_rows, ((npd, chunk, 0, down_ranges, swaps, none), (npd, chunk, share, up_ranges, (-1, -1), none)), 1
+            mesh, own_rows, ((npd, (chunk, chunk), 0, down_ranges, swaps, none), (npd, (chunk, chunk), share, up_ranges, (-1, -1), none)), 1
         )
 
         blocks = (share + width - 1) // width + 1
@@ -1176,7 +1220,7 @@
             first = g * group_rows + me * share - k_of * width
             inside = jnp.logical_and(first + rows_at >= 0, first + rows_at < n_of * width)
             start = first // width
-            shifts.append(jnp.clip(n_of - 1 - start - jnp.arange(blocks), 0, tall))
+            shifts.append(jnp.clip(n_of - 1 - start - jnp.arange(blocks), 0, jnp.where(branch == 0, talls[0], talls[1])))
             lead.append(first - start * width)
             insides.append(inside)
             kept = jnp.where(inside[:, None], own_rows[g * share : (g + 1) * share], 0)
@@ -1187,6 +1231,7 @@
         def windows_shape(kind):
             return jax.ShapeDtypeStruct((slots, tall, width), kind)
 
+        flat_shape = jax.ShapeDtypeStruct((slots * tall, width), BF)
         full = jax.ShapeDtypeStruct((slots // 2, length, width), BF)
         taps_shape = jax.ShapeDtypeStruct((reach, most, width), BF)
         part_shape = jax.ShapeDtypeStruct((max(r[1] - r[0] for r in down_ranges) * chunk, width), BF)
@@ -1207,7 +1252,7 @@
                 "H": pltpu.SemaphoreType.DMA((2, slots // 2)), "P": pltpu.SemaphoreType.DMA((2,)),
             }
             return pl.pallas_call(
-                functools.partial(body, k, n, pitch, off),
+                functools.partial(body, k, n, pitch, talls[index], off),
                 out_shape=outs,
                 in_specs=[spec[s] for s in kinds[: len(operands)]],
                 out_specs=tuple(spec[s] for s in kinds[len(operands) :]),
@@ -1218,7 +1263,7 @@
 
         def down_of(index):
             def run(*operands):
-                return call(down_body, index, 0, (windows_shape(F32), windows_shape(BF), taps_shape), "xwtf1SKS", "shhvvvh",
+                return call(down_body, index, 0, (windows_shape(F32), flat_shape, taps_shape), "xwtf1SKS", "shhvvvh",
                             *operands)
             return run
 
@@ -1229,28 +1274,33 @@
         pieces = 2 if per % 2 == 0 else 1
 
         def spread_windows(values, collective_id):
-            flat = values.reshape(slots * tall, width)
-            [every] = gather_rows(mesh, flat, ((2, slots * tall // 2, 0, ((0, 2 * members),) * 2, (-1, -1), none),), collective_id)
-            return every.reshape(members * slots, tall, width)
+            rows = tuple(slots * t // 2 for t in talls)
+            [every] = gather_rows(mesh, values, ((2, rows, 0, ((0, 2 * members),) * 2, (-1, -1), none),), collective_id)
+            return every
 
         def sum_windows(values, collective_id):
-            parts = values.reshape(members, passes, per, tall, width)
+            rows = tuple(per * t // pieces for t in talls)
+            parts = values.reshape(members, passes, per * tall, width)
             results = [
                 reduce_rows(mesh, [parts[:, p].reshape(-1, width)],
-                            ((pieces, per * tall // pieces, ((0, pieces * members),) * 2, (-1, -1), none),), collective_id + p, F32)[0]
+                            ((pieces, rows, ((0, pieces * members),) * 2, (-1, -1), none),), collective_id + p, F32)[0]
                 for p in range(passes)
             ]
-            return jnp.concatenate([r.reshape(per, tall, width) for r in results], axis=0)
+            return jnp.concatenate(results, axis=0)
+
+        def iso_of_branch(back):
+            return [lambda *operands, t=t: iso_call(back, t, *operands) for t in talls]
 
         acts = spread_windows(act, 3)
-        alive = acts[:, tall - 1, 0] > 0.5
+        flags = [acts[t - 1 : members * slots * t : t, 0] for t in talls]
+        alive = jnp.where(branch == 0, flags[0], flags[1]) > 0.5
         places = jnp.arange(members * slots)
         rank = jnp.sum(jnp.logical_and(alive[None, :], places[None, :] < places[:, None]).astype(jnp.int32), axis=1)
         order = jnp.sum(
             jnp.where(jnp.logical_and(alive[:, None], rank[:, None] == places[None, :]), places[:, None], 0), axis=0
         ).astype(jnp.int32)
         count = jnp.sum(alive.astype(jnp.int32))[None]
-        [terms] = iso_call(False, order, count, shift, iso_weight, acts)
+        [terms] = branch_index_pair(branch, *iso_of_branch(False), order, count, shift, iso_weight, acts)
         pre_iso = sum_windows(terms, 16)
 
         def up_of(index):
@@ -1268,7 +1318,7 @@
         def up_back_of(index):
             def run(*operands):
                 return call(up_back_body, index, up_offs[index],
-                            (windows_shape(BF), jax.ShapeDtypeStruct((8, width), F32), taps_shape, up_part_shape),
+                            (flat_shape, jax.ShapeDtypeStruct((8, width), F32), taps_shape, up_part_shape),
                             "owttpif1HKKKP", "sshhvhhvvvvhh", *operands)
             return run
 
@@ -1276,7 +1326,7 @@
             branch, up_back_of(0), up_back_of(1), live, half, grad_own.reshape(full.shape), arrived.reshape(full.shape), pre_iso, up_weight, taps, gain, bias
         )
         grads = spread_windows(grad_iso, 4)
-        back_terms, kernel_grad = iso_call(True, order, count, shift, iso_weight, acts, grads)
+        back_terms, kernel_grad = branch_index_pair(branch, *iso_of_branch(True), order, count, shift, iso_weight, acts, grads)
         grad_act = sum_windows(back_terms, 32)
         grad_act, wide = lax.optimization_barrier((grad_act, wide))
 
@@ -1302,7 +1352,7 @@
         up_sum, down_sum = [
             total.reshape(share, width)
             for total in reduce_rows(
-                mesh, [up_part, down_part], ((npd, chunk, up_ranges, (-1, -1), none), (npd, chunk, down_ranges, swaps, none)), 5,
+                mesh, [up_part, down_part], ((npd, (chunk, chunk), up_ranges, (-1, -1), none), (npd, (chunk, chunk), down_ranges, swaps, none)), 5,
                 BF, 6,
             )
         ]

time: 771 us -> 744 us (0.965)
  Pallas kernels: 697 us -> 681 us
    pallas_call x3, Pallas kernels: 209 us -> 194 us  [gather_rows(): pl.pallas_call(functools.partial(gather_body, depth, regions), out_shape=...]
    pallas_call x2, Pallas kernels: 65.3 us -> 56 us  [iso_call(): pl.pallas_call(functools.partial(body, tall, pitch, blocks, steps), out_s...]
where the time goes in v5:
time: 744 us; the launch traced here: 736 us
  Pallas kernels  681 us (92%)
  other arithmetic  24.8 us (3%)
  between operations  15.6 us (2%)
  local copies, waits for them, and re-layouts  12.1 us (2%)
    pallas_call x3, Pallas kernels, reduce_rows(): pl.pallas_call(functools.partial(reduce_body, depth, tuple(((*region, lag...  221 us
    pallas_call x3, Pallas kernels, gather_rows(): pl.pallas_call(functools.partial(gather_body, depth, regions), out_shape=...  194 us
    pallas_call x1, Pallas kernels, feed_call(): pl.pallas_call(functools.partial(feed_body, per_window, 512), out_shape=[...  114 us
    pallas_call x4, Pallas kernels, call(): pl.pallas_call(functools.partial(body, k, n, pitch, talls[index], off), o...  76.1 us
    pallas_call x2, Pallas kernels, iso_call(): pl.pallas_call(functools.partial(body, tall, pitch, blocks, steps), out_s...  56 us
    pallas_call x1, Pallas kernels, total_over(): pl.pallas_call(functools.partial(total_body, depth), out_shape=jax.ShapeD...  19.8 us
  transfers between devices with their start and end apart: 2, of which 0 were waited for; matrix products, arithmetic and copies ran while one was open for 3% of the time, Pallas kernels for 40%

profile of v5, /device:TPU:19, one launch (start us, length us, event | category | flops | bytes accessed | tf_op | source)
XLA Modules:
  0.0 735.6 jit_solution(11941979724744700835)
XLA Ops:
  7.3 107.3 %shard_map.203 = (bf16[8280,512]{1,0:T(8,128)(2,1)}, bf16[8280,512]{1,0:T(8,128)(2,1)}) custom-call(bf16[2944,512]{1,0:T(8,128)(2,1)} %bitcast.46), custom_call_target="tpu_custom_call" | custom-call | flops 49999998976 | bytes 16777216 | tf_op jit(solution)/shard_map/pallas_call | solution.py:221
  114.6 11.7 %conditional.6 = ((f32[6,72,512]{2,1,0:T(8,128)}, bf16[432,512]{1,0:T(8,128)(2,1)S(1)}, bf16[16,480,512]{2,1,0:T(8,128)(2,1)})) conditional(s32[]{:T(128)} %convert_element_type.50, (s32[1]{0:T(128)}, bf16[6,816,512]{2,1,0:T(8,128)(2,1)}, bf16[8280,512]{1,0:T(8,128)(2,1)}, f32[4,512]{1,0:T(4,128)S(1)}) %tuple.129, (s32[1]{0:T(128)}, ...), branch_computations={%region_0.1_spmd, %region_1.2_spmd} | conditional | flops 20000000000 | bytes 16777224 | solution.py:1179
  114.6 11.7 %branch_0_fun.8 = (f32[6,72,512]{2,1,0:T(8,128)}, bf16[432,512]{1,0:T(8,128)(2,1)S(1)}, bf16[16,480,512]{2,1,0:T(8,128)(2,1)}) custom-call(s32[1]{0:T(128)} %get-tuple-element.215.live, bf16[6,816,512]{2,1,0:T(8,128)(2,1)} %get-tuple-element.216.x, bf16[8280,512]{1,0:T(8,128)(2,1)} %get-tuple-element.217.weight, f32[4,512]{1,0:T(4,128)S(1)} %get-tuple-element.218.bias), custom_call_target="tpu_custom_call" | custom-call | flops 20000000000 | bytes 16777216 | tf_op jit(solution)/shard_map/cond/branch_0_fun/pallas_call | solution.py:1254
  126.3 41.3 %shard_map.204 = bf16[6912,512]{1,0:T(8,128)(2,1)} custom-call(bf16[432,512]{1,0:T(8,128)(2,1)S(1)} %get-tuple-element.348.refs_0_), custom_call_target="tpu_custom_call" | custom-call | flops 49999998976 | bytes 16777216 | tf_op jit(solution)/shard_map/pallas_call | solution.py:221
  167.7 1.5 slice.52
  169.2 1.4 slice.53
  173.4 2.3 pad_maximum_fusion
  176.3 18.9 %conditional.7 = (bf16[6912,512]{1,0:T(8,128)(2,1)}) conditional(s32[]{:T(128)} %convert_element_type.50, (s32[96]{0:T(128)S(1)}, s32[1]{0:T(128)}, s32[8]{0:T(128)}, bf16[6912,512]{1,0:T(8,128)(2,1)}, bf16[4096,512]{1,0:T(8,128)(2,1)}) %tuple.73, (s32[96]{0:T(128)S(1)}, s32[1]{0:T(128)}, s32[8]{0:T(128)}, bf16[6912,512]{1,0:T(8,128)(2,1)}, ...), branch_computations={%region_5.6_spmd, %region_6.7_spmd} | conditional | flops 9663676416 | bytes 4194312 | solution.py:1179
  176.3 18.7 %branch_0_fun.9 = bf16[6912,512]{1,0:T(8,128)(2,1)} custom-call(s32[96]{0:T(128)S(1)} %get-tuple-element.223.order, s32[1]{0:T(128)} %get-tuple-element.224.count, s32[8]{0:T(128)} %get-tuple-element.225.shift, bf16[6912,512]{1,0:T(8,128)(2,1)} %get-tuple-element.226.refs_0_.refs_1_.refs_2_.refs_3_.refs_4_.refs_5_.refs_6_.refs_7_, ...), custom_call_target="tpu_custom_call" | custom-call | flops 7516192768 | bytes 4194304 | tf_op jit(solution)/shard_map/cond/branch_0_fun/pallas_call | solution.py:961
  195.2 39.2 %shard_map.205 = f32[2,216,512]{2,1,0:T(8,128)} custom-call(bf16[6912,512]{1,0:T(8,128)(2,1)} %get-tuple-element.580.refs_0_), custom_call_target="tpu_custom_call" | custom-call | flops 49999998976 | bytes 16777216 | tf_op jit(solution)/shard_map/pallas_call | solution.py:458
  234.5 14.2 %conditional.8 = (bf16[2448,512]{1,0:T(8,128)(2,1)}, bf16[2448,512]{1,0:T(8,128)(2,1)}) conditional(s32[]{:T(128)} %convert_element_type.50, (s32[1]{0:T(128)}, s32[1]{0:T(128)}, f32[2,216,512]{2,1,0:T(8,128)}, bf16[8280,512]{1,0:T(8,128)(2,1)}, bf16[6,816,512]{2,1,0:T(8,128)(2,1)}, /*index=5*/f32[1,512]{1,0:T(1,128)S(1)}, ...), branch_computations={%region_7.8_spmd, %region_8.9_spmd} | conditional | flops 20000000000 | bytes 16777232 | solution.py:1179
  234.5 13.8 %branch_0_fun.10 = (bf16[3,816,512]{2,1,0:T(8,128)(2,1)}, bf16[3,816,512]{2,1,0:T(8,128)(2,1)}) custom-call(s32[1]{0:T(128)} %get-tuple-element.233.live, s32[1]{0:T(128)} %get-tuple-element.234.half, f32[2,216,512]{2,1,0:T(8,128)} %get-tuple-element.235.pre_iso, bf16[8280,512]{1,0:T(8,128)(2,1)} %get-tuple-element.236.weight, ...), custom_call_target="tpu_custom_call" | custom-call | flops 20000000000 | bytes 16777216 | tf_op jit(solution)/shard_map/cond/branch_0_fun/pallas_call | solution.py:1254
  248.7 113.6 %shard_map.206 = (bf16[2448,512]{1,0:T(8,128)(2,1)}, bf16[2448,512]{1,0:T(8,128)(2,1)S(1)}, bf16[2448,512]{1,0:T(8,128)(2,1)}, bf16[1024,512]{1,0:T(8,128)(2,1)}...) custom-call(s32[1]{0:T(128)S(6)} %copy.67.live, ...), custom_call_target="tpu_custom_call" | custom-call | flops 41070624768 | bytes 41943040 | tf_op jit(solution)/shard_map/pallas_call | solution.py:1088
  362.9 34.7 %conditional.9 = (bf16[432,512]{1,0:T(8,128)(2,1)S(1)}, bf16[16,480,512]{2,1,0:T(8,128)(2,1)}, bf16[8280,512]{1,0:T(8,128)(2,1)}, f32[1,512]{1,0:T(1,128)}, f32[3,512]{1,0:T(4,128)}) conditional(s32[]{:T(128)} %convert_element_type.50, (s32[1]{0:T(128)}, s32[1]{0:T(128)}, bf16[3,816,512]{2,1,0:T(8,128)(2,1)S(1)}, ...), branch_computations={%region_9.10_spmd.clone.clone, %region_10.11_spmd.clone.clone} | conditional | flops 20000000000 | bytes 16793640 | solution.py:1179
  362.9 31.9 %branch_0_fun.13 = (bf16[432,512]{1,0:T(8,128)(2,1)S(1)}, f32[8,512]{1,0:T(8,128)}, bf16[16,480,512]{2,1,0:T(8,128)(2,1)}, bf16[8280,512]{1,0:T(8,128)(2,1)}) custom-call(s32[1]{0:T(128)} %get-tuple-element.471.live, s32[1]{0:T(128)} %get-tuple-element.472.half, bf16[3,816,512]{2,1,0:T(8,128)(2,1)S(1)} %get-tuple-element.473.grad_own, ...), custom_call_target="tpu_custom_call" | custom-call | flops 20000000000 | bytes 16777216 | tf_op jit(solution)/shard_map/cond/branch_0_fun/pallas_call | solution.py:1254
  394.8 1.3 slice.71
  396.1 1.3 slice.70
  397.6 45.9 %shard_map.207 = bf16[6912,512]{1,0:T(8,128)(2,1)} custom-call(bf16[432,512]{1,0:T(8,128)(2,1)S(1)} %get-tuple-element.356.refs_0_), custom_call_target="tpu_custom_call" | custom-call | flops 49999998976 | bytes 16777216 | tf_op jit(solution)/shard_map/pallas_call | solution.py:221
  443.5 37.5 %conditional.10 = ((bf16[6912,512]{1,0:T(8,128)(2,1)}, f32[4096,512]{1,0:T(8,128)})) conditional(s32[]{:T(128)} %convert_element_type.50, (s32[96]{0:T(128)S(1)}, s32[1]{0:T(128)}, s32[8]{0:T(128)}, bf16[6912,512]{1,0:T(8,128)(2,1)}, bf16[6912,512]{1,0:T(8,128)(2,1)}, /*index=5*/bf16[4096,512]{1,0:T(8,128)(2,1)}) %tuple.127, (s32[96]{0:T(128)S(1)}, ...), branch_computations={%region_11.12_spmd, %region_12.13_spmd} | conditional | flops 19327352832 | bytes 4194312 | solution.py:1179
  443.5 37.3 %branch_0_fun.11 = (bf16[6912,512]{1,0:T(8,128)(2,1)}, f32[4096,512]{1,0:T(8,128)}) custom-call(s32[96]{0:T(128)S(1)} %get-tuple-element.277.order, s32[1]{0:T(128)} %get-tuple-element.278.count, s32[8]{0:T(128)} %get-tuple-element.279.shift, bf16[6912,512]{1,0:T(8,128)(2,1)} %get-tuple-element.280.refs_0_.refs_1_.refs_2_.refs_3_.refs_4_.refs_5_.refs_6_.refs_7_, ...), custom_call_target="tpu_custom_call" | custom-call | flops 15032385536 | bytes 4194304 | tf_op jit(solution)/shard_map/cond/branch_0_fun/pallas_call | solution.py:961
  482.6 57.5 %shard_map.208 = f32[2,216,512]{2,1,0:T(8,128)S(1)} custom-call(bf16[6912,512]{1,0:T(8,128)(2,1)} %get-tuple-element.357.refs_0_), custom_call_target="tpu_custom_call" | custom-call | flops 49999998976 | bytes 16777216 | tf_op jit(solution)/shard_map/pallas_call | solution.py:458
  540.1 19.0 %conditional.11 = ((bf16[3,816,512]{2,1,0:T(8,128)(2,1)}, bf16[3,816,512]{2,1,0:T(8,128)(2,1)}, f32[1,512]{1,0:T(1,128)S(1)}, bf16[8280,512]{1,0:T(8,128)(2,1)})) conditional(s32[]{:T(128)} %convert_element_type.50, (s32[1]{0:T(128)}, s32[1]{0:T(128)}, f32[2,216,512]{2,1,0:T(8,128)S(1)}, f32[6,72,512]{2,1,0:T(8,128)S(1)}, ...), branch_computations={%region_16.17_spmd, %region_17.18_spmd} | conditional | flops 20000000000 | bytes 16777224 | solution.py:1179
  540.2 18.7 %branch_0_fun.12 = (bf16[3,816,512]{2,1,0:T(8,128)(2,1)}, bf16[3,816,512]{2,1,0:T(8,128)(2,1)}, f32[1,512]{1,0:T(1,128)S(1)}, bf16[8280,512]{1,0:T(8,128)(2,1)}) custom-call(s32[1]{0:T(128)} %get-tuple-element.289.live, s32[1]{0:T(128)} %get-tuple-element.290.half, f32[2,216,512]{2,1,0:T(8,128)S(1)} %get-tuple-element.291.grad_act, ...), custom_call_target="tpu_custom_call" | custom-call | flops 20000000000 | bytes 16777216 | tf_op jit(solution)/shard_map/cond/branch_0_fun/pallas_call | solution.py:1254
  560.7 19.8 %shard_map.209 = f32[24,512]{1,0:T(8,128)} custom-call(f32[24,512]{1,0:T(8,128)} %maximum_maximum_fusion.values), custom_call_target="tpu_custom_call" | custom-call | tf_op jit(solution)/shard_map/pallas_call | solution.py:1164
  580.8 124.6 %shard_map.210 = (bf16[8,184,512]{2,1,0:T(8,128)(2,1)}, bf16[8,184,512]{2,1,0:T(8,128)(2,1)}) custom-call(bf16[8280,512]{1,0:T(8,128)(2,1)} %get-tuple-element.372.refs_0_, bf16[8280,512]{1,0:T(8,128)(2,1)} %get-tuple-element.468.refs_1_), custom_call_target="tpu_custom_call" | custom-call | flops 49999998976 | bytes 16777216 | tf_op jit(solution)/shard_map/pallas_call | solution.py:458
  707.8 4.3 convert_element_type.61
  712.1 2.7 convert_element_type.62
  714.9 1.6 convert_element_type.60
  718.0 1.5 fusion.4
  719.5 3.3 maximum_bitcast_fusion
  722.8 4.0 fusion.5
  726.9 1.5 copy.68
  (80 shorter events, 10.5 us)
Async XLA Ops:
  7.2 532.9 %all-reduce.3.cloned.1.call-start = ((), (), s32[]{:S(2)}) async-start(), calls=%async_computation | async-start | bytes 10485760 | tf_op jit(solution)/shard_map/psum | solution.py:1316
  7.3 107.3 %copy-start.15 = (f32[1,4,512]{2,1,0:T(4,128)S(1)}, f32[1,4,512]{2,1,0:T(4,128)}, u32[]{:S(2)}) copy-start(f32[1,4,512]{2,1,0:T(4,128)} %param.28) | copy-start | bytes 24580
  126.3 46.1 %copy-start = (bf16[1,2,1472,512]{3,2,1,0:T(8,128)(2,1)S(1)}, bf16[1,2,1472,512]{3,2,1,0:T(8,128)(2,1)}, u32[]{:S(2)}) copy-start(bf16[1,2,1472,512]{3,2,1,0:T(8,128)(2,1)} %param.26) | copy-start | bytes 9043972
  172.1 0.9 copy-start.7
  172.1 0.9 copy-start.9
  172.3 4.0 copy-start.13
  195.2 39.2 %copy-start.16 = (f32[1,512]{1,0:T(1,128)S(1)}, f32[1,512]{1,0:T(1,128)}, u32[]{:S(2)}) copy-start(f32[1,512]{1,0:T(1,128)} %param.27) | copy-start | bytes 6148
  397.6 45.9 %copy-start.14 = (s32[96]{0:T(128)S(1)}, s32[96]{0:T(128)}, u32[]{:S(2)}) copy-start(s32[96]{0:T(128)} %copy-done.13) | copy-start | bytes 1156
  443.5 37.6 %copy-start.18 = (pred[2]{0:T(512)(128)(4,1)S(1)}, pred[2]{0:T(512)(128)(4,1)}, u32[]{:S(2)}) copy-start(pred[2]{0:T(512)(128)(4,1)} %iota_compare_fusion.2) | copy-start | bytes 10
  443.5 38.2 %copy-start.12 = (f32[1,2048]{1,0:T(1,128)S(1)}, f32[1,2048]{1,0:T(1,128)}, u32[]{:S(2)}) copy-start(f32[1,2048]{1,0:T(1,128)} %get-tuple-element.367) | copy-start | bytes 24580
  482.6 57.6 %copy-start.17 = (f32[6,72,512]{2,1,0:T(8,128)S(1)}, f32[6,72,512]{2,1,0:T(8,128)}, u32[]{:S(2)}) copy-start(f32[6,72,512]{2,1,0:T(8,128)} %get-tuple-element.362) | copy-start | bytes 2654212
  540.1 19.8 %copy-start.11 = (f32[8,512]{1,0:T(8,128)S(1)}, f32[8,512]{1,0:T(8,128)}, u32[]{:S(2)}) copy-start(f32[8,512]{1,0:T(8,128)} %get-tuple-element.366) | copy-start | bytes 49156
  580.5 142.3 %collective-permute-start = (bf16[3,816,512]{2,1,0:T(8,128)(2,1)}, bf16[3,816,512]{2,1,0:T(8,128)(2,1)S(1)}, u32[]{:S(2)}, u32[]{:S(2)}) collective-permute-start(bf16[3,816,512]{2,1,0:T(8,128)(2,1)} %get-tuple-element.370), channel_id=1, source_target_pairs={{0,16},{16,0},{1,17},{17,1},{2,18},{18,2},{3,19},{19,3},{4,20},{20... | collective-permute-start | bytes 7520264 | tf_op jit(solution)/shard_map/ppermute | solution.py:1347
  580.8 124.6 %copy-start.6 = (f32[24,512]{1,0:T(8,128)S(1)}, f32[24,512]{1,0:T(8,128)}, u32[]{:S(2)}) copy-start(f32[24,512]{1,0:T(8,128)} %shard_map.209) | copy-start | bytes 147460
  707.8 4.3 copy-start.2
  707.8 9.2 %slice-start = ((s8[8388608]{0:T(1024)(128)(4,1)}), s8[4194304]{0:T(1024)(128)(4,1)S(1)}, s32[]{:S(2)}) async-start(s8[8388608]{0:T(1024)(128)(4,1)} %bitcast.44), calls=%async_computation.1 | async-start | bytes 8388608
  712.1 2.7 copy-start.5
  712.1 5.0 slice-start.1
  714.9 2.7 copy-start.3
  714.9 3.2 copy-start.4
  714.9 3.2 copy-start.8
  714.9 3.2 copy-start.10
  722.8 4.0 copy-start.1
Sparse Core Ops, SparseCore 0:
  362.5 177.4 all-reduce.2

commit v6 on v5

--- a/solution.py
+++ b/solution.py
@@ -21,11 +21,29 @@
     return found
 
 
-def meet(depth, b, me, z):
+def each_other_row(depth, z, what):
+    def each(other, carry):
+        @pl.when(other != z)
+        def _():
+            what(other)
+
+        return carry
+
+    lax.fori_loop(0, depth, each, 0)
+
+
+def meet(depth, b, me, z, wide=False):
     barrier = pltpu.get_barrier_semaphore()
     y, c = (me // 2) % 2, me % 2
     pl.semaphore_signal(barrier, 1, device_id=(b, me + 1 - 2 * c), device_id_type=MESH)
     pl.semaphore_signal(barrier, 1, device_id=(b, me + 2 - 4 * y), device_id_type=MESH)
+    if wide:
+        pl.semaphore_signal(barrier, 1, device_id=(1 - b, me), device_id_type=MESH)
+        each_other_row(
+            depth, z, lambda other: pl.semaphore_signal(barrier, 1, device_id=(b, me + 4 * (other - z)), device_id_type=MESH)
+        )
+        pl.semaphore_wait(barrier, 2 + depth)
+        return
 
     @pl.when(z > 0)
     def _():
@@ -407,34 +425,88 @@
     )
 
 
-def reduce_body(depth, regions, *refs):
-    count = len(regions)
-    srcs, outs, scratch = refs[:count], refs[count : 2 * count], refs[2 * count :]
+def total_steps(depth, values, out, pair, come, far, sent_sem, come_sem, far_sent, far_come):
     b, me, z, y, c = place()
-    meet(depth, b, me, z)
-    size = len(scratch) // count
+    peers = ((b, me + 1 - 2 * c), (b, me + 2 - 4 * y), (1 - b, me))
+
+    def swap(at, frm):
+        return pltpu.make_async_remote_copy(
+            pair.at[frm], come.at[at], sent_sem.at[at], come_sem.at[at], device_id=peers[at], device_id_type=MESH
+        )
+
+    def to_row(other, landing):
+        return pltpu.make_async_remote_copy(
+            pair.at[2], far.at[landing], far_sent.at[other], far_come.at[landing],
+            device_id=(b, me + 4 * (other - z)), device_id_type=MESH,
+        )
+
+    def start():
+        pair[0] = values[...]
+        swap(0, 0).start()
+
+    def step(s):
+        @pl.when(s == 4)
+        def _():
+            swap(0, 0).wait()
+            pair[1] = pair[0] + come[0]
+            swap(1, 1).start()
+
+        @pl.when(s == 12)
+        def _():
+            swap(1, 1).wait()
+            pair[2] = pair[1] + come[1]
+            each_other_row(depth, z, lambda other: to_row(other, z).start())
+            far[z] = pair[2]
+
+        @pl.when(s == 22)
+        def _():
+            each_other_row(depth, z, lambda other: to_row(other, z).wait_send())
+            each_other_row(depth, z, lambda other: to_row(other, other).wait_recv())
+            pair[3] = far[0]
+
+            def add(other, carry):
+                pair[3] += far[other]
+                return carry
+
+            lax.fori_loop(1, depth, add, 0)
+            swap(2, 3).start()
+
+    def end():
+        swap(2, 3).wait()
+        out[...] = pair[3] + come[2]
+
+    return start, step, end
+
+
+def reduce_body(depth, regions, extra, *refs):
+    count, size = len(regions), 10
+    many = count + extra
+    srcs, outs, scratch = refs[:many], refs[many : 2 * many], refs[2 * many :]
+    b, me, z, y, c = place()
+    meet(depth, b, me, z, extra)
+    side = [total_steps(depth, srcs[count], outs[count], *scratch[size * count :])] if extra else []
 
     def run(which):
         phases = [
             reduce_region(depth, npd, rows[which], *rest, srcs[r], outs[r], *scratch[size * r : size * (r + 1)])
             for r, (npd, rows, *rest) in enumerate(regions)
         ]
-        for begin, *_ in phases:
+        for begin, *_ in (*phases, *side):
             begin()
 
         def step(s, carry):
-            for phase in phases:
+            for phase in (*phases, *side):
                 phase[1](s)
             return carry
 
         lax.fori_loop(0, max(phase[3] for phase in phases), step, 0)
-        for phase in phases:
+        for phase in (*phases, *side):
             phase[2]()
 
     by_branch(b, regions, run)
 
 
-def reduce_rows(mesh, srcs, regions, collective_id, dtype, lag=2):
+def reduce_rows(mesh, srcs, regions, collective_id, dtype, lag=2, small=None):
     depth, width = mesh.shape["dp"] // 4, srcs[0].shape[1]
     kind = srcs[0].dtype
     shapes, scratch = [], []
@@ -455,11 +527,20 @@
             pltpu.SemaphoreType.DMA((2, held)),
             pltpu.SemaphoreType.DMA((3, held)),
         ]
+    vmem = pl.BlockSpec(memory_space=pltpu.VMEM)
+    in_specs, out_specs = [ANY] * len(srcs), [vmem] * len(shapes)
+    if small is not None:
+        shapes.append(jax.ShapeDtypeStruct(small.shape, jnp.float32))
+        in_specs.append(vmem)
+        out_specs.append(vmem)
+        scratch += [pltpu.VMEM((lead, *small.shape), jnp.float32) for lead in (4, 3, depth)]
+        scratch += [pltpu.SemaphoreType.DMA((lead,)) for lead in (3, 3, depth, depth)]
+        srcs = [*srcs, small]
     return pl.pallas_call(
-        functools.partial(reduce_body, depth, tuple((*region, lag) for region in regions)),
+        functools.partial(reduce_body, depth, tuple((*region, lag) for region in regions), small is not None),
         out_shape=shapes,
-        in_specs=[ANY] * len(srcs),
-        out_specs=[pl.BlockSpec(memory_space=pltpu.VMEM)] * len(shapes),
+        in_specs=in_specs,
+        out_specs=out_specs,
         scratch_shapes=scratch,
         compiler_params=pltpu.CompilerParams(
             collective_id=collective_id, has_side_effects=True, vmem_limit_bytes=60 * 2**20
@@ -1105,76 +1186,6 @@
     )(live, own, bo_send, d_out, *weights)
 
 
-def total_body(depth, values, out, pair, come, far, sent_sem, come_sem, far_sent, far_come):
-    b, me, z, y, c = place()
-    peers = ((b, me + 1 - 2 * c), (1 - b, me), (b, me + 2 - 4 * y))
-    barrier = pltpu.get_barrier_semaphore()
-    for peer in peers:
-        pl.semaphore_signal(barrier, 1, device_id=peer, device_id_type=MESH)
-
-    def along(what):
-        def each(other, carry):
-            @pl.when(other != z)
-            def _():
-                what(other)
-
-            return carry
-
-        lax.fori_loop(0, depth, each, 0)
-
-    def at_row(other):
-        return b, me + 4 * (other - z)
-
-    along(lambda other: pl.semaphore_signal(barrier, 1, device_id=at_row(other), device_id_type=MESH))
-    pl.semaphore_wait(barrier, len(peers) + depth - 1)
-    pair[0] = values[...]
-    for step, peer in enumerate(peers):
-        copy = pltpu.make_async_remote_copy(
-            pair.at[step], come.at[step], sent_sem.at[step], come_sem.at[step], device_id=peer, device_id_type=MESH
-        )
-        copy.start()
-        copy.wait()
-        pair[step + 1] = pair[step] + come[step]
-
-    def outward(other):
-        return pltpu.make_async_remote_copy(
-            pair.at[len(peers)], far.at[z], far_sent.at[other], far_come.at[z], device_id=at_row(other), device_id_type=MESH
-        )
-
-    def inward(other):
-        return pltpu.make_async_remote_copy(
-            pair.at[len(peers)], far.at[other], far_sent.at[other], far_come.at[other], device_id=at_row(other), device_id_type=MESH
-        )
-
-    along(lambda other: outward(other).start())
-    far[z] = pair[len(peers)]
-    along(lambda other: outward(other).wait_send())
-    along(lambda other: inward(other).wait_recv())
-    out[...] = far[0]
-
-    def add(other, carry):
-        out[...] += far[other]
-        return carry
-
-    lax.fori_loop(1, depth, add, 0)
-
-
-def total_over(mesh, values, collective_id):
-    depth = mesh.shape["dp"] // 4
-    return pl.pallas_call(
-        functools.partial(total_body, depth),
-        out_shape=jax.ShapeDtypeStruct(values.shape, F32),
-        in_specs=[VMEM],
-        out_specs=VMEM,
-        scratch_shapes=[
-            pltpu.VMEM((4, *values.shape), F32), pltpu.VMEM((3, *values.shape), F32), pltpu.VMEM((depth, *values.shape), F32),
-            pltpu.SemaphoreType.DMA((3,)), pltpu.SemaphoreType.DMA((3,)), pltpu.SemaphoreType.DMA((depth,)),
-            pltpu.SemaphoreType.DMA((depth,)),
-        ],
-        compiler_params=pltpu.CompilerParams(collective_id=collective_id, has_side_effects=True),
-    )(values)
-
-
 def branch_index_pair(branch, first, second, *operands):
     return lax.cond(branch == 0, first, second, *operands)
 
@@ -1342,20 +1353,17 @@
         vectors = jnp.concatenate([vectors[:1], down_vector, vectors[2:5]], axis=0)
         both = jnp.where((jnp.arange(2) == branch)[:, None, None], vectors[None], 0.0).reshape(10, width)
         pieces_of = bias_grad.shape[1] // width
-        small = total_over(mesh, jnp.concatenate([sums, bias_grad.reshape(pieces_of, width), both, jnp.zeros((2, width), F32)]), 8)
-        values_send, small = lax.optimization_barrier((values_send, small))
+        small = jnp.concatenate([sums, bias_grad.reshape(pieces_of, width), both, jnp.zeros((2, width), F32)])
         arrived_values = lax.ppermute(values_send, "branch", [(0, 1), (1, 0)])
         grad_inputs = (values_keep.astype(F32) + arrived_values.astype(F32)).astype(BF)
+        up_sum, down_sum, small = reduce_rows(
+            mesh, [up_part, down_part],
+            ((npd, (chunk, chunk), up_ranges, (-1, -1), none), (npd, (chunk, chunk), down_ranges, swaps, none)), 5, BF, 6, small,
+        )
+        up_sum, down_sum = up_sum.reshape(share, width), down_sum.reshape(share, width)
         own_vectors = lax.dynamic_slice_in_dim(small[8 + pieces_of :], 5 * branch, 5, 0)[None]
         bias_total = small[8 : 8 + pieces_of].reshape(-1)
 
-        up_sum, down_sum = [
-            total.reshape(share, width)
-            for total in reduce_rows(
-                mesh, [up_part, down_part], ((npd, (chunk, chunk), up_ranges, (-1, -1), none), (npd, (chunk, chunk), down_ranges, swaps, none)), 5,
-                BF, 6,
-            )
-        ]
         group_grads = []
         for g, side in enumerate((down_sum, up_sum)):
             at = g * group_rows + me * share + rows_at

time: 744 us -> 737 us (level)
  Pallas kernels: 681 us -> 654 us
  starting transfers between devices: 0.33 us -> 10.4 us
    pallas_call x1 -> x0, Pallas kernels: 19.8 us -> none  [total_over(): pl.pallas_call(functools.partial(total_body, depth), out_shape=jax.ShapeD...]
    ppermute x1, starting transfers between devices: 0.3 us -> 10.4 us  [per_device(): arrived_values = lax.ppermute(values_send, 'branch', [(0, 1), (1, 0)])]
    pallas_call x2, Pallas kernels: 56 us -> 48.5 us  [iso_call(): pl.pallas_call(functools.partial(body, tall, pitch, blocks, steps), out_s...]
  transfers between devices with their start and end apart: 2 -> 2, of which waited for: 0 -> 1; matrix products, arithmetic and copies ran while one was open for 3% -> 3% of each run, Pallas kernels for 40% -> 40%
where the time goes in v6:
time: 737 us; the launch traced here: 727 us
  Pallas kernels  654 us (89%)
  other arithmetic  24.7 us (3%)
  between operations  15.6 us (2%)
  local copies, waits for them, and re-layouts  14.3 us (2%)
  starting transfers between devices  10.4 us (1%)
    pallas_call x3, Pallas kernels, reduce_rows(): pl.pallas_call(functools.partial(reduce_body, depth, tuple(((*region, lag...  222 us
    pallas_call x3, Pallas kernels, gather_rows(): pl.pallas_call(functools.partial(gather_body, depth, regions), out_shape=...  195 us
    pallas_call x1, Pallas kernels, feed_call(): pl.pallas_call(functools.partial(feed_body, per_window, 512), out_shape=[...  114 us
    pallas_call x4, Pallas kernels, call(): pl.pallas_call(functools.partial(body, k, n, pitch, talls[index], off), o...  76.1 us
    pallas_call x2, Pallas kernels, iso_call(): pl.pallas_call(functools.partial(body, tall, pitch, blocks, steps), out_s...  48.5 us
  transfers between devices with their start and end apart: 2, of which 1 were waited for; matrix products, arithmetic and copies ran while one was open for 3% of the time, Pallas kernels for 40%

profile of v6, /device:TPU:19, one launch (start us, length us, event | category | flops | bytes accessed | tf_op | source)
XLA Modules:
  0.0 726.7 jit_solution(9572722350297864325)
XLA Ops:
  7.3 107.3 %shard_map.203 = (bf16[8280,512]{1,0:T(8,128)(2,1)}, bf16[8280,512]{1,0:T(8,128)(2,1)}) custom-call(bf16[2944,512]{1,0:T(8,128)(2,1)} %bitcast.46), custom_call_target="tpu_custom_call" | custom-call | flops 49999998976 | bytes 16777216 | tf_op jit(solution)/shard_map/pallas_call | solution.py:239
  114.6 11.7 %conditional.6 = ((f32[6,72,512]{2,1,0:T(8,128)}, bf16[432,512]{1,0:T(8,128)(2,1)S(1)}, bf16[16,480,512]{2,1,0:T(8,128)(2,1)})) conditional(s32[]{:T(128)} %convert_element_type.50, (s32[1]{0:T(128)}, bf16[6,816,512]{2,1,0:T(8,128)(2,1)}, bf16[8280,512]{1,0:T(8,128)(2,1)}, f32[4,512]{1,0:T(4,128)S(1)}) %tuple.127, (s32[1]{0:T(128)}, ...), branch_computations={%region_0.1_spmd, %region_1.2_spmd} | conditional | flops 20000000000 | bytes 16777224 | solution.py:1190
  114.6 11.7 %branch_0_fun.8 = (f32[6,72,512]{2,1,0:T(8,128)}, bf16[432,512]{1,0:T(8,128)(2,1)S(1)}, bf16[16,480,512]{2,1,0:T(8,128)(2,1)}) custom-call(s32[1]{0:T(128)} %get-tuple-element.215.live, bf16[6,816,512]{2,1,0:T(8,128)(2,1)} %get-tuple-element.216.x, bf16[8280,512]{1,0:T(8,128)(2,1)} %get-tuple-element.217.weight, f32[4,512]{1,0:T(4,128)S(1)} %get-tuple-element.218.bias), custom_call_target="tpu_custom_call" | custom-call | flops 20000000000 | bytes 16777216 | tf_op jit(solution)/shard_map/cond/branch_0_fun/pallas_call | solution.py:1265
  126.3 41.3 %shard_map.204 = bf16[6912,512]{1,0:T(8,128)(2,1)} custom-call(bf16[432,512]{1,0:T(8,128)(2,1)S(1)} %get-tuple-element.347.refs_0_), custom_call_target="tpu_custom_call" | custom-call | flops 49999998976 | bytes 16777216 | tf_op jit(solution)/shard_map/pallas_call | solution.py:239
  167.7 1.5 slice.52
  169.2 1.4 slice.53
  173.4 2.3 pad_maximum_fusion
  176.3 16.4 %conditional.7 = (bf16[6912,512]{1,0:T(8,128)(2,1)}) conditional(s32[]{:T(128)} %convert_element_type.50, (s32[96]{0:T(128)S(1)}, s32[1]{0:T(128)}, s32[8]{0:T(128)}, bf16[6912,512]{1,0:T(8,128)(2,1)}, bf16[4096,512]{1,0:T(8,128)(2,1)}) %tuple.72, (s32[96]{0:T(128)S(1)}, s32[1]{0:T(128)}, s32[8]{0:T(128)}, bf16[6912,512]{1,0:T(8,128)(2,1)}, ...), branch_computations={%region_5.6_spmd, %region_6.7_spmd} | conditional | flops 9663676416 | bytes 4194312 | solution.py:1190
  176.3 16.2 %branch_0_fun.9 = bf16[6912,512]{1,0:T(8,128)(2,1)} custom-call(s32[96]{0:T(128)S(1)} %get-tuple-element.223.order, s32[1]{0:T(128)} %get-tuple-element.224.count, s32[8]{0:T(128)} %get-tuple-element.225.shift, bf16[6912,512]{1,0:T(8,128)(2,1)} %get-tuple-element.226.refs_0_.refs_1_.refs_2_.refs_3_.refs_4_.refs_5_.refs_6_.refs_7_, ...), custom_call_target="tpu_custom_call" | custom-call | flops 7516192768 | bytes 4194304 | tf_op jit(solution)/shard_map/cond/branch_0_fun/pallas_call | solution.py:1042
  192.7 39.2 %shard_map.205 = f32[2,216,512]{2,1,0:T(8,128)} custom-call(bf16[6912,512]{1,0:T(8,128)(2,1)} %get-tuple-element.578.refs_0_), custom_call_target="tpu_custom_call" | custom-call | flops 49999998976 | bytes 16777216 | tf_op jit(solution)/shard_map/pallas_call | solution.py:539
  231.9 14.2 %conditional.8 = (bf16[2448,512]{1,0:T(8,128)(2,1)}, bf16[2448,512]{1,0:T(8,128)(2,1)}) conditional(s32[]{:T(128)} %convert_element_type.50, (s32[1]{0:T(128)}, s32[1]{0:T(128)}, f32[2,216,512]{2,1,0:T(8,128)}, bf16[8280,512]{1,0:T(8,128)(2,1)}, bf16[6,816,512]{2,1,0:T(8,128)(2,1)}, /*index=5*/f32[1,512]{1,0:T(1,128)S(1)}, ...), branch_computations={%region_7.8_spmd, %region_8.9_spmd} | conditional | flops 20000000000 | bytes 16777232 | solution.py:1190
  231.9 13.8 %branch_0_fun.10 = (bf16[3,816,512]{2,1,0:T(8,128)(2,1)}, bf16[3,816,512]{2,1,0:T(8,128)(2,1)}) custom-call(s32[1]{0:T(128)} %get-tuple-element.233.live, s32[1]{0:T(128)} %get-tuple-element.234.half, f32[2,216,512]{2,1,0:T(8,128)} %get-tuple-element.235.pre_iso, bf16[8280,512]{1,0:T(8,128)(2,1)} %get-tuple-element.236.weight, ...), custom_call_target="tpu_custom_call" | custom-call | flops 20000000000 | bytes 16777216 | tf_op jit(solution)/shard_map/cond/branch_0_fun/pallas_call | solution.py:1265
  246.1 113.6 %shard_map.206 = (bf16[2448,512]{1,0:T(8,128)(2,1)}, bf16[2448,512]{1,0:T(8,128)(2,1)S(1)}, bf16[2448,512]{1,0:T(8,128)(2,1)}, bf16[1024,512]{1,0:T(8,128)(2,1)}...) custom-call(s32[1]{0:T(128)S(6)} %copy.67.live, ...), custom_call_target="tpu_custom_call" | custom-call | flops 41070624768 | bytes 41943040 | tf_op jit(solution)/shard_map/pallas_call | solution.py:1169
  360.3 34.7 %conditional.9 = (bf16[432,512]{1,0:T(8,128)(2,1)S(1)}, bf16[16,480,512]{2,1,0:T(8,128)(2,1)}, bf16[8280,512]{1,0:T(8,128)(2,1)}, f32[1,512]{1,0:T(1,128)}, f32[3,512]{1,0:T(4,128)}) conditional(s32[]{:T(128)} %convert_element_type.50, (s32[1]{0:T(128)}, s32[1]{0:T(128)}, bf16[3,816,512]{2,1,0:T(8,128)(2,1)S(1)}, ...), branch_computations={%region_9.10_spmd.clone.clone, %region_10.11_spmd.clone.clone} | conditional | flops 20000000000 | bytes 16793640 | solution.py:1190
  360.3 31.9 %branch_0_fun.13 = (bf16[432,512]{1,0:T(8,128)(2,1)S(1)}, f32[8,512]{1,0:T(8,128)}, bf16[16,480,512]{2,1,0:T(8,128)(2,1)}, bf16[8280,512]{1,0:T(8,128)(2,1)}) custom-call(s32[1]{0:T(128)} %get-tuple-element.469.live, s32[1]{0:T(128)} %get-tuple-element.470.half, bf16[3,816,512]{2,1,0:T(8,128)(2,1)S(1)} %get-tuple-element.471.grad_own, ...), custom_call_target="tpu_custom_call" | custom-call | flops 20000000000 | bytes 16777216 | tf_op jit(solution)/shard_map/cond/branch_0_fun/pallas_call | solution.py:1265
  395.0 45.9 %shard_map.207 = bf16[6912,512]{1,0:T(8,128)(2,1)} custom-call(bf16[432,512]{1,0:T(8,128)(2,1)S(1)} %get-tuple-element.355.refs_0_), custom_call_target="tpu_custom_call" | custom-call | flops 49999998976 | bytes 16777216 | tf_op jit(solution)/shard_map/pallas_call | solution.py:239
  440.9 32.6 %conditional.10 = ((bf16[6912,512]{1,0:T(8,128)(2,1)}, f32[4096,512]{1,0:T(8,128)})) conditional(s32[]{:T(128)} %convert_element_type.50, (s32[96]{0:T(128)S(1)}, s32[1]{0:T(128)}, s32[8]{0:T(128)}, bf16[6912,512]{1,0:T(8,128)(2,1)}, bf16[6912,512]{1,0:T(8,128)(2,1)}, /*index=5*/bf16[4096,512]{1,0:T(8,128)(2,1)}) %tuple.125, (s32[96]{0:T(128)S(1)}, ...), branch_computations={%region_11.12_spmd, %region_12.13_spmd} | conditional | flops 19327352832 | bytes 4194312 | solution.py:1190
  441.0 32.4 %branch_0_fun.11 = (bf16[6912,512]{1,0:T(8,128)(2,1)}, f32[4096,512]{1,0:T(8,128)}) custom-call(s32[96]{0:T(128)S(1)} %get-tuple-element.277.order, s32[1]{0:T(128)} %get-tuple-element.278.count, s32[8]{0:T(128)} %get-tuple-element.279.shift, bf16[6912,512]{1,0:T(8,128)(2,1)} %get-tuple-element.280.refs_0_.refs_1_.refs_2_.refs_3_.refs_4_.refs_5_.refs_6_.refs_7_, ...), custom_call_target="tpu_custom_call" | custom-call | flops 15032385536 | bytes 4194304 | tf_op jit(solution)/shard_map/cond/branch_0_fun/pallas_call | solution.py:1042
  475.0 53.8 %shard_map.208 = f32[2,216,512]{2,1,0:T(8,128)S(1)} custom-call(bf16[6912,512]{1,0:T(8,128)(2,1)} %get-tuple-element.356.refs_0_), custom_call_target="tpu_custom_call" | custom-call | flops 49999998976 | bytes 16777216 | tf_op jit(solution)/shard_map/pallas_call | solution.py:539
  528.8 5.9 all-reduce.3.cloned.1.call-done
  534.7 19.0 %conditional.11 = ((bf16[3,816,512]{2,1,0:T(8,128)(2,1)}, bf16[3,816,512]{2,1,0:T(8,128)(2,1)}, f32[1,512]{1,0:T(1,128)S(1)}, bf16[8280,512]{1,0:T(8,128)(2,1)})) conditional(s32[]{:T(128)} %convert_element_type.50, (s32[1]{0:T(128)}, s32[1]{0:T(128)}, f32[2,216,512]{2,1,0:T(8,128)S(1)}, f32[6,72,512]{2,1,0:T(8,128)S(1)}, ...), branch_computations={%region_16.17_spmd, %region_17.18_spmd} | conditional | flops 20000000000 | bytes 16777224 | solution.py:1190
  534.7 18.7 %branch_0_fun.12 = (bf16[3,816,512]{2,1,0:T(8,128)(2,1)}, bf16[3,816,512]{2,1,0:T(8,128)(2,1)}, f32[1,512]{1,0:T(1,128)S(1)}, bf16[8280,512]{1,0:T(8,128)(2,1)}) custom-call(s32[1]{0:T(128)} %get-tuple-element.289.live, s32[1]{0:T(128)} %get-tuple-element.290.half, f32[2,216,512]{2,1,0:T(8,128)S(1)} %get-tuple-element.291.grad_act, ...), custom_call_target="tpu_custom_call" | custom-call | flops 20000000000 | bytes 16777216 | tf_op jit(solution)/shard_map/cond/branch_0_fun/pallas_call | solution.py:1265
  554.4 10.4 %collective-permute-start = (bf16[3,816,512]{2,1,0:T(8,128)(2,1)}, bf16[3,816,512]{2,1,0:T(8,128)(2,1)S(1)}, u32[]{:S(2)}, u32[]{:S(2)}) collective-permute-start(bf16[3,816,512]{2,1,0:T(8,128)(2,1)} %get-tuple-element.468), channel_id=1, source_target_pairs={{0,16},{16,0},{1,17},{17,1},{2,18},{18,2},{3,19},{19,3},{4,20},{20... | collective-permute-start | bytes 7520264 | tf_op jit(solution)/shard_map/ppermute | solution.py:1357
  565.6 128.7 %shard_map.209 = (bf16[8,184,512]{2,1,0:T(8,128)(2,1)}, bf16[8,184,512]{2,1,0:T(8,128)(2,1)}, f32[24,512]{1,0:T(8,128)}) custom-call(bf16[8280,512]{1,0:T(8,128)(2,1)} %get-tuple-element.366.refs_0_, bf16[8280,512]{1,0:T(8,128)(2,1)} %get-tuple-element.466.refs_1_, f32[24,512]{1,0:T(8,128)} %maximum_maximum_fusion.refs_2_), custom_call_target="tpu_custom_call" | custom-call | flops 49999998976 | bytes 16777216 | tf_op jit(solution)/shard_map/pallas_call | solution.py:539
  697.0 1.3 fusion.22
  698.9 4.3 convert_element_type.61
  703.2 2.7 convert_element_type.62
  706.0 1.6 convert_element_type.60
  709.1 1.5 fusion.4
  710.6 3.3 maximum_bitcast_fusion
  713.9 4.0 fusion.5
  717.9 1.5 copy.68
  (77 shorter events, 13.7 us)
Async XLA Ops:
  7.2 527.5 %all-reduce.3.cloned.1.call-start = ((), (), s32[]{:S(2)}) async-start(), calls=%async_computation | async-start | bytes 10485760 | tf_op jit(solution)/shard_map/psum | solution.py:1327
  7.3 107.3 %copy-start.14 = (f32[1,4,512]{2,1,0:T(4,128)S(1)}, f32[1,4,512]{2,1,0:T(4,128)}, u32[]{:S(2)}) copy-start(f32[1,4,512]{2,1,0:T(4,128)} %param.28) | copy-start | bytes 24580
  126.3 46.1 %copy-start = (bf16[1,2,1472,512]{3,2,1,0:T(8,128)(2,1)S(1)}, bf16[1,2,1472,512]{3,2,1,0:T(8,128)(2,1)}, u32[]{:S(2)}) copy-start(bf16[1,2,1472,512]{3,2,1,0:T(8,128)(2,1)} %param.26) | copy-start | bytes 9043972
  172.1 0.9 copy-start.6
  172.1 0.9 copy-start.8
  172.3 4.0 copy-start.12
  192.7 39.2 %copy-start.15 = (f32[1,512]{1,0:T(1,128)S(1)}, f32[1,512]{1,0:T(1,128)}, u32[]{:S(2)}) copy-start(f32[1,512]{1,0:T(1,128)} %param.27) | copy-start | bytes 6148
  395.0 45.9 %copy-start.13 = (s32[96]{0:T(128)S(1)}, s32[96]{0:T(128)}, u32[]{:S(2)}) copy-start(s32[96]{0:T(128)} %copy-done.12) | copy-start | bytes 1156
  440.9 32.6 %copy-start.17 = (pred[2]{0:T(512)(128)(4,1)S(1)}, pred[2]{0:T(512)(128)(4,1)}, u32[]{:S(2)}) copy-start(pred[2]{0:T(512)(128)(4,1)} %iota_compare_fusion.2) | copy-start | bytes 10
  440.9 33.3 %copy-start.11 = (f32[1,2048]{1,0:T(1,128)S(1)}, f32[1,2048]{1,0:T(1,128)}, u32[]{:S(2)}) copy-start(f32[1,2048]{1,0:T(1,128)} %get-tuple-element.369) | copy-start | bytes 24580
  475.0 59.7 %copy-start.16 = (f32[6,72,512]{2,1,0:T(8,128)S(1)}, f32[6,72,512]{2,1,0:T(8,128)}, u32[]{:S(2)}) copy-start(f32[6,72,512]{2,1,0:T(8,128)} %get-tuple-element.361) | copy-start | bytes 2654212
  534.7 30.2 %copy-start.10 = (f32[8,512]{1,0:T(8,128)S(1)}, f32[8,512]{1,0:T(8,128)}, u32[]{:S(2)}) copy-start(f32[8,512]{1,0:T(8,128)} %get-tuple-element.368) | copy-start | bytes 49156
  554.4 159.5 %collective-permute-start = (bf16[3,816,512]{2,1,0:T(8,128)(2,1)}, bf16[3,816,512]{2,1,0:T(8,128)(2,1)S(1)}, u32[]{:S(2)}, u32[]{:S(2)}) collective-permute-start(bf16[3,816,512]{2,1,0:T(8,128)(2,1)} %get-tuple-element.468), channel_id=1, source_target_pairs={{0,16},{16,0},{1,17},{17,1},{2,18},{18,2},{3,19},{19,3},{4,20},{20... | collective-permute-start | bytes 7520264 | tf_op jit(solution)/shard_map/ppermute | solution.py:1357
  698.9 4.3 copy-start.2
  698.9 9.2 %slice-start = ((s8[8388608]{0:T(1024)(128)(4,1)}), s8[4194304]{0:T(1024)(128)(4,1)S(1)}, s32[]{:S(2)}) async-start(s8[8388608]{0:T(1024)(128)(4,1)} %bitcast.44), calls=%async_computation.1 | async-start | bytes 8388608
  703.2 2.7 copy-start.5
  703.2 5.0 slice-start.1
  705.9 2.7 copy-start.3
  705.9 3.2 copy-start.4
  705.9 3.2 copy-start.7
  706.0 3.2 copy-start.9
  713.9 4.0 copy-start.1
Sparse Core Ops, SparseCore 0:
  359.9 174.7 all-reduce.2

commit v7 on v6

--- a/solution.py
+++ b/solution.py
@@ -1081,6 +1081,8 @@
         pl.semaphore_wait(barrier, 1)
         forth(0).start()
         forth(1).start()
+        forth(2).start()
+        forth(3).start()
         bias_grad[...] = jnp.zeros_like(bias_grad)
         sums[...] = jnp.zeros_like(sums)
         merge_sum[...] = jnp.zeros_like(merge_sum)
@@ -1089,9 +1091,9 @@
 
     forth(step).wait_recv()
 
-    @pl.when(step + 2 < steps)
+    @pl.when(step + 4 < steps)
     def _():
-        forth(step + 2).start()
+        forth(step + 4).start()
 
     alive = jnp.where(2 * (step // per_window) + branch < live[0], 1.0, 0.0)
     own_rows, other_rows = own[...], other_slots[step]
@@ -1303,8 +1305,9 @@
             return [lambda *operands, t=t: iso_call(back, t, *operands) for t in talls]
 
         acts = spread_windows(act, 3)
-        flags = [acts[t - 1 : members * slots * t : t, 0] for t in talls]
-        alive = jnp.where(branch == 0, flags[0], flags[1]) > 0.5
+        alive = branch_index_pair(
+            branch, *[lambda rows, t=t: rows[t - 1 : members * slots * t : t, 0] > 0.5 for t in talls], acts
+        )
         places = jnp.arange(members * slots)
         rank = jnp.sum(jnp.logical_and(alive[None, :], places[None, :] < places[:, None]).astype(jnp.int32), axis=1)
         order = jnp.sum(

time: 737 us -> 748 us (1.015)
  Pallas kernels: 654 us -> 666 us
  local copies, waits for them, and re-layouts: 14.3 us -> 23 us
    pallas_call x0 -> x1, local copies, waits for them, and re-layouts: none -> 10.5 us  [gather_rows(): pl.pallas_call(functools.partial(gather_body, depth, regions), out_shape=...]
    pallas_call x2, Pallas kernels: 48.5 us -> 56 us  [iso_call(): pl.pallas_call(functools.partial(body, tall, pitch, blocks, steps), out_s...]
  transfers between devices with their start and end apart: 2 -> 2, of which waited for: 1 -> 0; matrix products, arithmetic and copies ran while one was open for 3% -> 3% of each run, Pallas kernels for 40% -> 41%
where the time goes in v7:
time: 748 us; the launch traced here: 737 us
  Pallas kernels  666 us (89%)
  other arithmetic  25.2 us (3%)
  local copies, waits for them, and re-layouts  23 us (3%)
  between operations  15.6 us (2%)
    pallas_call x3, Pallas kernels, reduce_rows(): pl.pallas_call(functools.partial(reduce_body, depth, tuple(((*region, lag...  225 us
    pallas_call x3, Pallas kernels, gather_rows(): pl.pallas_call(functools.partial(gather_body, depth, regions), out_shape=...  194 us
    pallas_call x1, Pallas kernels, feed_call(): pl.pallas_call(functools.partial(feed_body, per_window, 512), out_shape=[...  114 us
    pallas_call x4, Pallas kernels, call(): pl.pallas_call(functools.partial(body, k, n, pitch, talls[index], off), o...  76.2 us
    pallas_call x2, Pallas kernels, iso_call(): pl.pallas_call(functools.partial(body, tall, pitch, blocks, steps), out_s...  56 us
  transfers between devices with their start and end apart: 2, of which 0 were waited for; matrix products, arithmetic and copies ran while one was open for 3% of the time, Pallas kernels for 41%

profile of v7, /device:TPU:19, one launch (start us, length us, event | category | flops | bytes accessed | tf_op | source)
XLA Modules:
  0.0 737.0 jit_solution(16216792254748350933)
XLA Ops:
  7.9 107.2 %shard_map.203 = (bf16[8280,512]{1,0:T(8,128)(2,1)}, bf16[8280,512]{1,0:T(8,128)(2,1)}) custom-call(bf16[2944,512]{1,0:T(8,128)(2,1)} %bitcast.53), custom_call_target="tpu_custom_call" | custom-call | flops 49999998976 | bytes 16777216 | tf_op jit(solution)/shard_map/pallas_call | solution.py:239
  115.8 11.7 %conditional.7 = ((f32[6,72,512]{2,1,0:T(8,128)}, bf16[432,512]{1,0:T(8,128)(2,1)S(1)}, bf16[16,480,512]{2,1,0:T(8,128)(2,1)})) conditional(s32[]{:T(128)} %convert_element_type.55, (s32[1]{0:T(128)}, bf16[6,816,512]{2,1,0:T(8,128)(2,1)}, bf16[8280,512]{1,0:T(8,128)(2,1)}, f32[4,512]{1,0:T(4,128)S(1)}) %tuple.141, (s32[1]{0:T(128)}, ...), branch_computations={%region_0.1_spmd, %region_1.2_spmd} | conditional | flops 20000000000 | bytes 16777224 | solution.py:1192
  115.8 11.7 %branch_0_fun.8 = (f32[6,72,512]{2,1,0:T(8,128)}, bf16[432,512]{1,0:T(8,128)(2,1)S(1)}, bf16[16,480,512]{2,1,0:T(8,128)(2,1)}) custom-call(s32[1]{0:T(128)} %get-tuple-element.219.live, bf16[6,816,512]{2,1,0:T(8,128)(2,1)} %get-tuple-element.220.x, bf16[8280,512]{1,0:T(8,128)(2,1)} %get-tuple-element.221.weight, f32[4,512]{1,0:T(4,128)S(1)} %get-tuple-element.222.bias), custom_call_target="tpu_custom_call" | custom-call | flops 20000000000 | bytes 16777216 | tf_op jit(solution)/shard_map/cond/branch_0_fun/pallas_call | solution.py:1267
  127.5 41.3 %shard_map.204 = bf16[6912,512]{1,0:T(8,128)(2,1)} custom-call(bf16[432,512]{1,0:T(8,128)(2,1)S(1)} %get-tuple-element.353.refs_0_), custom_call_target="tpu_custom_call" | custom-call | flops 49999998976 | bytes 16777216 | tf_op jit(solution)/shard_map/pallas_call | solution.py:239
  168.8 10.5 %copy.29 = bf16[6912,512]{0,1:T(8,128)(2,1)} copy(bf16[6912,512]{1,0:T(8,128)(2,1)} %shard_map.204) | data formatting | bytes 14155776 | tf_op jit(solution)/shard_map/pallas_call | solution.py:239
  179.3 1.7 conditional.8
  182.5 2.3 pad_maximum_fusion
  185.4 18.9 %conditional.9 = (bf16[6912,512]{1,0:T(8,128)(2,1)}) conditional(s32[]{:T(128)} %convert_element_type.55, (s32[96]{0:T(128)S(1)}, s32[1]{0:T(128)}, s32[8]{0:T(128)}, bf16[6912,512]{1,0:T(8,128)(2,1)}, bf16[4096,512]{1,0:T(8,128)(2,1)}) %tuple.82, (s32[96]{0:T(128)S(1)}, s32[1]{0:T(128)}, s32[8]{0:T(128)}, bf16[6912,512]{1,0:T(8,128)(2,1)}, ...), branch_computations={%region_8.9_spmd, %region_9.10_spmd} | conditional | flops 9663676416 | bytes 4194312 | solution.py:1192
  185.4 18.7 %branch_0_fun.9 = bf16[6912,512]{1,0:T(8,128)(2,1)} custom-call(s32[96]{0:T(128)S(1)} %get-tuple-element.227.order, s32[1]{0:T(128)} %get-tuple-element.228.count, s32[8]{0:T(128)} %get-tuple-element.229.shift, bf16[6912,512]{1,0:T(8,128)(2,1)} %get-tuple-element.230.refs_0_.refs_1_.refs_2_.refs_3_.refs_4_.refs_5_.refs_6_.refs_7_, ...), custom_call_target="tpu_custom_call" | custom-call | flops 7516192768 | bytes 4194304 | tf_op jit(solution)/shard_map/cond/branch_0_fun/pallas_call | solution.py:1042
  204.4 39.2 %shard_map.205 = f32[2,216,512]{2,1,0:T(8,128)} custom-call(bf16[6912,512]{1,0:T(8,128)(2,1)} %get-tuple-element.594.refs_0_), custom_call_target="tpu_custom_call" | custom-call | flops 49999998976 | bytes 16777216 | tf_op jit(solution)/shard_map/pallas_call | solution.py:539
  243.6 14.2 %conditional.10 = (bf16[2448,512]{1,0:T(8,128)(2,1)}, bf16[2448,512]{1,0:T(8,128)(2,1)}) conditional(s32[]{:T(128)} %convert_element_type.55, (s32[1]{0:T(128)}, s32[1]{0:T(128)}, f32[2,216,512]{2,1,0:T(8,128)}, bf16[8280,512]{1,0:T(8,128)(2,1)}, bf16[6,816,512]{2,1,0:T(8,128)(2,1)}, /*index=5*/f32[1,512]{1,0:T(1,128)S(1)}, ...), branch_computations={%region_10.11_spmd, %region_11.12_spmd} | conditional | flops 20000000000 | bytes 16777232 | solution.py:1192
  243.6 13.8 %branch_0_fun.10 = (bf16[3,816,512]{2,1,0:T(8,128)(2,1)}, bf16[3,816,512]{2,1,0:T(8,128)(2,1)}) custom-call(s32[1]{0:T(128)} %get-tuple-element.237.live, s32[1]{0:T(128)} %get-tuple-element.238.half, f32[2,216,512]{2,1,0:T(8,128)} %get-tuple-element.239.pre_iso, bf16[8280,512]{1,0:T(8,128)(2,1)} %get-tuple-element.240.weight, ...), custom_call_target="tpu_custom_call" | custom-call | flops 20000000000 | bytes 16777216 | tf_op jit(solution)/shard_map/cond/branch_0_fun/pallas_call | solution.py:1267
  257.8 113.6 %shard_map.206 = (bf16[2448,512]{1,0:T(8,128)(2,1)}, bf16[2448,512]{1,0:T(8,128)(2,1)S(1)}, bf16[2448,512]{1,0:T(8,128)(2,1)}, bf16[1024,512]{1,0:T(8,128)(2,1)}...) custom-call(s32[1]{0:T(128)S(6)} %copy.77.live, ...), custom_call_target="tpu_custom_call" | custom-call | flops 41070624768 | bytes 41943040 | tf_op jit(solution)/shard_map/pallas_call | solution.py:1171
  372.0 34.7 %conditional.11 = (bf16[432,512]{1,0:T(8,128)(2,1)S(1)}, bf16[16,480,512]{2,1,0:T(8,128)(2,1)}, bf16[8280,512]{1,0:T(8,128)(2,1)}, f32[1,512]{1,0:T(1,128)}, f32[3,512]{1,0:T(4,128)}) conditional(s32[]{:T(128)} %convert_element_type.55, (s32[1]{0:T(128)}, s32[1]{0:T(128)}, bf16[3,816,512]{2,1,0:T(8,128)(2,1)S(1)}, ...), branch_computations={%region_12.13_spmd.clone.clone, %region_13.14_spmd.clone.clone} | conditional | flops 20000000000 | bytes 16793640 | solution.py:1192
  372.0 31.9 %branch_0_fun.13 = (bf16[432,512]{1,0:T(8,128)(2,1)S(1)}, f32[8,512]{1,0:T(8,128)}, bf16[16,480,512]{2,1,0:T(8,128)(2,1)}, bf16[8280,512]{1,0:T(8,128)(2,1)}) custom-call(s32[1]{0:T(128)} %get-tuple-element.477.live, s32[1]{0:T(128)} %get-tuple-element.478.half, bf16[3,816,512]{2,1,0:T(8,128)(2,1)S(1)} %get-tuple-element.479.grad_own, ...), custom_call_target="tpu_custom_call" | custom-call | flops 20000000000 | bytes 16777216 | tf_op jit(solution)/shard_map/cond/branch_0_fun/pallas_call | solution.py:1267
  403.9 1.3 slice.69
  406.7 45.9 %shard_map.207 = bf16[6912,512]{1,0:T(8,128)(2,1)} custom-call(bf16[432,512]{1,0:T(8,128)(2,1)S(1)} %get-tuple-element.363.refs_0_), custom_call_target="tpu_custom_call" | custom-call | flops 49999998976 | bytes 16777216 | tf_op jit(solution)/shard_map/pallas_call | solution.py:239
  452.7 37.5 %conditional.12 = ((bf16[6912,512]{1,0:T(8,128)(2,1)}, f32[4096,512]{1,0:T(8,128)})) conditional(s32[]{:T(128)} %convert_element_type.55, (s32[96]{0:T(128)S(1)}, s32[1]{0:T(128)}, s32[8]{0:T(128)}, bf16[6912,512]{1,0:T(8,128)(2,1)}, bf16[6912,512]{1,0:T(8,128)(2,1)}, /*index=5*/bf16[4096,512]{1,0:T(8,128)(2,1)}) %tuple.139, (s32[96]{0:T(128)S(1)}, ...), branch_computations={%region_14.15_spmd, %region_15.16_spmd} | conditional | flops 19327352832 | bytes 4194312 | solution.py:1192
  452.7 37.3 %branch_0_fun.11 = (bf16[6912,512]{1,0:T(8,128)(2,1)}, f32[4096,512]{1,0:T(8,128)}) custom-call(s32[96]{0:T(128)S(1)} %get-tuple-element.281.order, s32[1]{0:T(128)} %get-tuple-element.282.count, s32[8]{0:T(128)} %get-tuple-element.283.shift, bf16[6912,512]{1,0:T(8,128)(2,1)} %get-tuple-element.284.refs_0_.refs_1_.refs_2_.refs_3_.refs_4_.refs_5_.refs_6_.refs_7_, ...), custom_call_target="tpu_custom_call" | custom-call | flops 15032385536 | bytes 4194304 | tf_op jit(solution)/shard_map/cond/branch_0_fun/pallas_call | solution.py:1042
  491.7 57.6 %shard_map.208 = f32[2,216,512]{2,1,0:T(8,128)S(1)} custom-call(bf16[6912,512]{1,0:T(8,128)(2,1)} %get-tuple-element.364.refs_0_), custom_call_target="tpu_custom_call" | custom-call | flops 49999998976 | bytes 16777216 | tf_op jit(solution)/shard_map/pallas_call | solution.py:539
  549.4 19.0 %conditional.13 = ((bf16[3,816,512]{2,1,0:T(8,128)(2,1)}, bf16[3,816,512]{2,1,0:T(8,128)(2,1)}, f32[1,512]{1,0:T(1,128)S(1)}, bf16[8280,512]{1,0:T(8,128)(2,1)})) conditional(s32[]{:T(128)} %convert_element_type.55, (s32[1]{0:T(128)}, s32[1]{0:T(128)}, f32[2,216,512]{2,1,0:T(8,128)S(1)}, f32[6,72,512]{2,1,0:T(8,128)S(1)}, ...), branch_computations={%region_19.20_spmd, %region_20.21_spmd} | conditional | flops 20000000000 | bytes 16777224 | solution.py:1192
  549.4 18.7 %branch_0_fun.12 = (bf16[3,816,512]{2,1,0:T(8,128)(2,1)}, bf16[3,816,512]{2,1,0:T(8,128)(2,1)}, f32[1,512]{1,0:T(1,128)S(1)}, bf16[8280,512]{1,0:T(8,128)(2,1)}) custom-call(s32[1]{0:T(128)} %get-tuple-element.293.live, s32[1]{0:T(128)} %get-tuple-element.294.half, f32[2,216,512]{2,1,0:T(8,128)S(1)} %get-tuple-element.295.grad_act, ...), custom_call_target="tpu_custom_call" | custom-call | flops 20000000000 | bytes 16777216 | tf_op jit(solution)/shard_map/cond/branch_0_fun/pallas_call | solution.py:1267
  569.1 6.1 collective-permute-start
  576.0 128.6 %shard_map.209 = (bf16[8,184,512]{2,1,0:T(8,128)(2,1)}, bf16[8,184,512]{2,1,0:T(8,128)(2,1)}, f32[24,512]{1,0:T(8,128)}) custom-call(bf16[8280,512]{1,0:T(8,128)(2,1)} %get-tuple-element.374.refs_0_, bf16[8280,512]{1,0:T(8,128)(2,1)} %get-tuple-element.474.refs_1_, f32[24,512]{1,0:T(8,128)} %maximum_maximum_fusion.refs_2_), custom_call_target="tpu_custom_call" | custom-call | flops 49999998976 | bytes 16777216 | tf_op jit(solution)/shard_map/pallas_call | solution.py:539
  707.3 1.3 fusion.22
  709.2 4.3 convert_element_type.65
  713.5 2.7 convert_element_type.66
  716.3 1.6 convert_element_type.64
  719.4 1.5 fusion.4
  720.9 3.3 maximum_bitcast_fusion
  724.2 4.0 fusion.5
  728.2 1.5 copy.78
  (79 shorter events, 14.0 us)
Async XLA Ops:
  7.2 542.2 %all-reduce.3.cloned.1.call-start = ((), (), s32[]{:S(2)}) async-start(), calls=%async_computation | async-start | bytes 10485760 | tf_op jit(solution)/shard_map/psum | solution.py:1330
  7.9 173.5 %copy-start.8 = (pred[1472]{0:T(1024)(128)(4,1)}, pred[1472]{0:T(1024)(128)(4,1)S(1)}, u32[]{:S(2)}) copy-start(pred[1472]{0:T(1024)(128)(4,1)S(1)} %get-tuple-element.527) | copy-start | bytes 4420
  7.9 107.9 %copy-start.14 = (f32[1,4,512]{2,1,0:T(4,128)S(1)}, f32[1,4,512]{2,1,0:T(4,128)}, u32[]{:S(2)}) copy-start(f32[1,4,512]{2,1,0:T(4,128)} %param.30) | copy-start | bytes 24580
  168.8 12.6 %copy-start = (bf16[1,2,1472,512]{3,2,1,0:T(8,128)(2,1)S(1)}, bf16[1,2,1472,512]{3,2,1,0:T(8,128)(2,1)}, u32[]{:S(2)}) copy-start(bf16[1,2,1472,512]{3,2,1,0:T(8,128)(2,1)} %param.28) | copy-start | bytes 9043972
  181.2 4.2 copy-start.12
  181.4 0.7 copy-start.6
  204.3 39.3 %copy-start.15 = (f32[1,4,512]{2,1,0:T(4,128)S(1)}, f32[1,4,512]{2,1,0:T(4,128)}, u32[]{:S(2)}) copy-start(f32[1,4,512]{2,1,0:T(4,128)} %param.30) | copy-start | bytes 24580
  204.3 39.3 %copy-start.16 = (f32[1,512]{1,0:T(1,128)S(1)}, f32[1,512]{1,0:T(1,128)}, u32[]{:S(2)}) copy-start(f32[1,512]{1,0:T(1,128)} %param.29) | copy-start | bytes 6148
  406.7 45.9 %copy-start.13 = (s32[96]{0:T(128)S(1)}, s32[96]{0:T(128)}, u32[]{:S(2)}) copy-start(s32[96]{0:T(128)} %copy-done.12) | copy-start | bytes 1156
  452.6 37.5 %copy-start.18 = (pred[2]{0:T(512)(128)(4,1)S(1)}, pred[2]{0:T(512)(128)(4,1)}, u32[]{:S(2)}) copy-start(pred[2]{0:T(512)(128)(4,1)} %iota_compare_fusion.2) | copy-start | bytes 10
  452.6 38.2 %copy-start.11 = (f32[1,2048]{1,0:T(1,128)S(1)}, f32[1,2048]{1,0:T(1,128)}, u32[]{:S(2)}) copy-start(f32[1,2048]{1,0:T(1,128)} %get-tuple-element.377) | copy-start | bytes 24580
  491.7 57.7 %copy-start.17 = (f32[6,72,512]{2,1,0:T(8,128)S(1)}, f32[6,72,512]{2,1,0:T(8,128)}, u32[]{:S(2)}) copy-start(f32[6,72,512]{2,1,0:T(8,128)} %get-tuple-element.369) | copy-start | bytes 2654212
  549.4 25.9 %copy-start.10 = (f32[8,512]{1,0:T(8,128)S(1)}, f32[8,512]{1,0:T(8,128)}, u32[]{:S(2)}) copy-start(f32[8,512]{1,0:T(8,128)} %get-tuple-element.376) | copy-start | bytes 49156
  569.1 155.1 %collective-permute-start = (bf16[3,816,512]{2,1,0:T(8,128)(2,1)}, bf16[3,816,512]{2,1,0:T(8,128)(2,1)S(1)}, u32[]{:S(2)}, u32[]{:S(2)}) collective-permute-start(bf16[3,816,512]{2,1,0:T(8,128)(2,1)} %get-tuple-element.476), channel_id=1, source_target_pairs={{0,16},{16,0},{1,17},{17,1},{2,18},{18,2},{3,19},{19,3},{4,20},{20... | collective-permute-start | bytes 7520264 | tf_op jit(solution)/shard_map/ppermute | solution.py:1360
  709.2 4.3 copy-start.2
  709.2 9.2 %slice-start = ((s8[8388608]{0:T(1024)(128)(4,1)}), s8[4194304]{0:T(1024)(128)(4,1)S(1)}, s32[]{:S(2)}) async-start(s8[8388608]{0:T(1024)(128)(4,1)} %bitcast.51), calls=%async_computation.1 | async-start | bytes 8388608
  713.5 2.7 copy-start.5
  713.5 5.0 slice-start.1
  716.2 2.7 copy-start.3
  716.2 3.2 copy-start.4
  716.2 3.2 copy-start.7
  716.3 3.2 copy-start.9
  724.2 4.0 copy-start.1
Sparse Core Ops, SparseCore 0:
  371.6 177.3 all-reduce.2
